TPU v7x, 32 devices: a whole 2x2x4 slice. The times are simulated.
32 devices in a mesh: rep: 2 (over y), shard: 16 (over z, x, core).
Axes of the slice: x: 2, y: 2, z: 4, core: 2. Of those that a mesh axis runs over, the one named last changes fastest.
Arguments:
- tokens: bfloat16 [16384, 896], P(('rep', 'shard')), may hold values from -6 to 6
- cotangent: bfloat16 [16384, 896], P(('rep', 'shard')), may hold values from -6 to 6
- place: int32 [16384], replicated, may hold values from 0 to 16383, as said below
- prefix: int32 [4], replicated, may hold values from 409 to 2048
- attn_norm: bfloat16 [896], P('shard'), may hold values from 0.5 to 1.5
- q_weight: bfloat16 [896, 896], P('shard'), may hold values from -0.1875 to 0.1875
- q_bias: bfloat16 [896], P('shard'), may hold values from -3 to 3
- k_weight: bfloat16 [896, 128], P('shard'), may hold values from -0.1875 to 0.1875
- k_bias: bfloat16 [128], P('shard'), may hold values from -3 to 3
- v_weight: bfloat16 [896, 128], P('shard'), may hold values from -0.1875 to 0.1875
- v_bias: bfloat16 [128], P('shard'), may hold values from -3 to 3
- o_weight: bfloat16 [896, 896], P('shard'), may hold values from -1.5 to 1.5
- mlp_norm: bfloat16 [896], P('shard'), may hold values from 0.5 to 1.5
- gate_weight: bfloat16 [896, 4864], P('shard'), may hold values from -0.1875 to 0.1875
- up_projection_weight: bfloat16 [896, 4864], P('shard'), may hold values from -0.1875 to 0.1875
- down_weight: bfloat16 [4864, 896], P('shard'), may hold values from -0.078125 to 0.078125
Outputs:
- output: bfloat16 [16384, 896], P(('rep', 'shard'))
- input_grad: bfloat16 [16384, 896], P(('rep', 'shard'))
- attn_norm_grad: float32 [896], P('shard')
- q_weight_grad: float32 [896, 896], P('shard')
- q_bias_grad: float32 [896], P('shard')
- k_weight_grad: float32 [896, 128], P('shard')
- k_bias_grad: float32 [128], P('shard')
- v_weight_grad: float32 [896, 128], P('shard')
- v_bias_grad: float32 [128], P('shard')
- o_weight_grad: float32 [896, 896], P('shard')
- mlp_norm_grad: float32 [896], P('shard')
- gate_weight_grad: float32 [896, 4864], P('shard')
- up_weight_grad: float32 [896, 4864], P('shard')
- down_weight_grad: float32 [4864, 896], P('shard')
Inputs may be any that keep to these rules, and one draw needn't show every extreme that they name: `place`: each value appears once. Rows of one device in one micro-batch are 256 consecutive positions of one sequence in order; the sequences of one micro-batch of one rep group are wholly held by that group's devices in that micro-batch, in blocks of 256 rows placed on its devices in any order.
All inputs are finite; a program needn't handle non-finite values.
Results may differ from a plain program's by a relative error of at most 0.019.
Values may be sent and summed in bfloat16 or wider, within the bound.
No kernel may reach another device: no remote copies, remote signals or barrier semaphores. Data moves between devices by JAX's collectives and lax.ppermute only.
A program may use at most 256 MiB of HBM per device.

v0:
```python
import jax
import jax.numpy as jnp
from jax import lax
from jax.sharding import PartitionSpec as P

HEADS = 14
KV_HEADS = 2
HEAD_DIM = 64
TMB = 256
MB = 2
SEQ_MAX = 4096


norm_eps = 1e-06
rope_base = 1000000.0
masked_score = -1e30


def shortened(value):
    return jax.tree.map(lambda a: a.astype(jnp.bfloat16) if a.dtype == jnp.float32 else a, value)


def dot_first(left_side, right_side):
    return lax.dot_general(
        left_side, right_side, (((0,), (0,)), ((), ())), preferred_element_type=jnp.float32
    )


def dot_last(left_side, right_side):
    return lax.dot_general(
        left_side, right_side, (((1,), (1,)), ((), ())), preferred_element_type=jnp.float32
    )


def rope_tables(positions, head_width):
    half_width = head_width // 2
    exponent = jnp.arange(half_width).astype(jnp.float32) * (2.0 / head_width)
    frequency = rope_base ** (-exponent)
    angles = positions.astype(jnp.float32)[:, None] * frequency[None, :]
    angles = jnp.concatenate([angles, angles], axis=1)
    return (jnp.cos(angles), jnp.sin(angles))


def rotate(values, cosine, sine_table, head_width):
    half_width = head_width // 2
    turned = jnp.concatenate([-values[..., half_width:], values[..., :half_width]], axis=-1)
    return values * cosine[:, None, :] + turned * sine_table[:, None, :]


def unrotate(grads_in, cosine, sine_table, head_width):
    half_width = head_width // 2
    scaled = grads_in * sine_table[:, None, :]
    turned = jnp.concatenate([scaled[..., half_width:], -scaled[..., :half_width]], axis=-1)
    return grads_in * cosine[:, None, :] + turned


def unchanged(state):
    return state


def load_block(key_rows, mask_for, groups, item_count, block_keys, kv_heads, head_width):
    block_start = item_count * block_keys
    block_part = lax.dynamic_slice_in_dim(key_rows, block_start, block_keys, 0)
    kv_width = kv_heads * head_width
    key_block = block_part[:, :kv_width].reshape(block_keys, kv_heads, head_width)
    value_block = block_part[:, kv_width:].reshape(block_keys, kv_heads, head_width)
    wide_mask = jnp.tile(mask_for(block_start), (groups, 1))
    return (key_block, value_block, wide_mask)


def score_block(query_heads, key_block, wide_mask, score_scale):
    raw_scores = jnp.einsum(
        "kqd,nkd->kqn", query_heads, key_block, preferred_element_type=jnp.float32
    )
    return jnp.where(wide_mask[None], raw_scores * score_scale, masked_score)


def attention_forward(query_heads, key_rows, mask_for, groups, block_keys, score_scale):
    kv_heads, query_rows, head_width = query_heads.shape
    block_count = key_rows.shape[0] // block_keys

    def stats_step(item_count, state):
        key_block, value_block, wide_mask = load_block(
            key_rows, mask_for, groups, item_count, block_keys, kv_heads, head_width
        )

        def stats_compute(state_in):
            row_max, row_sum = state_in
            attention_scores = score_block(query_heads, key_block, wide_mask, score_scale)
            new_max = jnp.maximum(row_max, jnp.max(attention_scores, axis=-1, keepdims=True))
            new_sum = row_sum * jnp.exp(row_max - new_max) + jnp.sum(
                jnp.exp(attention_scores - new_max), axis=-1, keepdims=True
            )
            return (new_max, new_sum)

        return lax.cond(jnp.any(wide_mask), stats_compute, unchanged, state)

    start_state = (
        jnp.full((kv_heads, query_rows, 1), masked_score, jnp.float32),
        jnp.zeros((kv_heads, query_rows, 1), jnp.float32),
    )
    row_max, row_sum = lax.fori_loop(0, block_count, stats_step, start_state)
    log_total = row_max + jnp.log(row_sum)

    def output_step(item_count, output):
        key_block, value_block, wide_mask = load_block(
            key_rows, mask_for, groups, item_count, block_keys, kv_heads, head_width
        )

        def output_compute(output_in):
            attention_scores = score_block(query_heads, key_block, wide_mask, score_scale)
            probs = jnp.exp(attention_scores - log_total).astype(jnp.bfloat16)
            return output_in + jnp.einsum(
                "kqn,nkd->kqd", probs, value_block, preferred_element_type=jnp.float32
            )

        return lax.cond(jnp.any(wide_mask), output_compute, unchanged, output)

    output = lax.fori_loop(0, block_count, output_step, jnp.zeros(query_heads.shape, jnp.float32))
    return (log_total, output)


def attention_backward(
    query_heads, key_rows, grad_heads, log_total, delta, mask_for, groups, block_keys, score_scale
):
    kv_heads, query_rows, head_width = query_heads.shape
    kv_width = kv_heads * head_width
    key_total = key_rows.shape[0]
    block_count = key_total // block_keys

    def grad_step(item_count, state):
        key_block, value_block, wide_mask = load_block(
            key_rows, mask_for, groups, item_count, block_keys, kv_heads, head_width
        )

        def grad_compute(state_in):
            grad_query_in, key_grads_in = state_in
            attention_scores = score_block(query_heads, key_block, wide_mask, score_scale)
            probs = jnp.exp(attention_scores - log_total)
            grad_probs = jnp.einsum(
                "kqd,nkd->kqn", grad_heads, value_block, preferred_element_type=jnp.float32
            )
            score_gradient = (probs * (grad_probs - delta)).astype(jnp.bfloat16)
            grad_query_out = grad_query_in + score_scale * jnp.einsum(
                "kqn,nkd->kqd", score_gradient, key_block, preferred_element_type=jnp.float32
            )
            grad_key_block = score_scale * jnp.einsum(
                "kqn,kqd->nkd", score_gradient, query_heads, preferred_element_type=jnp.float32
            )
            grad_value_block = jnp.einsum(
                "kqn,kqd->nkd",
                probs.astype(jnp.bfloat16),
                grad_heads,
                preferred_element_type=jnp.float32,
            )
            block_grads = jnp.concatenate(
                [
                    grad_key_block.reshape(block_keys, kv_width),
                    grad_value_block.reshape(block_keys, kv_width),
                ],
                axis=1,
            )
            return (
                grad_query_out,
                lax.dynamic_update_slice_in_dim(
                    key_grads_in, block_grads, item_count * block_keys, 0
                ),
            )

        return lax.cond(jnp.any(wide_mask), grad_compute, unchanged, state)

    start_state = (
        jnp.zeros(query_heads.shape, jnp.float32),
        jnp.zeros((key_total, 2 * kv_width), jnp.float32),
    )
    return lax.fori_loop(0, block_count, grad_step, start_state)


def on_device(
    tokens,
    cotangent,
    place,
    prefix,
    attn_norm,
    q_weight,
    q_bias,
    k_weight,
    k_bias,
    v_weight,
    v_bias,
    o_weight,
    mlp_norm,
    gate_weight,
    up_projection_weight,
    down_weight,
):
    shard_count = lax.axis_size("shard")
    seq_length = min(SEQ_MAX, TMB * shard_count)
    groups = HEADS // KV_HEADS
    kv_width = KV_HEADS * HEAD_DIM
    model_width = HEADS * HEAD_DIM
    score_scale = HEAD_DIM ** (-0.5)
    key_total = shard_count * TMB
    block_keys = TMB
    layout = place.reshape(lax.axis_size("rep"), shard_count, MB, TMB)
    group_places = lax.dynamic_index_in_dim(layout, lax.axis_index("rep"), 0, keepdims=False)
    shard_rank = lax.axis_index("shard")
    seq_count = prefix.shape[0]
    owned = (
        attn_norm,
        q_weight,
        q_bias,
        k_weight,
        k_bias,
        v_weight,
        v_bias,
        o_weight,
        mlp_norm,
        gate_weight,
        up_projection_weight,
        down_weight,
    )
    out_rows = []
    grad_rows = []
    running = None
    for micro in range(MB):
        inputs = tokens[micro * TMB : (micro + 1) * TMB]
        cot_rows = cotangent[micro * TMB : (micro + 1) * TMB]
        micro_places = group_places[:, micro, :]
        key_places = micro_places.reshape(key_total)
        query_places = lax.dynamic_index_in_dim(micro_places, shard_rank, 0, keepdims=False)
        key_seq = key_places // seq_length
        key_pos = key_places % seq_length
        query_seq = query_places // seq_length
        query_pos = query_places % seq_length
        matches = query_seq[:, None] == jnp.arange(seq_count)[None, :]
        query_limit = jnp.sum(jnp.where(matches, prefix[None, :], 0), axis=1)

        def mask_for(block_start):
            seq_part = lax.dynamic_slice_in_dim(key_seq, block_start, block_keys, 0)
            pos_part = lax.dynamic_slice_in_dim(key_pos, block_start, block_keys, 0)
            same_seq = seq_part[None, :] == query_seq[:, None]
            visible = (pos_part[None, :] <= query_pos[:, None]) | (
                pos_part[None, :] < query_limit[:, None]
            )
            return same_seq & visible

        gathered = (
            lax.all_gather(owned[0], "shard", axis=0, tiled=True),
            lax.all_gather(owned[1], "shard", axis=0, tiled=True),
            lax.all_gather(owned[2], "shard", axis=0, tiled=True),
            lax.all_gather(owned[3], "shard", axis=0, tiled=True),
            lax.all_gather(owned[4], "shard", axis=0, tiled=True),
            lax.all_gather(owned[5], "shard", axis=0, tiled=True),
            lax.all_gather(owned[6], "shard", axis=0, tiled=True),
            lax.all_gather(owned[7], "shard", axis=0, tiled=True),
            lax.all_gather(owned[8], "shard", axis=0, tiled=True),
            lax.all_gather(owned[9], "shard", axis=0, tiled=True),
            lax.all_gather(owned[10], "shard", axis=0, tiled=True),
            lax.all_gather(owned[11], "shard", axis=0, tiled=True),
        )
        (
            gain_one,
            q_full,
            q_add,
            k_full,
            k_add,
            v_full,
            v_add,
            o_full,
            gain_two,
            gate_full,
            up_full,
            down_full,
        ) = gathered
        gain_one_f = gain_one.astype(jnp.float32)
        gain_two_f = gain_two.astype(jnp.float32)
        input_vals = inputs.astype(jnp.float32)
        factor_one = lax.rsqrt(jnp.mean(input_vals * input_vals, axis=-1, keepdims=True) + norm_eps)
        normed = (input_vals * factor_one * gain_one_f).astype(jnp.bfloat16)
        query_lin = jnp.dot(normed, q_full, preferred_element_type=jnp.float32) + q_add.astype(
            jnp.float32
        )
        key_lin = jnp.dot(normed, k_full, preferred_element_type=jnp.float32) + k_add.astype(
            jnp.float32
        )
        value_rows = (
            jnp.dot(normed, v_full, preferred_element_type=jnp.float32) + v_add.astype(jnp.float32)
        ).astype(jnp.bfloat16)
        cosine, sine_table = rope_tables(query_pos, HEAD_DIM)
        rot_query = rotate(
            query_lin.reshape(TMB, HEADS, HEAD_DIM), cosine, sine_table, HEAD_DIM
        ).astype(jnp.bfloat16)
        rot_key = rotate(
            key_lin.reshape(TMB, KV_HEADS, HEAD_DIM), cosine, sine_table, HEAD_DIM
        ).astype(jnp.bfloat16)
        packed = jnp.concatenate([rot_key.reshape(TMB, kv_width), value_rows], axis=1)
        key_rows = lax.all_gather(packed, "shard", axis=0, tiled=True)
        query_heads = (
            rot_query.reshape(TMB, KV_HEADS, groups, HEAD_DIM)
            .transpose(1, 2, 0, 3)
            .reshape(KV_HEADS, groups * TMB, HEAD_DIM)
        )
        log_total, attended_heads = attention_forward(
            query_heads, key_rows, mask_for, groups, block_keys, score_scale
        )
        attended = (
            attended_heads.reshape(KV_HEADS, groups, TMB, HEAD_DIM)
            .transpose(2, 0, 1, 3)
            .reshape(TMB, model_width)
            .astype(jnp.bfloat16)
        )
        middle = input_vals + jnp.dot(attended, o_full, preferred_element_type=jnp.float32)
        factor_two = lax.rsqrt(jnp.mean(middle * middle, axis=-1, keepdims=True) + norm_eps)
        normed_two = (middle * factor_two * gain_two_f).astype(jnp.bfloat16)
        gate_pre = jnp.dot(normed_two, gate_full, preferred_element_type=jnp.float32)
        up_pre = jnp.dot(normed_two, up_full, preferred_element_type=jnp.float32)
        gate_sigmoid_values = jax.nn.sigmoid(gate_pre)
        silu_gate = gate_pre * gate_sigmoid_values
        hidden = (silu_gate * up_pre).astype(jnp.bfloat16)
        result = middle + jnp.dot(hidden, down_full, preferred_element_type=jnp.float32)
        out_rows.append(result.astype(jnp.bfloat16))
        back_weights = (
            lax.all_gather(owned[0], "shard", axis=0, tiled=True),
            lax.all_gather(owned[1], "shard", axis=0, tiled=True),
            lax.all_gather(owned[2], "shard", axis=0, tiled=True),
            lax.all_gather(owned[3], "shard", axis=0, tiled=True),
            lax.all_gather(owned[4], "shard", axis=0, tiled=True),
            lax.all_gather(owned[5], "shard", axis=0, tiled=True),
            lax.all_gather(owned[6], "shard", axis=0, tiled=True),
            lax.all_gather(owned[7], "shard", axis=0, tiled=True),
            lax.all_gather(owned[8], "shard", axis=0, tiled=True),
            lax.all_gather(owned[9], "shard", axis=0, tiled=True),
            lax.all_gather(owned[10], "shard", axis=0, tiled=True),
            lax.all_gather(owned[11], "shard", axis=0, tiled=True),
        )
        (
            gain_back,
            q_back,
            qadd_back,
            k_back,
            kadd_back,
            v_back,
            value_bias_backward,
            output_weight_backward,
            gain_two_back,
            gate_back,
            up_back,
            down_back,
        ) = back_weights
        cot_vals = cot_rows.astype(jnp.float32)
        grad_down = dot_first(hidden, cot_rows)
        grad_hidden = dot_last(cot_rows, down_back)
        slope = gate_sigmoid_values * (1.0 + gate_pre * (1.0 - gate_sigmoid_values))
        grad_gate = (grad_hidden * up_pre * slope).astype(jnp.bfloat16)
        grad_up = (grad_hidden * silu_gate).astype(jnp.bfloat16)
        grad_gate_w = dot_first(normed_two, grad_gate)
        grad_up_w = dot_first(normed_two, grad_up)
        grad_normed_two = dot_last(grad_gate, gate_back) + dot_last(grad_up, up_back)
        grad_gain_two = jnp.sum(grad_normed_two * (middle * factor_two), axis=0)
        inner_two = grad_normed_two * gain_two_f
        grad_middle = (
            cot_vals
            + factor_two * inner_two
            - middle * factor_two**3 * jnp.mean(inner_two * middle, axis=-1, keepdims=True)
        )
        grad_branch = grad_middle.astype(jnp.bfloat16)
        grad_out_w = dot_first(attended, grad_branch)
        grad_attended = dot_last(grad_branch, output_weight_backward).astype(jnp.bfloat16)
        grad_heads = (
            grad_attended.reshape(TMB, KV_HEADS, groups, HEAD_DIM)
            .transpose(1, 2, 0, 3)
            .reshape(KV_HEADS, groups * TMB, HEAD_DIM)
        )
        delta = jnp.sum(grad_heads.astype(jnp.float32) * attended_heads, axis=-1, keepdims=True)
        grad_query_heads, key_grads = attention_backward(
            query_heads,
            key_rows,
            grad_heads,
            log_total,
            delta,
            mask_for,
            groups,
            block_keys,
            score_scale,
        )
        key_share = lax.psum_scatter(key_grads, "shard", scatter_dimension=0, tiled=True)
        grad_rot_query = (
            grad_query_heads.reshape(KV_HEADS, groups, TMB, HEAD_DIM)
            .transpose(2, 0, 1, 3)
            .reshape(TMB, HEADS, HEAD_DIM)
        )
        grad_query = (
            unrotate(grad_rot_query, cosine, sine_table, HEAD_DIM)
            .reshape(TMB, model_width)
            .astype(jnp.bfloat16)
        )
        grad_key = (
            unrotate(
                key_share[:, :kv_width].reshape(TMB, KV_HEADS, HEAD_DIM),
                cosine,
                sine_table,
                HEAD_DIM,
            )
            .reshape(TMB, kv_width)
            .astype(jnp.bfloat16)
        )
        grad_value = key_share[:, kv_width:].astype(jnp.bfloat16)
        grad_q_w = dot_first(normed, grad_query)
        grad_q_b = jnp.sum(grad_query.astype(jnp.float32), axis=0)
        grad_k_w = dot_first(normed, grad_key)
        grad_k_b = jnp.sum(grad_key.astype(jnp.float32), axis=0)
        grad_v_w = dot_first(normed, grad_value)
        grad_v_b = jnp.sum(grad_value.astype(jnp.float32), axis=0)
        grad_normed = (
            dot_last(grad_query, q_back) + dot_last(grad_key, k_back) + dot_last(grad_value, v_back)
        )
        grad_gain_one = jnp.sum(grad_normed * (input_vals * factor_one), axis=0)
        inner_one = grad_normed * gain_one_f
        grad_input = (
            grad_middle
            + factor_one * inner_one
            - input_vals * factor_one**3 * jnp.mean(inner_one * input_vals, axis=-1, keepdims=True)
        )
        grad_rows.append(grad_input.astype(jnp.bfloat16))
        terms = (
            grad_gain_one,
            grad_q_w,
            grad_q_b,
            grad_k_w,
            grad_k_b,
            grad_v_w,
            grad_v_b,
            grad_out_w,
            grad_gain_two,
            grad_gate_w,
            grad_up_w,
            grad_down,
        )
        shares = (
            lax.psum_scatter(terms[0], "shard", scatter_dimension=0, tiled=True),
            lax.psum_scatter(terms[1], "shard", scatter_dimension=0, tiled=True),
            lax.psum_scatter(terms[2], "shard", scatter_dimension=0, tiled=True),
            lax.psum_scatter(terms[3], "shard", scatter_dimension=0, tiled=True),
            lax.psum_scatter(terms[4], "shard", scatter_dimension=0, tiled=True),
            lax.psum_scatter(terms[5], "shard", scatter_dimension=0, tiled=True),
            lax.psum_scatter(terms[6], "shard", scatter_dimension=0, tiled=True),
            lax.psum_scatter(terms[7], "shard", scatter_dimension=0, tiled=True),
            lax.psum_scatter(terms[8], "shard", scatter_dimension=0, tiled=True),
            lax.psum_scatter(terms[9], "shard", scatter_dimension=0, tiled=True),
            lax.psum_scatter(terms[10], "shard", scatter_dimension=0, tiled=True),
            lax.psum_scatter(terms[11], "shard", scatter_dimension=0, tiled=True),
        )
        running = shares if micro == 0 else jax.tree.map(jnp.add, running, shares)
    totals = jax.tree.map(
        lambda part: part.astype(jnp.float32), lax.psum(shortened(running), "rep")
    )
    return (jnp.concatenate(out_rows, axis=0), jnp.concatenate(grad_rows, axis=0)) + tuple(totals)


def solution(mesh):
    in_specs = (
        P(("rep", "shard"), None),
        P(("rep", "shard"), None),
        P(),
        P(),
        P("shard"),
        P("shard", None),
        P("shard"),
        P("shard", None),
        P("shard"),
        P("shard", None),
        P("shard"),
        P("shard", None),
        P("shard"),
        P("shard", None),
        P("shard", None),
        P("shard", None),
    )
    out_specs = (
        P(("rep", "shard"), None),
        P(("rep", "shard"), None),
        P("shard"),
        P("shard", None),
        P("shard"),
        P("shard", None),
        P("shard"),
        P("shard", None),
        P("shard"),
        P("shard", None),
        P("shard"),
        P("shard", None),
        P("shard", None),
        P("shard", None),
    )
    return jax.shard_map(
        on_device, mesh=mesh, in_specs=in_specs, out_specs=out_specs, check_vma=False
    )
```

profile of v0, /device:TPU:0, one launch (start us, length us, event | category | flops | bytes accessed | tf_op | source)
XLA Modules:
  0.0 2063.6 jit_solution(15582480982323746418)
XLA Ops:
  15.7 36.1 %all-reduce.15 = (bf16[128]{0:T(256)(128)(2,1)S(1)}, bf16[896]{0:T(1024)(128)(2,1)S(1)}, bf16[128]{0:T(256)(128)(2,1)S(1)}, bf16[896]{0:T(1024)(128)(2,1)S(1)}, bf16[896]{0:T(1024)(128)(2,1)S(1)}) all-reduce(bf16[128]{0:T(256)(128)(2,1)S(1)} %dynamic-update-slice.2, ...), channel_id=1, replica_groups=mesh['rep'=2,'shard'=16] {'shard'}, use_global_device_ids=true, to_apply=%add.2 | all-reduce | flops 2944 | bytes 11776
  51.9 18.1 all_gather.29
  73.8 19.8 all_gather.31
  111.2 21.8 %all-gather.20.cloned.1.call-done = bf16[4096,256]{0,1:T(8,128)(2,1)} async-done(((bf16[256,256]{0,1:T(8,128)(2,1)}), bf16[4096,256]{0,1:T(8,128)(2,1)}) %all-gather.20.cloned.1.call-update) | async-done | bytes 2097168 | tf_op jit(solution)/shard_map/all_gather | solution.py:298
  133.0 91.6 %while.94 = (s32[]{:T(128)}, f32[2,1792,1]{1,0,2:T(2,128)S(1)}, f32[2,1792,1]{1,0,2:T(2,128)S(1)}, s32[4096]{0:T(1024)}, s32[256]{0:T(256)S(1)}, /*index=5*/s32[...) while((s32[]{:T(128)}, f32[2,1792,1]{1,0,2:T(2,128)S(1)}, ...), condition=%wide.region_23.24_spmd, body=%wide.region_17.23_spmd.sunk | while | flops 122821640 | bytes 10222885 | solution.py:102
  136.7 4.4 conditional.14
  151.6 4.4 conditional.14
  163.0 4.4 conditional.14
  171.0 4.4 conditional.14
  178.9 4.4 conditional.14
  186.8 4.4 conditional.14
  205.2 4.4 conditional.14
  213.2 4.4 conditional.14
  224.7 91.4 %while.95 = (s32[]{:T(128)}, f32[2,1792,64]{1,2,0:T(8,128)S(1)}, s32[4096]{0:T(1024)}, s32[256]{0:T(256)S(1)}, s32[4096]{0:T(1024)}, /*index=5*/s32[256]{0:T(256...) while((s32[]{:T(128)}, f32[2,1792,64]{1,2,0:T(8,128)S(1)}, ...), condition=%wide.region_28.29_spmd, body=%wide.region_24.28_spmd.sunk | while | flops 239566848 | bytes 4742421 | solution.py:119
  228.2 4.4 conditional.15
  254.5 4.4 conditional.15
  262.4 4.4 conditional.15
  270.4 4.5 conditional.15
  278.3 4.5 conditional.15
  296.7 4.4 conditional.15
  317.0 53.7 %while.92 = (s32[]{:T(128)}, f32[2,1792,1]{1,0,2:T(2,128)S(1)}, f32[2,1792,1]{1,0,2:T(2,128)S(1)}, s32[4096]{0:T(1024)}, s32[256]{0:T(256)S(1)}, /*index=5*/s32[...) while((s32[]{:T(128)}, f32[2,1792,1]{1,0,2:T(2,128)S(1)}, ...), condition=%wide.region_8.9_spmd, body=%wide.region_2.8_spmd.sunk | while | flops 122821640 | bytes 10222885 | solution.py:102
  319.8 4.4 conditional.12
  357.9 4.4 conditional.12
  370.8 53.9 %while.93 = (s32[]{:T(128)}, f32[2,1792,64]{1,2,0:T(8,128)S(1)}, s32[4096]{0:T(1024)}, s32[256]{0:T(256)S(1)}, s32[4096]{0:T(1024)S(1)}, /*index=5*/s32[256]{0:T...) while((s32[]{:T(128)}, f32[2,1792,64]{1,2,0:T(8,128)S(1)}, ...), condition=%wide.region_13.14_spmd, body=%wide.region_9.13_spmd.sunk | while | flops 239566848 | bytes 4742421 | solution.py:119
  411.7 4.4 conditional.13
  431.7 8.4 fusion.115
  440.1 7.9 fusion.116
  448.2 10.7 multiply_convert_fusion.2
  458.9 7.1 fusion.119
  466.1 6.2 multiply_reduce_fusion.1
  472.3 5.0 fusion.117
  477.3 4.7 fusion.118
  481.9 10.7 multiply_convert_fusion
  492.6 5.5 fusion.121
  498.2 4.9 multiply_reduce_fusion
  509.1 144.0 %while.97 = (s32[]{:T(128)}, f32[2,1792,64]{1,2,0:T(8,128)S(1)}, f32[4096,256]{0,1:T(8,128)}, s32[4096]{0:T(1024)}, s32[256]{0:T(256)S(1)}, /*index=5*/s32[4096]...) while((s32[]{:T(128)}, f32[2,1792,64]{1,2,0:T(8,128)S(1)}, ...), condition=%wide.region_45.46_spmd, body=%wide.region_41.45_spmd.sunk | while | flops 594968576 | bytes 38180284 | solution.py:176
  512.7 11.0 conditional.17
  534.2 11.1 conditional.17
  552.2 11.1 conditional.17
  566.7 11.1 conditional.17
  581.2 11.1 conditional.17
  595.7 11.0 conditional.17
  620.7 11.0 conditional.17
  635.2 11.0 conditional.17
  661.8 66.8 %while.96 = (s32[]{:T(128)}, f32[2,1792,64]{1,2,0:T(8,128)S(1)}, f32[4096,256]{0,1:T(8,128)}, s32[4096]{0:T(1024)}, s32[256]{0:T(256)S(1)}, /*index=5*/s32[4096]...) while((s32[]{:T(128)}, f32[2,1792,64]{1,2,0:T(8,128)S(1)}, ...), condition=%wide.region_36.37_spmd, body=%wide.region_32.36_spmd.sunk | while | flops 594968576 | bytes 38180284 | solution.py:176
  664.5 11.0 conditional.16
  709.3 11.0 conditional.16
  745.3 10.4 convolution_add_fusion.4
  760.2 10.4 convolution_add_fusion.3
  771.0 4.6 fusion.61
  775.6 10.7 convolution_add_fusion.2
  789.4 7.3 fusion.25
  796.7 7.1 fusion.24
  803.8 175.8 %reduce-scatter.20.cloned.1.call-done = f32[256,256]{0,1:T(8,128)} async-done(((f32[4096,256]{0,1:T(8,128)}), f32[256,256]{0,1:T(8,128)}) %reduce-scatter.20.cloned.1.call-update) | async-done | bytes 262160 | tf_op jit(solution)/shard_map/reduce_scatter | solution.py:387
  982.3 194.0 %reduce-scatter.18.cloned.1.call-done = f32[256,256]{0,1:T(8,128)} async-done(((f32[4096,256]{0,1:T(8,128)}), f32[256,256]{0,1:T(8,128)}) %reduce-scatter.18.cloned.1.call-update) | async-done | bytes 262160 | tf_op jit(solution)/shard_map/reduce_scatter | solution.py:387
  1192.2 55.0 %reduce-scatter.28.cloned.1.call-done = f32[56,896]{1,0:T(8,128)} async-done(((f32[896,896]{1,0:T(8,128)}), f32[56,896]{1,0:T(8,128)}) %reduce-scatter.28.cloned.1.call-update) | async-done | bytes 200720
  1248.8 69.3 %reduce-scatter.34.cloned.1.call-done = f32[56,896]{1,0:T(8,128)} async-done(((f32[896,896]{1,0:T(8,128)}), f32[56,896]{1,0:T(8,128)}) %reduce-scatter.34.cloned.1.call-update) | async-done | bytes 200720
  1319.7 184.8 %reduce-scatter.22.cloned.1.call-done = f32[56,4864]{1,0:T(8,128)} async-done(((f32[896,4864]{1,0:T(8,128)}), f32[56,4864]{1,0:T(8,128)}) %reduce-scatter.22.cloned.1.call-update) | async-done | bytes 1089552 | tf_op jit(solution)/shard_map/reduce_scatter | solution.py:450
  1506.6 184.6 %reduce-scatter.24.cloned.1.call-done = f32[56,4864]{1,0:T(8,128)} async-done(((f32[896,4864]{1,0:T(8,128)}), f32[56,4864]{1,0:T(8,128)}) %reduce-scatter.24.cloned.1.call-update) | async-done | bytes 1089552 | tf_op jit(solution)/shard_map/reduce_scatter | solution.py:451
  1693.4 184.5 %reduce-scatter.26.cloned.1.call-done = f32[304,896]{1,0:T(8,128)} async-done(((f32[4864,896]{1,0:T(8,128)}), f32[304,896]{1,0:T(8,128)}) %reduce-scatter.26.cloned.1.call-update) | async-done | bytes 1089552 | tf_op jit(solution)/shard_map/reduce_scatter | solution.py:452
  1885.0 59.6 %all-reduce.14 = (bf16[896]{0:T(1024)(128)(2,1)S(1)}, bf16[896]{0:T(1024)(128)(2,1)S(1)}, bf16[128]{0:T(256)(128)(2,1)S(1)}, bf16[128]{0:T(256)(128)(2,1)S(1)}, bf16[896]{0:T(1024)(128)(2,1)S(1)}) all-reduce(f32[896]{0:T(1024)S(1)} %add.590, f32[896]{0:T(1024)S(1)} %reshape.1065, ...), channel_id=16, replica_groups=mesh['rep'=2,'shard'=16] {'shard'}, use_global_device_ids=true, to_apply=%region_49.50.clone | all-reduce | flops 2944 | bytes 17664
  1948.8 39.6 %reduce-scatter.32.cloned.1.call-done = f32[56,128]{1,0:T(8,128)} async-done(((f32[896,128]{1,0:T(8,128)}), f32[56,128]{1,0:T(8,128)}) %reduce-scatter.32.cloned.1.call-update) | async-done | bytes 28688
  1989.2 8.3 all-reduce.16
  2001.3 47.1 %all-reduce.20.cloned.1.call-done = (bf16[56,896]{1,0:T(8,128)(2,1)}, bf16[56,896]{1,0:T(8,128)(2,1)}, bf16[56,4864]{1,0:T(8,128)(2,1)}, bf16[56,4864]{1,0:T(8,128)(2,1)}, bf16[304,896]{1,0:T(8,128)(2,1)}) async-done(((bf16[56,896]{1,0:T(8,128)(2,1)}, bf16[56,896]{1,0:T(8,128)(2,1)}, bf16[56,4864]{1,0:T(8,128)(2,1)}, bf16[56,4864]{1,0:T(8,128)(2,1)}, bf16[304,896]{1,0:T(8,128)(2,1)}), ...) | async-done | bytes 1835024 | tf_op jit(solution)/shard_map/psum | solution.py:456
  (1079 shorter events, 570.2 us)
Async XLA Ops:
  7.2 86.4 %copy-start.11 = (bf16[512,896]{1,0:T(8,128)(2,1)S(1)}, bf16[512,896]{1,0:T(8,128)(2,1)}, u32[]{:S(2)}) copy-start(bf16[512,896]{1,0:T(8,128)(2,1)} %param.40) | copy-start | bytes 2752516
  7.2 66.6 %copy-start.80 = (bf16[56,128]{1,0:T(8,128)(2,1)S(1)}, bf16[56,128]{1,0:T(8,128)(2,1)}, u32[]{:S(2)}) copy-start(bf16[56,128]{1,0:T(8,128)(2,1)} %param.49) | copy-start | bytes 43012
  7.2 93.1 %all-gather.10.cloned.1.call-start = ((), (), s32[]{:S(2)}) async-start(), calls=%async_computation.10 | async-start | bytes 1705984 | tf_op jit(solution)/shard_map/all_gather | solution.py:250
  7.9 125.1 %all-gather.20.cloned.1.call-start = ((), (), s32[]{:S(2)}) async-start(), calls=%async_computation.15 | async-start | bytes 2228224 | tf_op jit(solution)/shard_map/all_gather | solution.py:298
  51.8 55.1 %copy-start.76 = (f32[896]{0:T(1024)}, f32[896]{0:T(1024)S(1)}, u32[]{:S(2)}) copy-start(f32[896]{0:T(1024)S(1)} %convert_element_type.345) | copy-start | bytes 10756
  69.9 25.4 %copy-start.57 = (bf16[896,128]{1,0:T(8,128)(2,1)}, bf16[896,128]{1,0:T(8,128)(2,1)S(1)}, u32[]{:S(2)}) copy-start(bf16[896,128]{1,0:T(8,128)(2,1)S(1)} %all_gather.29) | copy-start | bytes 688132
  70.2 25.1 %copy-start.59 = (f32[256,64]{0,1:T(8,128)}, f32[256,64]{0,1:T(8,128)S(1)}, u32[]{:S(2)}) copy-start(f32[256,64]{0,1:T(8,128)S(1)} %get-tuple-element.1709) | copy-start | bytes 196612
  70.2 34.9 %copy-start.51 = (f32[256,64]{0,1:T(8,128)}, f32[256,64]{0,1:T(8,128)S(1)}, u32[]{:S(2)}) copy-start(f32[256,64]{0,1:T(8,128)S(1)} %get-tuple-element.1708) | copy-start | bytes 196612
  72.3 23.4 %copy-start.81 = (f32[256]{0:T(256)}, f32[256]{0:T(256)S(1)}, u32[]{:S(2)}) copy-start(f32[256]{0:T(256)S(1)} %get-tuple-element.1741) | copy-start | bytes 3076
  72.3 28.0 %copy-start.78 = (f32[256]{0:T(256)}, f32[256]{0:T(256)S(1)}, u32[]{:S(2)}) copy-start(f32[256]{0:T(256)S(1)} %get-tuple-element.1720) | copy-start | bytes 3076
  93.6 5.3 copy-start.67
  93.6 6.6 copy-start.95
  94.6 222.2 %all-gather.8.cloned.1.call-start = ((), (), s32[]{:S(2)}) async-start(), calls=%async_computation.9 | async-start | bytes 2228224 | tf_op jit(solution)/shard_map/all_gather | solution.py:298
  94.8 5.5 copy-start.53
  94.8 5.5 copy-start.62
  96.4 330.9 %all-gather.12.cloned.1.call-start = ((), (), s32[]{:S(2)}) async-start(), calls=%async_computation.11 | async-start | bytes 1705984 | tf_op jit(solution)/shard_map/all_gather | solution.py:256
  97.0 334.7 %all-gather.14.cloned.1.call-start = ((), (), s32[]{:S(2)}) async-start(), calls=%async_computation.12 | async-start | bytes 9261056 | tf_op jit(solution)/shard_map/all_gather | solution.py:258
  97.5 342.5 %all-gather.16.cloned.1.call-start = ((), (), s32[]{:S(2)}) async-start(), calls=%async_computation.13 | async-start | bytes 9261056 | tf_op jit(solution)/shard_map/all_gather | solution.py:259
  98.1 350.0 %all-gather.18.cloned.1.call-start = ((), (), s32[]{:S(2)}) async-start(), calls=%async_computation.14 | async-start | bytes 9261056 | tf_op jit(solution)/shard_map/all_gather | solution.py:260
  98.9 880.8 %reduce-scatter.20.cloned.1.call-start = ((), (), s32[]{:S(2)}) async-start(), calls=%async_computation.17 | async-start | bytes 4456448 | tf_op jit(solution)/shard_map/reduce_scatter | solution.py:387
  316.8 113.0 %copy-start.42 = (bf16[256,2,7,64]{0,3,2,1:T(8,128)(2,1)}, bf16[256,2,7,64]{0,3,2,1:T(8,128)(2,1)S(1)}, u32[]{:S(2)}) copy-start(bf16[256,2,7,64]{0,3,2,1:T(8,128)(2,1)S(1)} %copy.159) | copy-start | bytes 1376260
  424.8 6.7 copy-start.24
  431.6 8.5 copy-start.20
  448.2 17.9 copy-start.7
  458.9 7.2 copy-start.26
  458.9 7.2 copy-start.47
  458.9 13.4 slice-start
  458.9 13.4 slice-start.1
  466.1 6.2 slice-start.2
  492.6 5.5 copy-start.48
  492.6 5.5 copy-start.49
  653.2 523.1 %reduce-scatter.18.cloned.1.call-start = ((), (), s32[]{:S(2)}) async-start(), calls=%async_computation.16 | async-start | bytes 4456448 | tf_op jit(solution)/shard_map/reduce_scatter | solution.py:387
  728.7 518.5 %reduce-scatter.28.cloned.1.call-start = ((), (), s32[]{:S(2)}) async-start(), calls=%async_computation.21 | async-start | bytes 3411968
  737.3 580.9 %reduce-scatter.34.cloned.1.call-start = ((), (), s32[]{:S(2)}) async-start(), calls=%async_computation.24 | async-start | bytes 3411968
  740.9 763.6 %reduce-scatter.22.cloned.1.call-start = ((), (), s32[]{:S(2)}) async-start(), calls=%async_computation.18 | async-start | bytes 18522112 | tf_op jit(solution)/shard_map/reduce_scatter | solution.py:450
  755.8 935.5 %reduce-scatter.24.cloned.1.call-start = ((), (), s32[]{:S(2)}) async-start(), calls=%async_computation.19 | async-start | bytes 18522112 | tf_op jit(solution)/shard_map/reduce_scatter | solution.py:451
  770.6 1107.3 %reduce-scatter.26.cloned.1.call-start = ((), (), s32[]{:S(2)}) async-start(), calls=%async_computation.20 | async-start | bytes 18522112 | tf_op jit(solution)/shard_map/reduce_scatter | solution.py:452
  786.3 1161.8 %reduce-scatter.30.cloned.1.call-start = ((), (), s32[]{:S(2)}) async-start(), calls=%async_computation.22 | async-start | bytes 487424
  789.4 7.4 copy-start.28
  789.4 7.3 copy-start.50
  796.7 183.9 %copy-start.61 = (f32[256,64]{0,1:T(8,128)S(1)}, f32[256,64]{0,1:T(8,128)}, u32[]{:S(2)}) copy-start(f32[256,64]{0,1:T(8,128)} %copy-done.59) | copy-start | bytes 196612
  796.7 380.5 %copy-start.65 = (f32[256,64]{0,1:T(8,128)S(1)}, f32[256,64]{0,1:T(8,128)}, u32[]{:S(2)}) copy-start(f32[256,64]{0,1:T(8,128)} %copy-done.62) | copy-start | bytes 196612
  796.7 380.6 %copy-start.56 = (f32[256,64]{0,1:T(8,128)S(1)}, f32[256,64]{0,1:T(8,128)}, u32[]{:S(2)}) copy-start(f32[256,64]{0,1:T(8,128)} %copy-done.53) | copy-start | bytes 196612
  796.7 382.2 %copy-start.13 = (bf16[512,896]{1,0:T(8,128)(2,1)S(1)}, bf16[512,896]{1,0:T(8,128)(2,1)}, u32[]{:S(2)}) copy-start(bf16[512,896]{1,0:T(8,128)(2,1)} %param.40) | copy-start | bytes 2752516
  803.8 376.8 %copy-start.6 = (f32[2,1792,64]{1,2,0:T(8,128)S(1)}, f32[2,1792,64]{1,2,0:T(8,128)}, u32[]{:S(2)}) copy-start(f32[2,1792,64]{1,2,0:T(8,128)} %copy-done.4) | copy-start | bytes 2752516
  980.6 201.5 %copy-start.88 = (f32[896]{0:T(1024)S(1)}, f32[896]{0:T(1024)}, u32[]{:S(2)}) copy-start(f32[896]{0:T(1024)} %get-tuple-element.1492) | copy-start | bytes 10756
  982.3 198.3 %copy-start.70 = (bf16[256,128]{0,1:T(8,128)(2,1)}, bf16[256,128]{0,1:T(8,128)(2,1)S(1)}, u32[]{:S(2)}) copy-start(bf16[256,128]{0,1:T(8,128)(2,1)S(1)} %get-tuple-element.1659) | copy-start | bytes 196612
  1180.5 8.4 copy-start.31
  1180.5 807.9 %reduce-scatter.32.cloned.1.call-start = ((), (), s32[]{:S(2)}) async-start(), calls=%async_computation.23 | async-start | bytes 487424
  1182.1 6.8 copy-start.35
  1184.2 6.3 copy-start.41
  1186.4 861.9 %all-reduce.20.cloned.1.call-start = ((), (), s32[]{:S(2)}) async-start(), calls=%async_computation.25 | async-start | bytes 3670016 | tf_op jit(solution)/shard_map/psum | solution.py:456
  1192.2 687.8 %copy-start.46 = (f32[256,896]{1,0:T(8,128)S(1)}, f32[256,896]{1,0:T(8,128)}, u32[]{:S(2)}) copy-start(f32[256,896]{1,0:T(8,128)} %fusion.122) | copy-start | bytes 2752516
  1192.2 687.8 %copy-start.58 = (bf16[896,128]{1,0:T(8,128)(2,1)S(1)}, bf16[896,128]{1,0:T(8,128)(2,1)}, u32[]{:S(2)}) copy-start(bf16[896,128]{1,0:T(8,128)(2,1)} %copy-done.57) | copy-start | bytes 688132
  1192.2 687.8 %copy-start.71 = (bf16[256,128]{0,1:T(8,128)(2,1)S(1)}, bf16[256,128]{0,1:T(8,128)(2,1)}, u32[]{:S(2)}) copy-start(bf16[256,128]{0,1:T(8,128)(2,1)} %copy-done.70) | copy-start | bytes 196612
  1506.6 373.7 %copy-start.75 = (bf16[256,128]{0,1:T(8,128)(2,1)S(1)}, bf16[256,128]{0,1:T(8,128)(2,1)}, u32[]{:S(2)}) copy-start(bf16[256,128]{0,1:T(8,128)(2,1)} %copy-done.74) | copy-start | bytes 196612
  1693.4 188.7 %copy-start.66 = (f32[256,256]{0,1:T(8,128)S(1)}, f32[256,256]{0,1:T(8,128)}, u32[]{:S(2)}) copy-start(f32[256,256]{0,1:T(8,128)} %reduce-scatter.20.cloned.1.call-done) | copy-start | bytes 786436
  1693.4 188.7 %copy-start.68 = (bf16[896,128]{1,0:T(8,128)(2,1)S(1)}, bf16[896,128]{1,0:T(8,128)(2,1)}, u32[]{:S(2)}) copy-start(bf16[896,128]{1,0:T(8,128)(2,1)} %copy-done.67) | copy-start | bytes 688132
  1880.4 64.6 %copy-start.16 = (f32[256,896]{1,0:T(8,128)S(1)}, f32[256,896]{1,0:T(8,128)}, u32[]{:S(2)}) copy-start(f32[256,896]{1,0:T(8,128)} %get-tuple-element.1686) | copy-start | bytes 2752516
  1880.4 64.6 %copy-start.19 = (f32[256,896]{1,0:T(8,128)S(1)}, f32[256,896]{1,0:T(8,128)}, u32[]{:S(2)}) copy-start(f32[256,896]{1,0:T(8,128)} %copy-done.17) | copy-start | bytes 2752516
  1882.1 63.0 %copy-start.85 = (f32[256]{0:T(256)S(1)}, f32[256]{0:T(256)}, u32[]{:S(2)}) copy-start(f32[256]{0:T(256)} %copy-done.81) | copy-start | bytes 3076
  1882.1 63.0 %copy-start.86 = (f32[256]{0:T(256)S(1)}, f32[256]{0:T(256)}, u32[]{:S(2)}) copy-start(f32[256]{0:T(256)} %get-tuple-element.1719) | copy-start | bytes 3076
  1882.1 63.0 %copy-start.87 = (f32[256]{0:T(256)S(1)}, f32[256]{0:T(256)}, u32[]{:S(2)}) copy-start(f32[256]{0:T(256)} %get-tuple-element.1742) | copy-start | bytes 3076
  2048.4 7.4 copy-start.72
  (60 other events, 140.0 us)
Sparse Core Ops, SparseCore 0:
  10.2 42.7 all-gather.9
  94.8 38.2 all-gather.19
  135.8 40.0 all-gather.7
  177.9 38.7 all-gather.11
  218.7 75.1 all-gather.13
  296.0 74.9 all-gather.15
  373.1 75.0 all-gather.17
  653.3 326.2 reduce-scatter.19
  983.5 192.7 reduce-scatter.17
  1180.0 67.1 reduce-scatter.27
  1251.1 67.0 reduce-scatter.33
  1322.1 182.3 reduce-scatter.21
  1508.7 182.5 reduce-scatter.23
  1695.3 182.5 reduce-scatter.25
  1881.2 51.9 reduce-scatter.29
  1936.6 51.8 reduce-scatter.31
  1992.0 56.3 all-reduce.19
where the time goes:
time: 2080 us; the launch traced here: 2060 us
  waiting for transfers between devices  1160 us (56%)
  matrix products  283 us (14%)
  local copies, waits for them, and re-layouts  209 us (10%)
  other arithmetic  181 us (9%)
  blocking collectives  142 us (7%)
  loops' own time  68.8 us (3%)
    reduce_scatter x2, waiting for transfers between devices, on_device(): lax.psum_scatter(key_grads, 'shard', scatter_dimension=0, tiled=True)  370 us
    reduce_scatter x1, waiting for transfers between devices, on_device(): lax.psum_scatter(terms[9], 'shard', scatter_dimension=0, tiled=True)  185 us
    reduce_scatter x1, waiting for transfers between devices, on_device(): lax.psum_scatter(terms[10], 'shard', scatter_dimension=0, tiled=True)  185 us
    reduce_scatter x1, waiting for transfers between devices, on_device(): lax.psum_scatter(terms[11], 'shard', scatter_dimension=0, tiled=True)  184 us
    unnamed x21, waiting for transfers between devices  167 us
    unnamed x2, blocking collectives  95.7 us
    dynamic_slice x96, local copies, waits for them, and re-layouts, mask_for(): seq_part = lax.dynamic_slice_in_dim(key_seq, block_start, block_keys, 0)  72.5 us
    dot_general x14, matrix products, dot_first(): lax.dot_general(left_side, right_side, (((0,), (0,)), ((), ())), preferre...  56.1 us
  transfers between devices with their start and end apart: 17, of which 11 were waited for; matrix products, arithmetic and copies ran while one was open for 22% of the time, Pallas kernels for 0%

commit v1 on v0

v1 whole, which is shorter than its diff:
```python
import functools

import jax
import jax.numpy as jnp
from jax import lax
from jax.experimental import pallas as pl
from jax.experimental.pallas import tpu as pltpu
from jax.sharding import Mesh
from jax.sharding import PartitionSpec as P

HEADS = 14
KV_HEADS = 2
HEAD_DIM = 64
GROUPS = HEADS // KV_HEADS
TMB = 256
MB = 2
SEQ_MAX = 4096
QW = GROUPS * HEAD_DIM
DIRECT_MAX = 8

norm_eps = 1e-06
rope_base = 1000000.0
masked_score = -1e30

bf16 = jnp.bfloat16
f32 = jnp.float32
NN = ((1,), (0,))
NT = ((1,), (1,))
TN = ((0,), (0,))


def mm(a, b, dims=NN):
    return lax.dot_general(a, b, (dims, ((), ())), preferred_element_type=f32)


def swap(a, axis):
    return lax.ppermute(a, axis, [(0, 1), (1, 0)])


def block_mask(kpos, qinfo, b, j):
    ks = kpos[j] + lax.broadcasted_iota(jnp.int32, (TMB, TMB), 0)
    qs = qinfo[b, 0] + lax.broadcasted_iota(jnp.int32, (TMB, TMB), 1)
    return (ks <= qs) | (ks < qinfo[b, 1])


def each_block(count, kind, b, process):
    def step(j, carry):
        @pl.when(kind[b, j] == 1)
        def _():
            process(j, False)

        @pl.when(kind[b, j] == 2)
        def _():
            process(j, True)

        return carry

    lax.fori_loop(0, count, step, 0)


def forward_kernel(count, kind, kpos, qinfo, q_ref, kv_ref, o_ref, lse_ref, m_s, l_s, acc):
    b = pl.program_id(0)
    m_s[...] = jnp.full_like(m_s, masked_score)
    l_s[...] = jnp.zeros_like(l_s)
    acc[...] = jnp.zeros_like(acc)

    def process(j, masked):
        k_rows = kv_ref[j, :HEAD_DIM, :].T
        v_cols = kv_ref[j, HEAD_DIM:, :]
        if masked:
            ok = block_mask(kpos, qinfo, b, j)
        for h in range(GROUPS):
            hs = slice(h * HEAD_DIM, (h + 1) * HEAD_DIM)
            s = mm(k_rows, q_ref[hs, :])
            if masked:
                s = jnp.where(ok, s, masked_score)
            old_max = m_s[h : h + 1, :]
            new_max = jnp.maximum(old_max, jnp.max(s, axis=0, keepdims=True))
            p = jnp.exp(s - new_max)
            fade = jnp.exp(old_max - new_max)
            m_s[h : h + 1, :] = new_max
            l_s[h : h + 1, :] = l_s[h : h + 1, :] * fade + jnp.sum(p, axis=0, keepdims=True)
            acc[hs, :] = acc[hs, :] * fade + mm(v_cols, p.astype(bf16))

    each_block(count, kind, b, process)
    for h in range(GROUPS):
        hs = slice(h * HEAD_DIM, (h + 1) * HEAD_DIM)
        o_ref[hs, :] = acc[hs, :] / l_s[h : h + 1, :]
    lse_ref[...] = m_s[...] + jnp.log(l_s[...])


def attention_forward(kind, kpos, qinfo, q_cols, kv):
    count = kv.shape[0]
    grid_spec = pltpu.PrefetchScalarGridSpec(
        num_scalar_prefetch=3,
        grid=(2,),
        in_specs=[
            pl.BlockSpec((QW, TMB), lambda b, *_: (0, b)),
            pl.BlockSpec((count, 2 * HEAD_DIM, TMB), lambda b, *_: (0, 0, 0)),
        ],
        out_specs=[
            pl.BlockSpec((QW, TMB), lambda b, *_: (0, b)),
            pl.BlockSpec((8, TMB), lambda b, *_: (0, b)),
        ],
        scratch_shapes=[
            pltpu.VMEM((8, TMB), f32),
            pltpu.VMEM((8, TMB), f32),
            pltpu.VMEM((QW, TMB), f32),
        ],
    )
    pairs = count * TMB * TMB * GROUPS
    return pl.pallas_call(
        functools.partial(forward_kernel, count),
        grid_spec=grid_spec,
        out_shape=[
            jax.ShapeDtypeStruct((QW, 2 * TMB), f32),
            jax.ShapeDtypeStruct((8, 2 * TMB), f32),
        ],
        cost_estimate=pl.CostEstimate(
            flops=pairs * 16 * HEAD_DIM,
            transcendentals=pairs,
            bytes_accessed=count * TMB * 4 * HEAD_DIM,
        ),
        compiler_params=pltpu.CompilerParams(dimension_semantics=("arbitrary",)),
        name="attention_forward",
    )(kind, kpos, qinfo, q_cols, kv)


def backward_kernel(
    count, kind, kpos, qinfo, q_ref, kv_ref, do_ref, lse_ref, delta_ref, dq_ref, dkv_ref
):
    b = pl.program_id(0)

    @pl.when(b == 0)
    def _():
        dkv_ref[...] = jnp.zeros_like(dkv_ref)

    dq_ref[...] = jnp.zeros_like(dq_ref)

    def process(j, masked):
        k_cols = kv_ref[j, :HEAD_DIM, :]
        k_rows = k_cols.T
        v_rows = kv_ref[j, HEAD_DIM:, :].T
        if masked:
            ok = block_mask(kpos, qinfo, b, j)
        dk = dv = None
        for h in range(GROUPS):
            hs = slice(h * HEAD_DIM, (h + 1) * HEAD_DIM)
            s = mm(k_rows, q_ref[hs, :])
            if masked:
                s = jnp.where(ok, s, masked_score)
            p = jnp.exp(s - lse_ref[h : h + 1, :])
            dp = mm(v_rows, do_ref[hs, :])
            ds = (p * (dp - delta_ref[h : h + 1, :])).astype(bf16)
            dq_ref[hs, :] += mm(k_cols, ds)
            dk_part = mm(q_ref[hs, :], ds, NT)
            dv_part = mm(do_ref[hs, :], p.astype(bf16), NT)
            dk = dk_part if dk is None else dk + dk_part
            dv = dv_part if dv is None else dv + dv_part
        dkv_ref[j, :HEAD_DIM, :] += dk
        dkv_ref[j, HEAD_DIM:, :] += dv

    each_block(count, kind, b, process)


def attention_backward(kind, kpos, qinfo, q_cols, kv, do_cols, lse, delta):
    count = kv.shape[0]
    grid_spec = pltpu.PrefetchScalarGridSpec(
        num_scalar_prefetch=3,
        grid=(2,),
        in_specs=[
            pl.BlockSpec((QW, TMB), lambda b, *_: (0, b)),
            pl.BlockSpec((count, 2 * HEAD_DIM, TMB), lambda b, *_: (0, 0, 0)),
            pl.BlockSpec((QW, TMB), lambda b, *_: (0, b)),
            pl.BlockSpec((8, TMB), lambda b, *_: (0, b)),
            pl.BlockSpec((8, TMB), lambda b, *_: (0, b)),
        ],
        out_specs=[
            pl.BlockSpec((QW, TMB), lambda b, *_: (0, b)),
            pl.BlockSpec((count, 2 * HEAD_DIM, TMB), lambda b, *_: (0, 0, 0)),
        ],
    )
    pairs = count * TMB * TMB * GROUPS
    return pl.pallas_call(
        functools.partial(backward_kernel, count),
        grid_spec=grid_spec,
        out_shape=[
            jax.ShapeDtypeStruct((QW, 2 * TMB), f32),
            jax.ShapeDtypeStruct((count, 2 * HEAD_DIM, TMB), f32),
        ],
        cost_estimate=pl.CostEstimate(
            flops=pairs * 24 * HEAD_DIM,
            transcendentals=pairs,
            bytes_accessed=count * TMB * 12 * HEAD_DIM,
        ),
        compiler_params=pltpu.CompilerParams(dimension_semantics=("arbitrary",)),
        name="attention_backward",
    )(kind, kpos, qinfo, q_cols, kv, do_cols, lse, delta)


def rotate(values, cosine, sine):
    half = HEAD_DIM // 2
    low, high = values[:, :half], values[:, half:]
    return jnp.concatenate([low * cosine - high * sine, high * cosine + low * sine], axis=1)


def unrotate(grads, cosine, sine):
    half = HEAD_DIM // 2
    low, high = grads[:, :half], grads[:, half:]
    return jnp.concatenate([low * cosine + high * sine, high * cosine - low * sine], axis=1)


def ordered(first, own, other, axis):
    return jnp.where(
        first, jnp.concatenate([own, other], axis), jnp.concatenate([other, own], axis)
    )


def on_device(
    tokens,
    cotangent,
    place,
    prefix,
    attn_norm,
    q_weight,
    q_bias,
    k_weight,
    k_bias,
    v_weight,
    v_bias,
    o_weight,
    mlp_norm,
    gate_weight,
    up_projection_weight,
    down_weight,
):
    chips = lax.axis_size("chip")
    chip = lax.axis_index("chip")
    core = lax.axis_index("core")
    rep = lax.axis_index("rep")
    lead_core = core == 0
    lead_rep = rep == 0
    direct = chips <= DIRECT_MAX
    width = q_weight.shape[1]
    rows = q_weight.shape[0]
    seq_length = min(SEQ_MAX, TMB * chips * 2)
    block_count = 2 * chips

    def gather_chips(a):
        if not direct:
            return lax.all_gather(a, "chip", axis=0, tiled=False)
        parts = [a]
        for k in range(1, chips):
            parts.append(lax.ppermute(a, "chip", [(i, (i + k) % chips) for i in range(chips)]))
        return jnp.stack(parts, axis=0)

    def back_to_chips(chunk_of, order_stack):
        if not direct:
            return lax.psum_scatter(
                order_stack().astype(bf16), "chip", scatter_dimension=0, tiled=False
            ).astype(f32)
        total = chunk_of(0).astype(f32)
        for k in range(1, chips):
            sent = lax.ppermute(
                chunk_of(k).astype(bf16), "chip", [(i, (i - k) % chips) for i in range(chips)]
            )
            total = total + sent.astype(f32)
        return total

    def scatter_chips(stacked):
        def chunk_of(k):
            return lax.dynamic_index_in_dim(stacked, (chip - k) % chips, 0, keepdims=False)

        return back_to_chips(chunk_of, lambda: stacked)

    order = (chip - jnp.arange(chips)) % chips if direct else jnp.arange(chips)
    own_slot = 0 if direct else chip

    with jax.named_scope("weights_qkv"):
        row_pad = -(-(rows + 1) // 16) * 16 - rows - 1
        vectors = jnp.concatenate([attn_norm, mlp_norm, q_bias, k_bias, v_bias])
        vec_count = vectors.shape[0]
        vectors = jnp.pad(vectors, (0, QW + 2 * HEAD_DIM - vec_count))[None]

        def head_columns(c):
            part = jnp.concatenate(
                [
                    q_weight[:, c * QW : (c + 1) * QW],
                    k_weight[:, c * HEAD_DIM : (c + 1) * HEAD_DIM],
                    v_weight[:, c * HEAD_DIM : (c + 1) * HEAD_DIM],
                ],
                axis=1,
            )
            return jnp.pad(jnp.concatenate([part, vectors], axis=0), ((0, row_pad), (0, 0)))

        columns = (head_columns(0), head_columns(1))
        own_columns = jnp.where(lead_core, columns[0], columns[1])
        sent_columns = jnp.where(lead_core, columns[1], columns[0])
        chip_rows = ordered(lead_core, own_columns[None], swap(sent_columns, "core")[None], 0)
        qkv_all = lax.all_gather(chip_rows, "chip", axis=0, tiled=False)
        qkv_full = qkv_all[:, :, :rows].reshape(width, QW + 2 * HEAD_DIM)
        vec_all = qkv_all[:, :, rows, :vec_count].reshape(2 * chips, vec_count).astype(f32)
        kv_rows = k_bias.shape[0]
        gain_one = vec_all[:, :rows].reshape(1, width)
        gain_two = vec_all[:, rows : 2 * rows].reshape(1, width)
        q_add = vec_all[:, 2 * rows : 3 * rows].reshape(2, QW)
        k_add = vec_all[:, 3 * rows : 3 * rows + kv_rows].reshape(2, HEAD_DIM)
        v_add = vec_all[:, 3 * rows + kv_rows :].reshape(2, HEAD_DIM)
        biases = jnp.concatenate([q_add, k_add, v_add], axis=1)
        bias_col = jnp.where(lead_core, biases[0], biases[1])[:, None]

    with jax.named_scope("weights_mlp"):
        ff_rows = down_weight.shape[0]
        half_rows = ff_rows // 2
        half_pad = -(-half_rows // 16) * 16
        quarter = chips * half_pad

        def quarter_columns(w, c):
            split = w.reshape(rows, chips, 2, 2, half_rows)[:, :, c]
            part = jnp.where(lead_rep, split[:, :, 0], split[:, :, 1])
            return jnp.pad(part, ((0, 0), (0, 0), (0, half_pad - half_rows))).reshape(rows, quarter)

        def quarter_pair(c):
            return jnp.concatenate(
                [quarter_columns(gate_weight, c), quarter_columns(up_projection_weight, c)], axis=1
            )

        pairs = (quarter_pair(0), quarter_pair(1))
        own_pair = jnp.where(lead_core, pairs[0], pairs[1])
        sent_pair = jnp.where(lead_core, pairs[1], pairs[0])
        pair_rows = ordered(lead_core, own_pair, swap(sent_pair, "core"), 0)
        gate_up = lax.all_gather(pair_rows, "chip", axis=0, tiled=True)
        down_half = jnp.where(lead_rep, down_weight[:half_rows], down_weight[half_rows:])
        down_half = jnp.pad(down_half, ((0, half_pad - half_rows), (0, 0)))
        o_full = lax.all_gather(o_weight, ("chip", "core"), axis=0, tiled=True)
        down = lax.all_gather(down_half, "chip", axis=0, tiled=True)

    with jax.named_scope("visibility"):
        starts = place.reshape(-1, TMB)[:, 0].reshape(2, chips, 2, MB)
        starts = jnp.where(lead_rep, starts[0], starts[1])
        starts = jnp.where(lead_core, starts, starts[:, ::-1])
        key_starts = starts[order]
        own_starts = starts[chip]
        seq_ids = jnp.arange(prefix.shape[0])
        tables = []
        for m in range(MB):
            ks = key_starts[:, :, m].reshape(block_count)
            qs = own_starts[:, m]
            k_seq, k_pos = ks // seq_length, ks % seq_length
            q_seq, q_pos = qs // seq_length, qs % seq_length
            limit = jnp.sum(
                jnp.where(q_seq[:, None] == seq_ids[None], prefix[None], 0), axis=1
            )
            same = k_seq[None] == q_seq[:, None]
            kp, qp, lim = k_pos[None], q_pos[:, None], limit[:, None]
            full = same & ((kp + TMB - 1 <= qp) | (kp + TMB <= lim))
            part = same & ((kp <= qp + TMB - 1) | (kp < lim))
            kind = jnp.where(full, 1, jnp.where(part, 2, 0)).astype(jnp.int32)
            tables.append((kind, k_pos.astype(jnp.int32), jnp.stack([q_pos, limit], 1)))

    exponent = jnp.arange(HEAD_DIM // 2).astype(f32) * (2.0 / HEAD_DIM)
    frequency = (rope_base ** (-exponent))[:, None]

    def group_rows(a):
        both = jnp.concatenate([a, swap(a, "rep")], axis=0)
        return jnp.concatenate([both, swap(both, "core")], axis=0)

    def group_sum(a):
        half = a.shape[0] // 2
        s = a[:half] + swap(a[half:].astype(bf16), "core").astype(f32)
        half = half // 2
        return s[:half] + swap(s[half:].astype(bf16), "rep").astype(f32)

    def core_pair_sum(a):
        half = a.shape[0] // 2
        return a[:half] + swap(a[half:].astype(bf16), "core").astype(f32)

    fwd = []
    for m in range(MB):
        ms = slice(m * TMB, (m + 1) * TMB)
        with jax.named_scope("project"):
            own = tokens[ms]
            x = own.astype(f32)
            pair = jnp.concatenate([own, swap(own, "core")], axis=0)
            pair_f = pair.astype(f32)
            r_pair = lax.rsqrt(jnp.mean(pair_f * pair_f, axis=-1, keepdims=True) + norm_eps)
            normed = (pair_f * r_pair * gain_one).astype(bf16)
            qkv = mm(qkv_full, normed, ((0,), (1,))) + bias_col
            pos = (tables[m][2][:, :1] + jnp.arange(TMB)[None]).reshape(1, 2 * TMB)
            angles = frequency * pos.astype(f32)
            cosine, sine = jnp.cos(angles)[None], jnp.sin(angles)[None]
            q_rot = rotate(qkv[:QW].reshape(GROUPS, HEAD_DIM, 2 * TMB), cosine, sine)
            q_cols = (q_rot.astype(bf16) * HEAD_DIM**-0.5).astype(bf16).reshape(QW, 2 * TMB)
            k_rot = rotate(qkv[None, QW : QW + HEAD_DIM], cosine, sine)[0].astype(bf16)
            v_cols = qkv[QW + HEAD_DIM :].astype(bf16)
            kv_own = jnp.concatenate([k_rot, v_cols], axis=0)
            kv_own = jnp.stack([kv_own[:, :TMB], kv_own[:, TMB:]], axis=0)
        with jax.named_scope("gather_keys"):
            kv = gather_chips(kv_own).reshape(block_count, 2 * HEAD_DIM, TMB)
        with jax.named_scope("gather_cotangent"):
            cot_group = group_rows(cotangent[ms])
        fwd.append((x, r_pair, normed, cosine, sine, q_cols, kv, cot_group))

    outs, mid = [], []
    for m in range(MB):
        x, r_pair, normed, cosine, sine, q_cols, kv, cot_group = fwd[m]
        heads, lse = attention_forward(*tables[m], q_cols, kv)
        with jax.named_scope("attention_out"):
            att = heads.astype(bf16)
            att_cols = ordered(lead_core, att[:, :TMB], swap(att[:, TMB:], "core"), 0)
            middle = x + mm(att_cols, o_full, TN)
            r2 = lax.rsqrt(jnp.mean(middle * middle, axis=-1, keepdims=True) + norm_eps)
            normed_two = (middle * r2 * gain_two).astype(bf16)
            n2_group = group_rows(normed_two)
        with jax.named_scope("feed_forward"):
            gate_up_pre = mm(n2_group, gate_up)
            gate, up = gate_up_pre[:, :quarter], gate_up_pre[:, quarter:]
            sig = jax.nn.sigmoid(gate)
            silu = gate * sig
            hidden = (silu * up).astype(bf16)
            outs.append((middle + group_sum(mm(hidden, down))).astype(bf16))
        with jax.named_scope("feed_forward_grad"):
            dh = mm(cot_group, down, NT)
            dgate = (dh * up * (sig * (1.0 + gate * (1.0 - sig)))).astype(bf16)
            dup = (dh * silu).astype(bf16)
            dgu = jnp.concatenate([dgate, dup], axis=1)
            dn2 = group_sum(mm(dgu, gate_up, NT))
        mid.append((heads, lse, att_cols, middle, r2, n2_group, hidden, dgu, dn2))

    with jax.named_scope("feed_forward_weight_grads"):
        down_grad = sum(mm(mid[m][6], fwd[m][7], TN) for m in range(MB))
        down_share = lax.psum_scatter(
            down_grad.astype(bf16), "chip", scatter_dimension=0, tiled=True
        )
        gate_up_grad = sum(mm(mid[m][5], mid[m][7], TN) for m in range(MB))
        gate_up_share = lax.psum_scatter(
            gate_up_grad.astype(bf16), "chip", scatter_dimension=0, tiled=True
        )

    o_grad = 0.0
    gain_two_grad = 0.0
    back = []
    for m in range(MB):
        heads, lse, att_cols, middle, r2, _, _, _, dn2 = mid[m]
        x, r_pair, normed, cosine, sine, q_cols, kv, _ = fwd[m]
        ms = slice(m * TMB, (m + 1) * TMB)
        with jax.named_scope("attention_out_grad"):
            gain_two_grad = gain_two_grad + jnp.sum(dn2 * (middle * r2), axis=0)
            e = dn2 * gain_two
            dmiddle = (
                cotangent[ms].astype(f32)
                + r2 * e
                - middle * r2**3 * jnp.mean(e * middle, axis=-1, keepdims=True)
            )
            dbranch = dmiddle.astype(bf16)
            o_grad = o_grad + mm(att_cols, dbranch)
            datt = mm(o_full, dbranch, NT).astype(bf16)
            own_datt = jnp.where(lead_core, datt[:QW], datt[QW:])
            sent_datt = jnp.where(lead_core, datt[QW:], datt[:QW])
            do_cols = jnp.concatenate([own_datt, swap(sent_datt, "core")], axis=1)
            delta = jnp.sum(
                (do_cols.astype(f32) * heads).reshape(GROUPS, HEAD_DIM, 2 * TMB), axis=1
            )
            delta = jnp.pad(delta, ((0, 8 - GROUPS), (0, 0)))
        dq, dkv = attention_backward(*tables[m], q_cols, kv, do_cols, lse, delta)
        with jax.named_scope("return_keys"):
            dkv = dkv.reshape(chips, 2, 2 * HEAD_DIM, TMB)
            dkv_own = back_to_chips(lambda k: dkv[k], lambda: dkv)
            dkv_own = jnp.concatenate([dkv_own[0], dkv_own[1]], axis=1)
        with jax.named_scope("unrotate"):
            dq = unrotate(
                dq.reshape(GROUPS, HEAD_DIM, 2 * TMB) * HEAD_DIM**-0.5, cosine, sine
            ).reshape(QW, 2 * TMB)
            dk = unrotate(dkv_own[None, :HEAD_DIM], cosine, sine)[0]
            dq = dq.astype(bf16)
            dkv_low = jnp.concatenate([dk, dkv_own[HEAD_DIM:]], axis=0).astype(bf16)
        back.append((dmiddle, dq, dkv_low))

    with jax.named_scope("o_weight_grad"):
        o_parts = o_grad.reshape(chips, 2, rows, width)
        o_own = jnp.where(lead_core, o_parts[:, 0], o_parts[:, 1])
        o_sent = jnp.where(lead_core, o_parts[:, 1], o_parts[:, 0])
        o_own = o_own + swap(o_sent.astype(bf16), "core").astype(f32)
        o_share = scatter_chips(o_own)

    with jax.named_scope("project_grad"):
        q_grad = sum(mm(fwd[m][2], back[m][1], ((0,), (1,))) for m in range(MB))
        q_share = scatter_chips(q_grad.reshape(chips, 2 * rows, QW))
        kv_grad = sum(mm(fwd[m][2], back[m][2], ((0,), (1,))) for m in range(MB))
        bias_grad = sum(
            jnp.concatenate(
                [
                    jnp.sum(back[m][1].astype(f32), axis=1),
                    jnp.sum(back[m][2].astype(f32), axis=1),
                ]
            )
            for m in range(MB)
        )
        gain_one_grad = 0.0
        grads_in = []
        for m in range(MB):
            x, r_pair, normed = fwd[m][:3]
            dmiddle, dq, dkv_low = back[m]
            dn1 = core_pair_sum(
                mm(dq, qkv_full[:, :QW], ((0,), (1,)))
                + mm(dkv_low, qkv_full[:, QW:], ((0,), (1,)))
            )
            r1 = r_pair[:TMB]
            gain_one_grad = gain_one_grad + jnp.sum(dn1 * (x * r1), axis=0)
            e1 = dn1 * gain_one
            dx = dmiddle + r1 * e1 - x * r1**3 * jnp.mean(e1 * x, axis=-1, keepdims=True)
            grads_in.append(dx.astype(bf16))

    with jax.named_scope("shares"):
        kv_width = 2 * HEAD_DIM
        packed = jnp.concatenate([bias_grad, gain_one_grad, gain_two_grad])
        pack_count = packed.shape[0]
        pack_rows = -(-pack_count // (kv_width * 16)) * 16
        packed = jnp.pad(packed, (0, pack_rows * kv_width - pack_count)).reshape(
            pack_rows, kv_width
        )
        tail = jnp.concatenate(
            [
                kv_grad.reshape(chips, 2 * rows, kv_width),
                jnp.broadcast_to(packed[None], (chips, pack_rows, kv_width)),
            ],
            axis=1,
        )
        tail_share = scatter_chips(tail)

    def rows_of_core(a):
        own = jnp.where(lead_core, a[:rows], a[rows:])
        sent = jnp.where(lead_core, a[rows:], a[:rows])
        return own, swap(sent, "core")

    def rep_sum(a):
        low = a.astype(bf16)
        return low.astype(f32) + swap(low, "rep").astype(f32)

    with jax.named_scope("owners"):
        o_total = rep_sum(o_share)
        q_own, q_other = rows_of_core(q_share.astype(bf16))
        q_total = rep_sum(ordered(lead_core, q_own, q_other, 1))
        kv_own, kv_other = rows_of_core(tail_share[: 2 * rows].astype(bf16))
        kv_total = rep_sum(ordered(lead_core, kv_own[:, None], kv_other[:, None], 1))
        k_total = kv_total[:, :, :HEAD_DIM].reshape(rows, kv_width)
        v_total = kv_total[:, :, HEAD_DIM:].reshape(rows, kv_width)
        vec = tail_share[2 * rows :].reshape(-1)[:pack_count]
        vec_other = swap(vec.astype(bf16)[None], "core").astype(f32)[0]
        col_count = QW + kv_width
        b_own, b_other = vec[:col_count], vec_other[:col_count]
        bias_all = ordered(lead_core, b_own[None], b_other[None], 0)
        q_b = bias_all[:, :QW].reshape(2 * QW)
        k_b = bias_all[:, QW : QW + HEAD_DIM].reshape(2 * HEAD_DIM)
        v_b = bias_all[:, QW + HEAD_DIM :].reshape(2 * HEAD_DIM)
        gains = vec[col_count:] + vec_other[col_count:]
        everything = rep_sum(jnp.concatenate([q_b, k_b, v_b, gains])[None])[0]
        shard = 2 * chip + core
        sizes = (2 * QW, 2 * HEAD_DIM, 2 * HEAD_DIM, width, width)
        vec_outs, offset = [], 0
        for size in sizes:
            each = size // (2 * chips)
            vec_outs.append(lax.dynamic_slice_in_dim(everything, offset + shard * each, each, 0))
            offset += size
        q_b, k_b, v_b, gain_one_out, gain_two_out = vec_outs

        def whole_columns(part):
            own, other = rows_of_core(part)
            two = ordered(lead_core, own[None], other[None], 0)
            four = ordered(lead_rep, two[None], swap(two, "rep")[None], 0)
            four = four.reshape(2, 2, rows, chips, half_pad)[..., :half_rows]
            return four.transpose(2, 3, 1, 0, 4).reshape(rows, 4 * chips * half_rows).astype(f32)

        gate_out = whole_columns(gate_up_share[:, :quarter])
        up_out = whole_columns(gate_up_share[:, quarter:])
        down_mine = down_share[:half_rows]
        down_out = ordered(lead_rep, down_mine, swap(down_mine, "rep"), 0).astype(f32)

    return (
        jnp.concatenate(outs, axis=0),
        jnp.concatenate(grads_in, axis=0),
        gain_one_out,
        q_total,
        q_b,
        k_total,
        k_b,
        v_total,
        v_b,
        o_total,
        gain_two_out,
        gate_out,
        up_out,
        down_out,
    )


def solution(mesh):
    split = Mesh(mesh.devices.reshape(mesh.shape["rep"], -1, 2), ("rep", "chip", "core"))
    shard = ("chip", "core")
    token_spec = P(("rep", "chip", "core"), None)
    row_spec, vec_spec = P(shard, None), P(shard)
    in_specs = (
        token_spec,
        token_spec,
        P(),
        P(),
        vec_spec,
        row_spec,
        vec_spec,
        row_spec,
        vec_spec,
        row_spec,
        vec_spec,
        row_spec,
        vec_spec,
        row_spec,
        row_spec,
        row_spec,
    )
    out_specs = (token_spec, token_spec) + in_specs[4:]
    return jax.shard_map(
        on_device, mesh=split, in_specs=in_specs, out_specs=out_specs, check_vma=False
    )
```

time: 2080 us -> 801 us (0.39)
  waiting for transfers between devices: 1160 us -> 145 us
  starting transfers between devices: 1.48 us -> 229 us
  matrix products: 283 us -> 108 us
  blocking collectives: 142 us -> 0 us
  Pallas kernels: 0 us -> 128 us
  local copies, waits for them, and re-layouts: 209 us -> 93.8 us
  other arithmetic: 181 us -> 66.6 us
  loops' own time: 68.8 us -> 0 us
    reduce_scatter x5 -> x2, waiting for transfers between devices: 924 us -> 0.01 us  [the longest x1 0.01 us: on_device(): lax.psum_scatter(down_grad.astype(bf16), 'chip', scatter_dimension=0, til...]
    ppermute x0 -> x88, starting transfers between devices: none -> 228 us  [the longest x35 144 us: back_to_chips(): lax.ppermute(chunk_of(k).astype(bf16), 'chip', [(i, (i - k) % chips) for...]
    dot_general x112 -> x28, matrix products: 283 us -> 108 us  [mm(): return lax.dot_general(a, b, (dims, ((), ())), preferred_element_type=f32)]
    unnamed x21 -> x6, waiting for transfers between devices: 167 us -> 0.78 us
    pallas_call x0 -> x4, Pallas kernels: none -> 128 us  [the longest x2 68.3 us: attention_backward(): pl.pallas_call(functools.partial(backward_kernel, count), grid_spec=grid_...]
    reduce_or x96 -> x0, other arithmetic: 106 us -> none  [the longest x32 35.3 us: grad_step(): return lax.cond(jnp.any(wide_mask), grad_compute, unchanged, state)]
    dynamic_slice x194 -> x5, local copies, waits for them, and re-layouts: 113 us -> 12 us  [the longest x3 10.8 us: chunk_of(): lax.dynamic_index_in_dim(stacked, (chip - k) % chips, 0, keepdims=False)]
    unnamed x2 -> x0, blocking collectives: 95.7 us -> none
  transfers between devices with their start and end apart: 17 -> 94, of which waited for: 11 -> 30; matrix products, arithmetic and copies ran while one was open for 22% -> 31% of each run, Pallas kernels for 0% -> 16%
where the time goes in v1:
time: 801 us; the launch traced here: 787 us
  starting transfers between devices  229 us (29%)
  waiting for transfers between devices  145 us (18%)
  Pallas kernels  128 us (16%)
  matrix products  108 us (13%)
  local copies, waits for them, and re-layouts  93.8 us (12%)
  other arithmetic  66.6 us (8%)
  between operations  17 us (2%)
    ppermute x35, starting transfers between devices, back_to_chips(): lax.ppermute(chunk_of(k).astype(bf16), 'chip', [(i, (i - k) % chips) for...  144 us
    dot_general x28, matrix products, mm(): return lax.dot_general(a, b, (dims, ((), ())), preferred_element_type=f32)  108 us
    pallas_call x2, Pallas kernels, attention_backward(): pl.pallas_call(functools.partial(backward_kernel, count), grid_spec=grid_...  68.3 us
    pallas_call x2, Pallas kernels, attention_forward(): pl.pallas_call(functools.partial(forward_kernel, count), grid_spec=grid_s...  59.3 us
    ppermute x39, waiting for transfers between devices, swap(): return lax.ppermute(a, axis, [(0, 1), (1, 0)])  53.1 us
    ppermute x14, starting transfers between devices, gather_chips(): lax.ppermute(a, 'chip', [(i, (i + k) % chips) for i in range(chips)])  51.4 us
    all_gather x1, waiting for transfers between devices, on_device(): down = lax.all_gather(down_half, 'chip', axis=0, tiled=True)  41.5 us
    ppermute x39, starting transfers between devices, swap(): return lax.ppermute(a, axis, [(0, 1), (1, 0)])  33.1 us
  transfers between devices with their start and end apart: 94, of which 30 were waited for; matrix products, arithmetic and copies ran while one was open for 31% of the time, Pallas kernels for 16%

profile of v1, /device:TPU:0, one launch (start us, length us, event | category | flops | bytes accessed | tf_op | source)
XLA Modules:
  0.0 787.3 jit_solution(17830662085271376253)
XLA Ops:
  7.2 3.5 concatenate.308
  15.8 2.5 reshape.1071
  18.9 2.5 reshape.1069
  30.9 2.9 collective-permute-start.28
  42.1 3.4 collective-permute-done.28
  46.8 12.8 %all-gather.5.cloned.1.call-done = bf16[8,2,64,576]{3,2,1,0:T(8,128)(2,1)} async-done(((bf16[1,2,64,576]{3,2,1,0:T(8,128)(2,1)}), bf16[8,2,64,576]{3,2,1,0:T(8,128)(2,1)}) %all-gather.5.cloned.1.call-update) | async-done | bytes 1179664 | tf_op jit(solution)/shard_map/weights_qkv/all_gather | solution.py:300
  74.3 4.2 collective-permute-done.2
  79.2 14.1 %collective-permute-start.6 = (bf16[2,128,256]{2,1,0:T(8,128)(2,1)S(1)}, bf16[2,128,256]{2,1,0:T(8,128)(2,1)S(1)}, u32[]{:S(2)}, u32[]{:S(2)}) collective-permute-start(bf16[2,128,256]{2,1,0:T(8,128)(2,1)S(1)} %pad_maximum_fusion.34), channel_id=1, source_target_pairs={{0,10},{2,12},{4,14},{6,0},{8,2},{10,4},{12,6},{14,8},{1,11},{3,13... | collective-permute-start | bytes 393224 | tf_op jit(solution)/shard_map/gather_keys/ppermute | solution.py:254
  93.9 2.6 collective-permute-start.7
  100.5 2.6 collective-permute-done.7
  103.8 4.5 collective-permute-done.8
  108.9 44.1 %attention_forward.2 = (f32[448,512]{1,0:T(8,128)}, f32[8,512]{1,0:T(8,128)}) custom-call(s32[2,16]{1,0:T(2,128)} %fusion.150.kind, s32[16]{0:T(128)} %copy-done.96, s32[2,2]{1,0:T(2,128)} %pad_add_fusion.qinfo, bf16[448,512]{1,0:T(8,128)(2,1)} %bitcast.329, bf16[16,128,256]{2,1,0:T(8,128)(2,1)} %bitcast.355), custom_call_target="tpu_custom_call" | custom-call | flops 7516192768 | bytes 1048576 | tf_op jit(solution)/shard_map/attention_forward/pallas_call | solution.py:112
  158.7 3.0 collective-permute-start.10
  162.4 4.0 collective-permute-start.20
  168.0 4.3 collective-permute-done.10
  172.3 14.5 %collective-permute-start.21 = (bf16[2,128,256]{2,1,0:T(8,128)(2,1)S(1)}, bf16[2,128,256]{2,1,0:T(8,128)(2,1)S(1)}, u32[]{:S(2)}, u32[]{:S(2)}) collective-permute-start(bf16[2,128,256]{2,1,0:T(8,128)(2,1)S(1)} %pad_maximum_fusion.35), channel_id=1, source_target_pairs={{0,12},{2,14},{4,0},{6,2},{8,4},{10,6},{12,8},{14,10},{1,13},{3,15... | collective-permute-start | bytes 393224 | tf_op jit(solution)/shard_map/gather_keys/ppermute | solution.py:254
  188.5 9.9 %collective-permute-start.22 = (bf16[2,128,256]{2,1,0:T(8,128)(2,1)S(1)}, bf16[2,128,256]{2,1,0:T(8,128)(2,1)S(1)}, u32[]{:S(2)}, u32[]{:S(2)}) collective-permute-start(bf16[2,128,256]{2,1,0:T(8,128)(2,1)S(1)} %pad_maximum_fusion.35), channel_id=1, source_target_pairs={{0,14},{2,0},{4,2},{6,4},{8,6},{10,8},{12,10},{14,12},{1,15},{3,1}... | collective-permute-start | bytes 393224 | tf_op jit(solution)/shard_map/gather_keys/ppermute | solution.py:254
  199.8 4.0 collective-permute-done.22
  204.4 6.3 all-gather.9.cloned.1.call-done
  210.7 10.3 %fusion.38 = f32[1024,2560]{1,0:T(8,128)} fusion(bf16[896,2560]{1,0:T(8,128)(2,1)} %all-gather.9.cloned.1.call-done, bf16[512,896]{1,0:T(8,128)(2,1)} %collective-permute-done.11, bf16[256,896]{1,0:T(8,128)(2,1)} %copy-done.66, bf16[256,896]{1,0:T(8,128)(2,1)S(1)} %multiply_convert_fusion.7), kind=kOutput, calls=%fused_computation.150 | convolution fusion | flops 4703125504 | bytes 16908288 | tf_op jit(solution)/shard_map/feed_forward/dot_general | solution.py:33
  221.0 41.5 %all-gather.11.cloned.1.call-done = bf16[1280,896]{1,0:T(8,128)(2,1)} async-done(((bf16[160,896]{1,0:T(8,128)(2,1)}), bf16[1280,896]{1,0:T(8,128)(2,1)}) %all-gather.11.cloned.1.call-update) | async-done | bytes 2293776 | tf_op jit(solution)/shard_map/weights_mlp/all_gather | solution.py:336
  262.5 9.9 %multiply_convert_fusion.3 = (bf16[1024,1280]{1,0:T(8,128)(2,1)S(1)}, bf16[1024,1280]{1,0:T(8,128)(2,1)S(1)}, bf16[1024,1280]{1,0:T(8,128)(2,1)}) fusion(f32[1024,2560]{1,0:T(8,128)} %fusion.38, bf16[1280,896]{1,0:T(8,128)(2,1)} %all-gather.11.cloned.1.call-done, bf16[512,896]{1,0:T(8,128)(2,1)} %collective-permute-done.29, ...), kind=kOutput, calls=%fused_computation.7 | convolution fusion | flops 2373976064 | bytes 22478848 | tf_op jit(solution)/shard_map/feed_forward_grad/dot_general | solution.py:33
  272.4 5.6 fusion.4
  281.0 15.2 %attention_forward.3 = (f32[448,512]{1,0:T(8,128)}, f32[8,512]{1,0:T(8,128)}) custom-call(s32[2,16]{1,0:T(2,128)} %fusion.152.kind, s32[16]{0:T(128)} %copy-done.95, s32[2,2]{1,0:T(2,128)} %pad_add_fusion.1.qinfo, bf16[448,512]{1,0:T(8,128)(2,1)} %bitcast.327, bf16[16,128,256]{2,1,0:T(8,128)(2,1)} %bitcast.353), custom_call_target="tpu_custom_call" | custom-call | flops 7516192768 | bytes 1048576 | tf_op jit(solution)/shard_map/attention_forward/pallas_call | solution.py:112
  300.0 11.3 %collective-permute-start.31 = (bf16[256,896]{1,0:T(8,128)(2,1)S(1)}, bf16[256,896]{1,0:T(8,128)(2,1)S(1)}, u32[]{:S(2)}, u32[]{:S(2)}) collective-permute-start(bf16[256,896]{1,0:T(8,128)(2,1)S(1)} %slice.1089), channel_id=1, source_target_pairs={{0,16},{16,0},{1,17},{17,1},{2,18},{18,2},{3,19},{19,3},{4,20},{20... | collective-permute-start | bytes 1376264 | tf_op jit(solution)/shard_map/feed_forward_grad/ppermute | solution.py:37
  312.1 9.9 %collective-permute-done.31 = bf16[256,896]{1,0:T(8,128)(2,1)S(1)} collective-permute-done((bf16[256,896]{1,0:T(8,128)(2,1)S(1)}, bf16[256,896]{1,0:T(8,128)(2,1)S(1)}, u32[]{:S(2)}, u32[]{:S(2)}) %collective-permute-start.31) | collective-permute-done | bytes 458784 | tf_op jit(solution)/shard_map/feed_forward_grad/ppermute | solution.py:37
  324.6 2.9 fusion.208
  331.5 3.4 collective-permute-done.24
  341.1 12.0 %fusion.37 = f32[1024,2560]{1,0:T(8,128)} fusion(bf16[896,2560]{1,0:T(8,128)(2,1)} %all-gather.9.cloned.1.call-done, bf16[512,896]{1,0:T(8,128)(2,1)S(1)} %collective-permute-done.25, bf16[256,896]{1,0:T(8,128)(2,1)S(1)} %collective-permute-done.24, bf16[256,896]{1,0:T(8,128)(2,1)S(1)} %get-tuple-element.178), kind=kOutput, calls=%fused_computation.149 | convolution fusion | flops 4703125504 | bytes 16908288 | tf_op jit(solution)/shard_map/feed_forward/dot_general | solution.py:33
  353.1 9.3 %multiply_convert_fusion.1 = (bf16[1024,1280]{1,0:T(8,128)(2,1)}, bf16[1024,1280]{1,0:T(8,128)(2,1)}, bf16[1024,1280]{1,0:T(8,128)(2,1)S(1)}) fusion(f32[1024,2560]{1,0:T(8,128)} %fusion.37, bf16[1280,896]{1,0:T(8,128)(2,1)S(1)} %copy-done.100, bf16[512,896]{1,0:T(8,128)(2,1)S(1)} %collective-permute-done.42, bf16[256,896]{1,0:T(8,128)(2,1)} %collective-permute-done.41, ...), kind=kOutput, calls=%fused_computation.5 | convolution fusion | flops 2373976064 | bytes 22478848 | tf_op jit(solution)/shard_map/feed_forward_grad/dot_general | solution.py:33
  362.4 5.0 fusion.34
  367.4 5.8 add_convert_fusion.1
  373.3 9.5 %fusion.3 = f32[1024,896]{1,0:T(8,128)S(1)} fusion(bf16[896,2560]{1,0:T(8,128)(2,1)} %all-gather.9.cloned.1.call-done, bf16[1024,1280]{1,0:T(8,128)(2,1)} %get-tuple-element.65, bf16[1024,1280]{1,0:T(8,128)(2,1)} %get-tuple-element.64), kind=kOutput, calls=%fused_computation.16 | convolution fusion | flops 4708106240 | bytes 13500416 | tf_op jit(solution)/shard_map/feed_forward_grad/dot_general | solution.py:33
  383.2 2.9 fusion.209
  387.3 6.8 fusion.2
  399.4 9.5 %add_convert_fusion = bf16[896,2560]{1,0:T(8,128)(2,1)} fusion(f32[896,2560]{1,0:T(8,128)S(1)} %fusion.2, bf16[1024,1280]{1,0:T(8,128)(2,1)} %copy-done.108, bf16[1024,1280]{1,0:T(8,128)(2,1)S(1)} %copy-done.107, bf16[512,896]{1,0:T(8,128)(2,1)} %collective-permute-done.11, bf16[256,896]{1,0:T(8,128)(2,1)S(1)} %copy-done.67, ...), kind=kOutput, calls=%fused_computation.1 | convolution fusion | flops 4718198784 | bytes 20840448 | tf_op jit(solution)/shard_map/feed_forward_weight_grads/dot_general | solution.py:33
  410.7 7.3 collective-permute-done.27
  418.0 3.5 multiply_subtract_fusion.1
  433.9 50.3 %attention_backward.2 = (f32[448,512]{1,0:T(8,128)}, f32[16,128,256]{2,1,0:T(8,128)}) custom-call(s32[2,16]{1,0:T(2,128)} %fusion.150.kind, s32[16]{0:T(128)} %copy-done.96, s32[2,2]{1,0:T(2,128)} %pad_add_fusion.qinfo, bf16[448,512]{1,0:T(8,128)(2,1)} %bitcast.330, bf16[16,128,256]{2,1,0:T(8,128)(2,1)} %bitcast.356, ...), custom_call_target="tpu_custom_call" | custom-call | flops 11274289152 | bytes 3145728 | tf_op jit(solution)/shard_map/attention_backward/pallas_call | solution.py:184
  492.7 18.0 %attention_backward.3 = (f32[448,512]{1,0:T(8,128)}, f32[16,128,256]{2,1,0:T(8,128)}) custom-call(s32[2,16]{1,0:T(2,128)} %fusion.152.kind, s32[16]{0:T(128)} %copy-done.95, s32[2,2]{1,0:T(2,128)} %pad_add_fusion.1.qinfo, bf16[448,512]{1,0:T(8,128)(2,1)} %bitcast.328, bf16[16,128,256]{2,1,0:T(8,128)(2,1)} %bitcast.354, ...), custom_call_target="tpu_custom_call" | custom-call | flops 11274289152 | bytes 3145728 | tf_op jit(solution)/shard_map/attention_backward/pallas_call | solution.py:184
  510.7 2.8 convert.151
  521.0 3.1 reshape.1081
  524.1 8.4 %constant_dynamic-slice_fusion.10 = (bf16[1,112,448]{1,0,2:T(2,128)(2,1)S(1)}, bf16[1,112,448]{1,0,2:T(2,128)(2,1)}, bf16[1,112,448]{1,0,2:T(2,128)(2,1)}, bf16[...) fusion(f32[8,112,448]{1,0,2:T(8,128)} %reshape.1081, ...), kind=kLoop, calls=%fused_computation.410 | loop fusion | bytes 1404956 | tf_op jit(solution)/shard_map/project_grad/jit(dynamic_index_in_dim)/dynamic_slice | solution.py:272
  534.2 37.4 %collective-permute-start.69 = (bf16[112,448]{1,0:T(8,128)(2,1)}, bf16[112,448]{1,0:T(8,128)(2,1)S(1)}, u32[]{:S(2)}, u32[]{:S(2)}) collective-permute-start(bf16[112,448]{1,0:T(8,128)(2,1)} %bitcast.333), channel_id=1, source_target_pairs={{0,2},{2,4},{4,6},{6,8},{8,10},{10,12},{12,14},{14,0},{1,3},{3,5},... | collective-permute-start | bytes 301064 | tf_op jit(solution)/shard_map/project_grad/ppermute | solution.py:264
  573.3 11.6 %collective-permute-start.68 = (bf16[112,448]{1,0:T(8,128)(2,1)}, bf16[112,448]{1,0:T(8,128)(2,1)}, u32[]{:S(2)}, u32[]{:S(2)}) collective-permute-start(bf16[112,448]{1,0:T(8,128)(2,1)} %bitcast.332), channel_id=1, source_target_pairs={{0,4},{2,6},{4,8},{6,10},{8,12},{10,14},{12,0},{14,2},{1,5},{3,7},... | collective-permute-start | bytes 301064 | tf_op jit(solution)/shard_map/project_grad/ppermute | solution.py:264
  591.4 34.8 %collective-permute-start.67 = (bf16[112,448]{1,0:T(8,128)(2,1)}, bf16[112,448]{1,0:T(8,128)(2,1)}, u32[]{:S(2)}, u32[]{:S(2)}) collective-permute-start(bf16[112,448]{1,0:T(8,128)(2,1)} %bitcast.337), channel_id=1, source_target_pairs={{0,6},{2,8},{4,10},{6,12},{8,14},{10,0},{12,2},{14,4},{1,7},{3,9},... | collective-permute-start | bytes 301064 | tf_op jit(solution)/shard_map/project_grad/ppermute | solution.py:264
  629.6 3.8 collective-permute-start.65
  635.9 2.9 collective-permute-start.64
  644.0 3.3 collective-permute-start.36
  653.1 6.3 collective-permute-done.37
  659.9 5.3 collective-permute-start.51
  665.2 2.9 collective-permute-start.50
  668.1 4.1 collective-permute-start.49
  675.8 6.0 collective-permute-start.47
  682.9 3.1 collective-permute-done.48
  697.5 4.5 collective-permute-done.71
  708.2 3.5 collective-permute-start.59
  714.6 3.2 collective-permute-start.56
  725.6 2.8 collective-permute-start.78
  730.7 3.4 collective-permute-done.62
  736.2 3.0 collective-permute-done.73
  763.1 6.1 collective-permute-done.84
  771.4 3.2 reshape.1086
  777.0 3.2 reshape.1087
  (655 shorter events, 206.1 us)
Async XLA Ops:
  7.2 52.4 %all-gather.5.cloned.1.call-start = ((), (), s32[]{:S(2)}) async-start(), calls=%async_computation.2 | async-start | bytes 1474560 | tf_op jit(solution)/shard_map/weights_qkv/all_gather | solution.py:300
  15.0 141.2 %all-gather.7.cloned.1.call-start = ((), (), s32[]{:S(2)}) async-start(), calls=%async_computation.3 | async-start | bytes 1705984 | tf_op jit(solution)/shard_map/weights_mlp/all_gather | solution.py:335
  15.7 195.0 %all-gather.9.cloned.1.call-start = ((), (), s32[]{:S(2)}) async-start(), calls=%async_computation.4 | async-start | bytes 5160960 | tf_op jit(solution)/shard_map/weights_mlp/all_gather | solution.py:332
  29.2 233.4 %all-gather.11.cloned.1.call-start = ((), (), s32[]{:S(2)}) async-start(), calls=%async_computation.5 | async-start | bytes 2580480 | tf_op jit(solution)/shard_map/weights_mlp/all_gather | solution.py:336
  29.3 11.1 %collective-permute-start.1 = (bf16[256,896]{1,0:T(8,128)(2,1)S(1)}, bf16[256,896]{1,0:T(8,128)(2,1)S(1)}, u32[]{:S(2)}, u32[]{:S(2)}) collective-permute-start(bf16[256,896]{1,0:T(8,128)(2,1)S(1)} %get-tuple-element.112), channel_id=1, source_target_pairs={{0,1},{1,0},{2,3},{3,2},{4,5},{5,4},{6,7},{7,6},{8,9},{9,8},{10,11... | collective-permute-start | bytes 1376264 | tf_op jit(solution)/shard_map/project/ppermute | solution.py:37
  29.8 11.0 %collective-permute-start.15 = (bf16[256,896]{1,0:T(8,128)(2,1)S(1)}, bf16[256,896]{1,0:T(8,128)(2,1)}, u32[]{:S(2)}, u32[]{:S(2)}) collective-permute-start(bf16[256,896]{1,0:T(8,128)(2,1)S(1)} %get-tuple-element.113), channel_id=1, source_target_pairs={{0,1},{1,0},{2,3},{3,2},{4,5},{5,4},{6,7},{7,6},{8,9},{9,8},{10,11... | collective-permute-start | bytes 1376264 | tf_op jit(solution)/shard_map/project/ppermute | solution.py:37
  30.9 14.5 %collective-permute-start.28 = (bf16[256,896]{1,0:T(8,128)(2,1)}, bf16[256,896]{1,0:T(8,128)(2,1)}, u32[]{:S(2)}, u32[]{:S(2)}) collective-permute-start(bf16[256,896]{1,0:T(8,128)(2,1)} %get-tuple-element.110), channel_id=1, source_target_pairs={{0,16},{16,0},{1,17},{17,1},{2,18},{18,2},{3,19},{19,3},{4,20},{20... | collective-permute-start | bytes 1376264 | tf_op jit(solution)/shard_map/gather_cotangent/ppermute | solution.py:37
  33.8 296.0 %collective-permute-start.41 = (bf16[256,896]{1,0:T(8,128)(2,1)}, bf16[256,896]{1,0:T(8,128)(2,1)}, u32[]{:S(2)}, u32[]{:S(2)}) collective-permute-start(bf16[256,896]{1,0:T(8,128)(2,1)} %get-tuple-element.111), channel_id=1, source_target_pairs={{0,16},{16,0},{1,17},{17,1},{2,18},{18,2},{3,19},{19,3},{4,20},{20... | collective-permute-start | bytes 1376264 | tf_op jit(solution)/shard_map/gather_cotangent/ppermute | solution.py:37
  34.6 714.4 %reduce-scatter.5.cloned.1.call-start = ((), (), s32[]{:S(2)}) async-start(), calls=%async_computation.7 | async-start | bytes 2580480 | tf_op jit(solution)/shard_map/feed_forward_weight_grads/reduce_scatter | solution.py:432
  46.7 174.3 %collective-permute-start.29 = (bf16[512,896]{1,0:T(8,128)(2,1)S(1)}, bf16[512,896]{1,0:T(8,128)(2,1)}, u32[]{:S(2)}, u32[]{:S(2)}) collective-permute-start(bf16[512,896]{1,0:T(8,128)(2,1)S(1)} %pad_maximum_fusion.19), channel_id=1, source_target_pairs={{0,1},{1,0},{2,3},{3,2},{4,5},{5,4},{6,7},{7,6},{8,9},{9,8},{10,11... | collective-permute-start | bytes 2752520 | tf_op jit(solution)/shard_map/gather_cotangent/ppermute | solution.py:37
  67.2 11.3 %collective-permute-start.2 = (bf16[2,128,256]{2,1,0:T(8,128)(2,1)S(1)}, bf16[2,128,256]{2,1,0:T(8,128)(2,1)S(1)}, u32[]{:S(2)}, u32[]{:S(2)}) collective-permute-start(bf16[2,128,256]{2,1,0:T(8,128)(2,1)S(1)} %pad_maximum_fusion.34), channel_id=1, source_target_pairs={{0,2},{2,4},{4,6},{6,8},{8,10},{10,12},{12,14},{14,0},{1,3},{3,5},... | collective-permute-start | bytes 393224 | tf_op jit(solution)/shard_map/gather_keys/ppermute | solution.py:254
  67.8 11.3 %collective-permute-start.3 = (bf16[2,128,256]{2,1,0:T(8,128)(2,1)S(1)}, bf16[2,128,256]{2,1,0:T(8,128)(2,1)S(1)}, u32[]{:S(2)}, u32[]{:S(2)}) collective-permute-start(bf16[2,128,256]{2,1,0:T(8,128)(2,1)S(1)} %pad_maximum_fusion.34), channel_id=1, source_target_pairs={{0,4},{2,6},{4,8},{6,10},{8,12},{10,14},{12,0},{14,2},{1,5},{3,7},... | collective-permute-start | bytes 393224 | tf_op jit(solution)/shard_map/gather_keys/ppermute | solution.py:254
  69.1 24.8 %collective-permute-start.4 = (bf16[2,128,256]{2,1,0:T(8,128)(2,1)S(1)}, bf16[2,128,256]{2,1,0:T(8,128)(2,1)S(1)}, u32[]{:S(2)}, u32[]{:S(2)}) collective-permute-start(bf16[2,128,256]{2,1,0:T(8,128)(2,1)S(1)} %pad_maximum_fusion.34), channel_id=1, source_target_pairs={{0,6},{2,8},{4,10},{6,12},{8,14},{10,0},{12,2},{14,4},{1,7},{3,9},... | collective-permute-start | bytes 393224 | tf_op jit(solution)/shard_map/gather_keys/ppermute | solution.py:254
  78.5 18.7 %collective-permute-start.5 = (bf16[2,128,256]{2,1,0:T(8,128)(2,1)S(1)}, bf16[2,128,256]{2,1,0:T(8,128)(2,1)S(1)}, u32[]{:S(2)}, u32[]{:S(2)}) collective-permute-start(bf16[2,128,256]{2,1,0:T(8,128)(2,1)S(1)} %pad_maximum_fusion.34), channel_id=1, source_target_pairs={{0,8},{2,10},{4,12},{6,14},{8,0},{10,2},{12,4},{14,6},{1,9},{3,11}... | collective-permute-start | bytes 393224 | tf_op jit(solution)/shard_map/gather_keys/ppermute | solution.py:254
  79.2 19.4 %collective-permute-start.6 = (bf16[2,128,256]{2,1,0:T(8,128)(2,1)S(1)}, bf16[2,128,256]{2,1,0:T(8,128)(2,1)S(1)}, u32[]{:S(2)}, u32[]{:S(2)}) collective-permute-start(bf16[2,128,256]{2,1,0:T(8,128)(2,1)S(1)} %pad_maximum_fusion.34), channel_id=1, source_target_pairs={{0,10},{2,12},{4,14},{6,0},{8,2},{10,4},{12,6},{14,8},{1,11},{3,13... | collective-permute-start | bytes 393224 | tf_op jit(solution)/shard_map/gather_keys/ppermute | solution.py:254
  97.2 11.1 %collective-permute-start.8 = (bf16[2,128,256]{2,1,0:T(8,128)(2,1)S(1)}, bf16[2,128,256]{2,1,0:T(8,128)(2,1)S(1)}, u32[]{:S(2)}, u32[]{:S(2)}) collective-permute-start(bf16[2,128,256]{2,1,0:T(8,128)(2,1)S(1)} %pad_maximum_fusion.34), channel_id=1, source_target_pairs={{0,14},{2,0},{4,2},{6,4},{8,6},{10,8},{12,10},{14,12},{1,15},{3,1}... | collective-permute-start | bytes 393224 | tf_op jit(solution)/shard_map/gather_keys/ppermute | solution.py:254
  98.6 56.0 %collective-permute-start.16 = (bf16[2,128,256]{2,1,0:T(8,128)(2,1)S(1)}, bf16[2,128,256]{2,1,0:T(8,128)(2,1)S(1)}, u32[]{:S(2)}, u32[]{:S(2)}) collective-permute-start(bf16[2,128,256]{2,1,0:T(8,128)(2,1)S(1)} %pad_maximum_fusion.35), channel_id=1, source_target_pairs={{0,2},{2,4},{4,6},{6,8},{8,10},{10,12},{12,14},{14,0},{1,3},{3,5},... | collective-permute-start | bytes 393224 | tf_op jit(solution)/shard_map/gather_keys/ppermute | solution.py:254
  103.1 55.6 %collective-permute-start.17 = (bf16[2,128,256]{2,1,0:T(8,128)(2,1)S(1)}, bf16[2,128,256]{2,1,0:T(8,128)(2,1)S(1)}, u32[]{:S(2)}, u32[]{:S(2)}) collective-permute-start(bf16[2,128,256]{2,1,0:T(8,128)(2,1)S(1)} %pad_maximum_fusion.35), channel_id=1, source_target_pairs={{0,4},{2,6},{4,8},{6,10},{8,12},{10,14},{12,0},{14,2},{1,5},{3,7},... | collective-permute-start | bytes 393224 | tf_op jit(solution)/shard_map/gather_keys/ppermute | solution.py:254
  108.3 54.1 %collective-permute-start.18 = (bf16[2,128,256]{2,1,0:T(8,128)(2,1)S(1)}, bf16[2,128,256]{2,1,0:T(8,128)(2,1)}, u32[]{:S(2)}, u32[]{:S(2)}) collective-permute-start(bf16[2,128,256]{2,1,0:T(8,128)(2,1)S(1)} %pad_maximum_fusion.35), channel_id=1, source_target_pairs={{0,6},{2,8},{4,10},{6,12},{8,14},{10,0},{12,2},{14,4},{1,7},{3,9},... | collective-permute-start | bytes 393224 | tf_op jit(solution)/shard_map/gather_keys/ppermute | solution.py:254
  156.2 30.7 %collective-permute-start.19 = (bf16[2,128,256]{2,1,0:T(8,128)(2,1)S(1)}, bf16[2,128,256]{2,1,0:T(8,128)(2,1)}, u32[]{:S(2)}, u32[]{:S(2)}) collective-permute-start(bf16[2,128,256]{2,1,0:T(8,128)(2,1)S(1)} %pad_maximum_fusion.35), channel_id=1, source_target_pairs={{0,8},{2,10},{4,12},{6,14},{8,0},{10,2},{12,4},{14,6},{1,9},{3,11}... | collective-permute-start | bytes 393224 | tf_op jit(solution)/shard_map/gather_keys/ppermute | solution.py:254
  158.7 13.6 %collective-permute-start.10 = (bf16[256,896]{1,0:T(8,128)(2,1)S(1)}, bf16[256,896]{1,0:T(8,128)(2,1)S(1)}, u32[]{:S(2)}, u32[]{:S(2)}) collective-permute-start(bf16[256,896]{1,0:T(8,128)(2,1)S(1)} %multiply_convert_fusion.7), channel_id=1, source_target_pairs={{0,16},{16,0},{1,17},{17,1},{2,18},{18,2},{3,19},{19,3},{4,20},{20... | collective-permute-start | bytes 1376264 | tf_op jit(solution)/shard_map/attention_out/ppermute | solution.py:37
  162.4 26.1 %collective-permute-start.20 = (bf16[2,128,256]{2,1,0:T(8,128)(2,1)S(1)}, bf16[2,128,256]{2,1,0:T(8,128)(2,1)S(1)}, u32[]{:S(2)}, u32[]{:S(2)}) collective-permute-start(bf16[2,128,256]{2,1,0:T(8,128)(2,1)S(1)} %pad_maximum_fusion.35), channel_id=1, source_target_pairs={{0,10},{2,12},{4,14},{6,0},{8,2},{10,4},{12,6},{14,8},{1,11},{3,13... | collective-permute-start | bytes 393224 | tf_op jit(solution)/shard_map/gather_keys/ppermute | solution.py:254
  172.3 26.8 %collective-permute-start.21 = (bf16[2,128,256]{2,1,0:T(8,128)(2,1)S(1)}, bf16[2,128,256]{2,1,0:T(8,128)(2,1)S(1)}, u32[]{:S(2)}, u32[]{:S(2)}) collective-permute-start(bf16[2,128,256]{2,1,0:T(8,128)(2,1)S(1)} %pad_maximum_fusion.35), channel_id=1, source_target_pairs={{0,12},{2,14},{4,0},{6,2},{8,4},{10,6},{12,8},{14,10},{1,13},{3,15... | collective-permute-start | bytes 393224 | tf_op jit(solution)/shard_map/gather_keys/ppermute | solution.py:254
  186.9 17.5 %collective-permute-start.11 = (bf16[512,896]{1,0:T(8,128)(2,1)S(1)}, bf16[512,896]{1,0:T(8,128)(2,1)}, u32[]{:S(2)}, u32[]{:S(2)}) collective-permute-start(bf16[512,896]{1,0:T(8,128)(2,1)S(1)} %pad_maximum_fusion.15), channel_id=1, source_target_pairs={{0,1},{1,0},{2,3},{3,2},{4,5},{5,4},{6,7},{7,6},{8,9},{9,8},{10,11... | collective-permute-start | bytes 2752520 | tf_op jit(solution)/shard_map/attention_out/ppermute | solution.py:37
  188.5 15.2 %collective-permute-start.22 = (bf16[2,128,256]{2,1,0:T(8,128)(2,1)S(1)}, bf16[2,128,256]{2,1,0:T(8,128)(2,1)S(1)}, u32[]{:S(2)}, u32[]{:S(2)}) collective-permute-start(bf16[2,128,256]{2,1,0:T(8,128)(2,1)S(1)} %pad_maximum_fusion.35), channel_id=1, source_target_pairs={{0,14},{2,0},{4,2},{6,4},{8,6},{10,8},{12,10},{14,12},{1,15},{3,1}... | collective-permute-start | bytes 393224 | tf_op jit(solution)/shard_map/gather_keys/ppermute | solution.py:254
  281.0 17.0 %collective-permute-start.30 = (bf16[512,896]{1,0:T(8,128)(2,1)}, bf16[512,896]{1,0:T(8,128)(2,1)}, u32[]{:S(2)}, u32[]{:S(2)}) collective-permute-start(bf16[512,896]{1,0:T(8,128)(2,1)} %slice.1083), channel_id=1, source_target_pairs={{0,1},{1,0},{2,3},{3,2},{4,5},{5,4},{6,7},{7,6},{8,9},{9,8},{10,11... | collective-permute-start | bytes 2752520 | tf_op jit(solution)/shard_map/feed_forward_grad/ppermute | solution.py:37
  297.4 13.8 %collective-permute-start.23 = (bf16[448,256]{1,0:T(8,128)(2,1)S(1)}, bf16[448,256]{1,0:T(8,128)(2,1)S(1)}, u32[]{:S(2)}, u32[]{:S(2)}) collective-permute-start(bf16[448,256]{1,0:T(8,128)(2,1)S(1)} %get-tuple-element.137), channel_id=1, source_target_pairs={{0,1},{1,0},{2,3},{3,2},{4,5},{5,4},{6,7},{7,6},{8,9},{9,8},{10,11... | collective-permute-start | bytes 688136 | tf_op jit(solution)/shard_map/attention_out/ppermute | solution.py:37
  300.0 22.1 %collective-permute-start.31 = (bf16[256,896]{1,0:T(8,128)(2,1)S(1)}, bf16[256,896]{1,0:T(8,128)(2,1)S(1)}, u32[]{:S(2)}, u32[]{:S(2)}) collective-permute-start(bf16[256,896]{1,0:T(8,128)(2,1)S(1)} %slice.1089), channel_id=1, source_target_pairs={{0,16},{16,0},{1,17},{17,1},{2,18},{18,2},{3,19},{19,3},{4,20},{20... | collective-permute-start | bytes 1376264 | tf_op jit(solution)/shard_map/feed_forward_grad/ppermute | solution.py:37
  322.9 12.0 %collective-permute-start.24 = (bf16[256,896]{1,0:T(8,128)(2,1)S(1)}, bf16[256,896]{1,0:T(8,128)(2,1)S(1)}, u32[]{:S(2)}, u32[]{:S(2)}) collective-permute-start(bf16[256,896]{1,0:T(8,128)(2,1)S(1)} %get-tuple-element.178), channel_id=1, source_target_pairs={{0,16},{16,0},{1,17},{17,1},{2,18},{18,2},{3,19},{19,3},{4,20},{20... | collective-permute-start | bytes 1376264 | tf_op jit(solution)/shard_map/attention_out/ppermute | solution.py:37
  331.2 22.0 %collective-permute-start.42 = (bf16[512,896]{1,0:T(8,128)(2,1)S(1)}, bf16[512,896]{1,0:T(8,128)(2,1)S(1)}, u32[]{:S(2)}, u32[]{:S(2)}) collective-permute-start(bf16[512,896]{1,0:T(8,128)(2,1)S(1)} %pad_maximum_fusion.20), channel_id=1, source_target_pairs={{0,1},{1,0},{2,3},{3,2},{4,5},{5,4},{6,7},{7,6},{8,9},{9,8},{10,11... | collective-permute-start | bytes 2752520 | tf_op jit(solution)/shard_map/gather_cotangent/ppermute | solution.py:37
  339.7 71.0 %collective-permute-start.14 = (bf16[256,896]{1,0:T(8,128)(2,1)}, bf16[256,896]{1,0:T(8,128)(2,1)}, u32[]{:S(2)}, u32[]{:S(2)}) collective-permute-start(bf16[256,896]{1,0:T(8,128)(2,1)} %slice.1091), channel_id=1, source_target_pairs={{0,16},{16,0},{1,17},{17,1},{2,18},{18,2},{3,19},{19,3},{4,20},{20... | collective-permute-start | bytes 1376264 | tf_op jit(solution)/shard_map/feed_forward/ppermute | solution.py:37
  373.2 378.6 %reduce-scatter.3.cloned.1.call-start = ((), (), s32[]{:S(2)}) async-start(), calls=%async_computation.6 | async-start | bytes 5160960 | tf_op jit(solution)/shard_map/feed_forward_weight_grads/reduce_scatter | solution.py:436
  383.0 11.1 %collective-permute-start.43 = (bf16[512,896]{1,0:T(8,128)(2,1)S(1)}, bf16[512,896]{1,0:T(8,128)(2,1)S(1)}, u32[]{:S(2)}, u32[]{:S(2)}) collective-permute-start(bf16[512,896]{1,0:T(8,128)(2,1)S(1)} %slice.1082), channel_id=1, source_target_pairs={{0,1},{1,0},{2,3},{3,2},{4,5},{5,4},{6,7},{7,6},{8,9},{9,8},{10,11... | collective-permute-start | bytes 2752520 | tf_op jit(solution)/shard_map/feed_forward_grad/ppermute | solution.py:37
  395.1 13.8 %collective-permute-start.44 = (bf16[256,896]{1,0:T(8,128)(2,1)}, bf16[256,896]{1,0:T(8,128)(2,1)}, u32[]{:S(2)}, u32[]{:S(2)}) collective-permute-start(bf16[256,896]{1,0:T(8,128)(2,1)} %slice.1087), channel_id=1, source_target_pairs={{0,16},{16,0},{1,17},{17,1},{2,18},{18,2},{3,19},{19,3},{4,20},{20... | collective-permute-start | bytes 1376264 | tf_op jit(solution)/shard_map/feed_forward_grad/ppermute | solution.py:37
  398.0 20.0 %collective-permute-start.27 = (bf16[256,896]{1,0:T(8,128)(2,1)}, bf16[256,896]{1,0:T(8,128)(2,1)}, u32[]{:S(2)}, u32[]{:S(2)}) collective-permute-start(bf16[256,896]{1,0:T(8,128)(2,1)} %slice.1090), channel_id=1, source_target_pairs={{0,16},{16,0},{1,17},{17,1},{2,18},{18,2},{3,19},{19,3},{4,20},{20... | collective-permute-start | bytes 1376264 | tf_op jit(solution)/shard_map/feed_forward/ppermute | solution.py:37
  423.8 63.2 %collective-permute-start.45 = (bf16[448,256]{1,0:T(8,128)(2,1)}, bf16[448,256]{1,0:T(8,128)(2,1)}, u32[]{:S(2)}, u32[]{:S(2)}) collective-permute-start(bf16[448,256]{1,0:T(8,128)(2,1)} %get-tuple-element.131), channel_id=1, source_target_pairs={{0,1},{1,0},{2,3},{3,2},{4,5},{5,4},{6,7},{7,6},{8,9},{9,8},{10,11... | collective-permute-start | bytes 688136 | tf_op jit(solution)/shard_map/attention_out_grad/ppermute | solution.py:37
  534.2 101.8 %collective-permute-start.69 = (bf16[112,448]{1,0:T(8,128)(2,1)}, bf16[112,448]{1,0:T(8,128)(2,1)S(1)}, u32[]{:S(2)}, u32[]{:S(2)}) collective-permute-start(bf16[112,448]{1,0:T(8,128)(2,1)} %bitcast.333), channel_id=1, source_target_pairs={{0,2},{2,4},{4,6},{6,8},{8,10},{10,12},{12,14},{14,0},{1,3},{3,5},... | collective-permute-start | bytes 301064 | tf_op jit(solution)/shard_map/project_grad/ppermute | solution.py:264
  573.3 65.6 %collective-permute-start.68 = (bf16[112,448]{1,0:T(8,128)(2,1)}, bf16[112,448]{1,0:T(8,128)(2,1)}, u32[]{:S(2)}, u32[]{:S(2)}) collective-permute-start(bf16[112,448]{1,0:T(8,128)(2,1)} %bitcast.332), channel_id=1, source_target_pairs={{0,4},{2,6},{4,8},{6,10},{8,12},{10,14},{12,0},{14,2},{1,5},{3,7},... | collective-permute-start | bytes 301064 | tf_op jit(solution)/shard_map/project_grad/ppermute | solution.py:264
  591.4 49.9 %collective-permute-start.67 = (bf16[112,448]{1,0:T(8,128)(2,1)}, bf16[112,448]{1,0:T(8,128)(2,1)}, u32[]{:S(2)}, u32[]{:S(2)}) collective-permute-start(bf16[112,448]{1,0:T(8,128)(2,1)} %bitcast.337), channel_id=1, source_target_pairs={{0,6},{2,8},{4,10},{6,12},{8,14},{10,0},{12,2},{14,4},{1,7},{3,9},... | collective-permute-start | bytes 301064 | tf_op jit(solution)/shard_map/project_grad/ppermute | solution.py:264
  627.9 15.4 %collective-permute-start.66 = (bf16[112,448]{1,0:T(8,128)(2,1)}, bf16[112,448]{1,0:T(8,128)(2,1)}, u32[]{:S(2)}, u32[]{:S(2)}) collective-permute-start(bf16[112,448]{1,0:T(8,128)(2,1)} %bitcast.336), channel_id=1, source_target_pairs={{0,8},{2,10},{4,12},{6,14},{8,0},{10,2},{12,4},{14,6},{1,9},{3,11}... | collective-permute-start | bytes 301064 | tf_op jit(solution)/shard_map/project_grad/ppermute | solution.py:264
  629.6 13.7 %collective-permute-start.65 = (bf16[112,448]{1,0:T(8,128)(2,1)}, bf16[112,448]{1,0:T(8,128)(2,1)}, u32[]{:S(2)}, u32[]{:S(2)}) collective-permute-start(bf16[112,448]{1,0:T(8,128)(2,1)} %bitcast.335), channel_id=1, source_target_pairs={{0,10},{2,12},{4,14},{6,0},{8,2},{10,4},{12,6},{14,8},{1,11},{3,13... | collective-permute-start | bytes 301064 | tf_op jit(solution)/shard_map/project_grad/ppermute | solution.py:264
  643.4 16.1 %collective-permute-start.37 = (bf16[2,128,256]{2,1,0:T(8,128)(2,1)}, bf16[2,128,256]{2,1,0:T(8,128)(2,1)S(1)}, u32[]{:S(2)}, u32[]{:S(2)}) collective-permute-start(bf16[2,128,256]{2,1,0:T(8,128)(2,1)} %get-tuple-element.96), channel_id=1, source_target_pairs={{0,6},{2,8},{4,10},{6,12},{8,14},{10,0},{12,2},{14,4},{1,7},{3,9},... | collective-permute-start | bytes 393224 | tf_op jit(solution)/shard_map/return_keys/ppermute | solution.py:264
  644.0 16.0 %collective-permute-start.36 = (bf16[2,128,256]{2,1,0:T(8,128)(2,1)}, bf16[2,128,256]{2,1,0:T(8,128)(2,1)S(1)}, u32[]{:S(2)}, u32[]{:S(2)}) collective-permute-start(bf16[2,128,256]{2,1,0:T(8,128)(2,1)} %get-tuple-element.97), channel_id=1, source_target_pairs={{0,8},{2,10},{4,12},{6,14},{8,0},{10,2},{12,4},{14,6},{1,9},{3,11}... | collective-permute-start | bytes 393224 | tf_op jit(solution)/shard_map/return_keys/ppermute | solution.py:264
  647.3 17.9 %collective-permute-start.35 = (bf16[2,128,256]{2,1,0:T(8,128)(2,1)}, bf16[2,128,256]{2,1,0:T(8,128)(2,1)S(1)}, u32[]{:S(2)}, u32[]{:S(2)}) collective-permute-start(bf16[2,128,256]{2,1,0:T(8,128)(2,1)} %get-tuple-element.98), channel_id=1, source_target_pairs={{0,10},{2,12},{4,14},{6,0},{8,2},{10,4},{12,6},{14,8},{1,11},{3,13... | collective-permute-start | bytes 393224 | tf_op jit(solution)/shard_map/return_keys/ppermute | solution.py:264
  650.7 17.4 %collective-permute-start.34 = (bf16[2,128,256]{2,1,0:T(8,128)(2,1)}, bf16[2,128,256]{2,1,0:T(8,128)(2,1)S(1)}, u32[]{:S(2)}, u32[]{:S(2)}) collective-permute-start(bf16[2,128,256]{2,1,0:T(8,128)(2,1)} %get-tuple-element.99), channel_id=1, source_target_pairs={{0,12},{2,14},{4,0},{6,2},{8,4},{10,6},{12,8},{14,10},{1,13},{3,15... | collective-permute-start | bytes 393224 | tf_op jit(solution)/shard_map/return_keys/ppermute | solution.py:264
  652.5 19.6 %collective-permute-start.33 = (bf16[2,128,256]{2,1,0:T(8,128)(2,1)}, bf16[2,128,256]{2,1,0:T(8,128)(2,1)S(1)}, u32[]{:S(2)}, u32[]{:S(2)}) collective-permute-start(bf16[2,128,256]{2,1,0:T(8,128)(2,1)} %get-tuple-element.93), channel_id=1, source_target_pairs={{0,14},{2,0},{4,2},{6,4},{8,6},{10,8},{12,10},{14,12},{1,15},{3,1}... | collective-permute-start | bytes 393224 | tf_op jit(solution)/shard_map/return_keys/ppermute | solution.py:264
  659.4 16.4 %collective-permute-start.52 = (bf16[2,128,256]{2,1,0:T(8,128)(2,1)}, bf16[2,128,256]{2,1,0:T(8,128)(2,1)S(1)}, u32[]{:S(2)}, u32[]{:S(2)}) collective-permute-start(bf16[2,128,256]{2,1,0:T(8,128)(2,1)} %get-tuple-element.85), channel_id=1, source_target_pairs={{0,2},{2,4},{4,6},{6,8},{8,10},{10,12},{12,14},{14,0},{1,3},{3,5},... | collective-permute-start | bytes 393224 | tf_op jit(solution)/shard_map/return_keys/ppermute | solution.py:264
  659.9 21.9 %collective-permute-start.51 = (bf16[2,128,256]{2,1,0:T(8,128)(2,1)}, bf16[2,128,256]{2,1,0:T(8,128)(2,1)S(1)}, u32[]{:S(2)}, u32[]{:S(2)}) collective-permute-start(bf16[2,128,256]{2,1,0:T(8,128)(2,1)} %get-tuple-element.86), channel_id=1, source_target_pairs={{0,4},{2,6},{4,8},{6,10},{8,12},{10,14},{12,0},{14,2},{1,5},{3,7},... | collective-permute-start | bytes 393224 | tf_op jit(solution)/shard_map/return_keys/ppermute | solution.py:264
  665.2 17.1 %collective-permute-start.50 = (bf16[2,128,256]{2,1,0:T(8,128)(2,1)}, bf16[2,128,256]{2,1,0:T(8,128)(2,1)S(1)}, u32[]{:S(2)}, u32[]{:S(2)}) collective-permute-start(bf16[2,128,256]{2,1,0:T(8,128)(2,1)} %get-tuple-element.87), channel_id=1, source_target_pairs={{0,6},{2,8},{4,10},{6,12},{8,14},{10,0},{12,2},{14,4},{1,7},{3,9},... | collective-permute-start | bytes 393224 | tf_op jit(solution)/shard_map/return_keys/ppermute | solution.py:264
  668.1 14.3 %collective-permute-start.49 = (bf16[2,128,256]{2,1,0:T(8,128)(2,1)}, bf16[2,128,256]{2,1,0:T(8,128)(2,1)S(1)}, u32[]{:S(2)}, u32[]{:S(2)}) collective-permute-start(bf16[2,128,256]{2,1,0:T(8,128)(2,1)} %get-tuple-element.88), channel_id=1, source_target_pairs={{0,8},{2,10},{4,12},{6,14},{8,0},{10,2},{12,4},{14,6},{1,9},{3,11}... | collective-permute-start | bytes 393224 | tf_op jit(solution)/shard_map/return_keys/ppermute | solution.py:264
  672.2 13.8 %collective-permute-start.48 = (bf16[2,128,256]{2,1,0:T(8,128)(2,1)}, bf16[2,128,256]{2,1,0:T(8,128)(2,1)S(1)}, u32[]{:S(2)}, u32[]{:S(2)}) collective-permute-start(bf16[2,128,256]{2,1,0:T(8,128)(2,1)} %get-tuple-element.89), channel_id=1, source_target_pairs={{0,10},{2,12},{4,14},{6,0},{8,2},{10,4},{12,6},{14,8},{1,11},{3,13... | collective-permute-start | bytes 393224 | tf_op jit(solution)/shard_map/return_keys/ppermute | solution.py:264
  675.8 10.2 %collective-permute-start.47 = (bf16[2,128,256]{2,1,0:T(8,128)(2,1)S(1)}, bf16[2,128,256]{2,1,0:T(8,128)(2,1)S(1)}, u32[]{:S(2)}, u32[]{:S(2)}) collective-permute-start(bf16[2,128,256]{2,1,0:T(8,128)(2,1)S(1)} %copy-done.73), channel_id=1, source_target_pairs={{0,12},{2,14},{4,0},{6,2},{8,4},{10,6},{12,8},{14,10},{1,13},{3,15... | collective-permute-start | bytes 393224 | tf_op jit(solution)/shard_map/return_keys/ppermute | solution.py:264
  682.3 20.4 %collective-permute-start.74 = (bf16[8,56,896]{2,1,0:T(8,128)(2,1)S(1)}, bf16[8,56,896]{2,1,0:T(8,128)(2,1)S(1)}, u32[]{:S(2)}, u32[]{:S(2)}) collective-permute-start(bf16[8,56,896]{2,1,0:T(8,128)(2,1)S(1)} %copy-done.54), channel_id=1, source_target_pairs={{0,1},{1,0},{2,3},{3,2},{4,5},{5,4},{6,7},{7,6},{8,9},{9,8},{10,11... | collective-permute-start | bytes 2408456 | tf_op jit(solution)/shard_map/o_weight_grad/ppermute | solution.py:37
  682.4 14.8 %collective-permute-start.70 = (bf16[56,448]{1,0:T(8,128)(2,1)S(1)}, bf16[56,448]{1,0:T(8,128)(2,1)S(1)}, u32[]{:S(2)}, u32[]{:S(2)}) collective-permute-start(bf16[56,448]{1,0:T(8,128)(2,1)S(1)} %get-tuple-element.157), channel_id=1, source_target_pairs={{0,1},{1,0},{2,3},{3,2},{4,5},{5,4},{6,7},{7,6},{8,9},{9,8},{10,11... | collective-permute-start | bytes 150536 | tf_op jit(solution)/shard_map/owners/ppermute | solution.py:37
  691.0 12.8 %collective-permute-start.40 = (bf16[256,896]{1,0:T(8,128)(2,1)S(1)}, bf16[256,896]{1,0:T(8,128)(2,1)S(1)}, u32[]{:S(2)}, u32[]{:S(2)}) collective-permute-start(bf16[256,896]{1,0:T(8,128)(2,1)S(1)} %slice.1088), channel_id=1, source_target_pairs={{0,1},{1,0},{2,3},{3,2},{4,5},{5,4},{6,7},{7,6},{8,9},{9,8},{10,11... | collective-permute-start | bytes 1376264 | tf_op jit(solution)/shard_map/project_grad/ppermute | solution.py:37
  693.2 10.7 %collective-permute-start.53 = (bf16[256,896]{1,0:T(8,128)(2,1)S(1)}, bf16[256,896]{1,0:T(8,128)(2,1)S(1)}, u32[]{:S(2)}, u32[]{:S(2)}) collective-permute-start(bf16[256,896]{1,0:T(8,128)(2,1)S(1)} %slice.1086), channel_id=1, source_target_pairs={{0,1},{1,0},{2,3},{3,2},{4,5},{5,4},{6,7},{7,6},{8,9},{9,8},{10,11... | collective-permute-start | bytes 1376264 | tf_op jit(solution)/shard_map/project_grad/ppermute | solution.py:37
  706.4 11.5 %collective-permute-start.60 = (bf16[144,128]{1,0:T(8,128)(2,1)S(1)}, bf16[144,128]{1,0:T(8,128)(2,1)S(1)}, u32[]{:S(2)}, u32[]{:S(2)}) collective-permute-start(bf16[144,128]{1,0:T(8,128)(2,1)S(1)} %fusion.138), channel_id=1, source_target_pairs={{0,2},{2,4},{4,6},{6,8},{8,10},{10,12},{12,14},{14,0},{1,3},{3,5},... | collective-permute-start | bytes 110600 | tf_op jit(solution)/shard_map/shares/ppermute | solution.py:264
  708.2 11.1 %collective-permute-start.59 = (bf16[144,128]{1,0:T(8,128)(2,1)S(1)}, bf16[144,128]{1,0:T(8,128)(2,1)S(1)}, u32[]{:S(2)}, u32[]{:S(2)}) collective-permute-start(bf16[144,128]{1,0:T(8,128)(2,1)S(1)} %get-tuple-element.123), channel_id=1, source_target_pairs={{0,4},{2,6},{4,8},{6,10},{8,12},{10,14},{12,0},{14,2},{1,5},{3,7},... | collective-permute-start | bytes 110600 | tf_op jit(solution)/shard_map/shares/ppermute | solution.py:264
  713.1 10.4 %collective-permute-start.57 = (bf16[144,128]{1,0:T(8,128)(2,1)S(1)}, bf16[144,128]{1,0:T(8,128)(2,1)S(1)}, u32[]{:S(2)}, u32[]{:S(2)}) collective-permute-start(bf16[144,128]{1,0:T(8,128)(2,1)S(1)} %get-tuple-element.121), channel_id=1, source_target_pairs={{0,8},{2,10},{4,12},{6,14},{8,0},{10,2},{12,4},{14,6},{1,9},{3,11}... | collective-permute-start | bytes 110600 | tf_op jit(solution)/shard_map/shares/ppermute | solution.py:264
  722.9 17.9 %collective-permute-start.81 = (bf16[56,896]{1,0:T(8,128)(2,1)}, bf16[56,896]{1,0:T(8,128)(2,1)S(1)}, u32[]{:S(2)}, u32[]{:S(2)}) collective-permute-start(bf16[56,896]{1,0:T(8,128)(2,1)} %get-tuple-element.76), channel_id=1, source_target_pairs={{0,2},{2,4},{4,6},{6,8},{8,10},{10,12},{12,14},{14,0},{1,3},{3,5},... | collective-permute-start | bytes 301064 | tf_op jit(solution)/shard_map/o_weight_grad/ppermute | solution.py:264
  723.5 18.6 %collective-permute-start.80 = (bf16[56,896]{1,0:T(8,128)(2,1)}, bf16[56,896]{1,0:T(8,128)(2,1)S(1)}, u32[]{:S(2)}, u32[]{:S(2)}) collective-permute-start(bf16[56,896]{1,0:T(8,128)(2,1)} %get-tuple-element.77), channel_id=1, source_target_pairs={{0,4},{2,6},{4,8},{6,10},{8,12},{10,14},{12,0},{14,2},{1,5},{3,7},... | collective-permute-start | bytes 301064 | tf_op jit(solution)/shard_map/o_weight_grad/ppermute | solution.py:264
  724.1 21.2 %collective-permute-start.79 = (bf16[56,896]{1,0:T(8,128)(2,1)}, bf16[56,896]{1,0:T(8,128)(2,1)S(1)}, u32[]{:S(2)}, u32[]{:S(2)}) collective-permute-start(bf16[56,896]{1,0:T(8,128)(2,1)} %get-tuple-element.78), channel_id=1, source_target_pairs={{0,6},{2,8},{4,10},{6,12},{8,14},{10,0},{12,2},{14,4},{1,7},{3,9},... | collective-permute-start | bytes 301064 | tf_op jit(solution)/shard_map/o_weight_grad/ppermute | solution.py:264
  725.6 19.8 %collective-permute-start.78 = (bf16[56,896]{1,0:T(8,128)(2,1)}, bf16[56,896]{1,0:T(8,128)(2,1)S(1)}, u32[]{:S(2)}, u32[]{:S(2)}) collective-permute-start(bf16[56,896]{1,0:T(8,128)(2,1)} %get-tuple-element.79), channel_id=1, source_target_pairs={{0,8},{2,10},{4,12},{6,14},{8,0},{10,2},{12,4},{14,6},{1,9},{3,11}... | collective-permute-start | bytes 301064 | tf_op jit(solution)/shard_map/o_weight_grad/ppermute | solution.py:264
  761.2 13.6 %collective-permute-start.86 = (bf16[2,56,1280]{2,1,0:T(8,128)(2,1)S(1)}, bf16[2,56,1280]{2,1,0:T(8,128)(2,1)S(1)}, u32[]{:S(2)}, u32[]{:S(2)}) collective-permute-start(bf16[2,56,1280]{2,1,0:T(8,128)(2,1)S(1)} %maximum_select_fusion.7), channel_id=1, source_target_pairs={{0,16},{16,0},{1,17},{17,1},{2,18},{18,2},{3,19},{19,3},{4,20},{20... | collective-permute-start | bytes 860168 | tf_op jit(solution)/shard_map/owners/ppermute | solution.py:37
  (144 other events, 2072.8 us)
Sparse Core Ops, SparseCore 0:
  15.1 44.4 all-gather.4
  61.7 50.6 all-gather.6
  115.2 95.4 all-gather.8
  213.3 49.2 all-gather.10
  373.4 106.3 reduce-scatter.4
  483.2 92.8 reduce-scatter.2

commit v2 on v1

v2 whole, which is shorter than its diff:
```python
import functools

import jax
import jax.numpy as jnp
from jax import lax
from jax.experimental import pallas as pl
from jax.experimental.pallas import tpu as pltpu
from jax.sharding import Mesh
from jax.sharding import PartitionSpec as P

HEADS = 14
KV_HEADS = 2
HEAD_DIM = 64
GROUPS = HEADS // KV_HEADS
TMB = 256
MB = 2
SEQ_MAX = 4096
QW = GROUPS * HEAD_DIM
DIRECT_MAX = 8

norm_eps = 1e-06
rope_base = 1000000.0
masked_score = -1e30

bf16 = jnp.bfloat16
f32 = jnp.float32
NN = ((1,), (0,))
NT = ((1,), (1,))
TN = ((0,), (0,))


def mm(a, b, dims=NN):
    return lax.dot_general(a, b, (dims, ((), ())), preferred_element_type=f32)


def swap(a, axis):
    return lax.ppermute(a, axis, [(0, 1), (1, 0)])


class Layout:
    def __init__(self, m, chips, seq_length, rotated):
        self.m, self.chips, self.seq_length, self.rotated = m, chips, seq_length, rotated

    def start(self, starts, ids, chip, second):
        core = jnp.where(second, 1 - ids[2], ids[2])
        return starts[((ids[0] * self.chips + chip) * 2 + core) * MB + self.m]

    def query(self, starts, ids, prefix, b):
        at = self.start(starts, ids, ids[1], b == 1)
        seq = at // self.seq_length
        return seq, at - seq * self.seq_length, prefix[seq]

    def key(self, starts, ids, j):
        chip = j // 2
        if self.rotated:
            chip = ids[1] - chip
            chip = jnp.where(chip < 0, chip + self.chips, chip)
        at = self.start(starts, ids, chip, j % 2 == 1)
        seq = at // self.seq_length
        return seq, at - seq * self.seq_length


def each_block(layout, starts, ids, prefix, process):
    q_seq, q_pos, limit = layout.query(starts, ids, prefix, pl.program_id(0))

    def step(j, carry):
        k_seq, k_pos = layout.key(starts, ids, j)
        same = k_seq == q_seq
        full = same & ((k_pos + TMB - 1 <= q_pos) | (k_pos + TMB <= limit))
        some = same & ((k_pos <= q_pos + TMB - 1) | (k_pos < limit))

        @pl.when(full)
        def _():
            process(j, None)

        @pl.when(some & jnp.logical_not(full))
        def _():
            ks = k_pos + lax.broadcasted_iota(jnp.int32, (TMB, TMB), 0)
            qs = q_pos + lax.broadcasted_iota(jnp.int32, (TMB, TMB), 1)
            process(j, (ks <= qs) | (ks < limit))

        return carry

    lax.fori_loop(0, 2 * layout.chips, step, 0)


def forward_kernel(layout, starts, ids, prefix, q_ref, kv_ref, o_ref, lse_ref, m_s, l_s, acc):
    m_s[...] = jnp.full_like(m_s, masked_score)
    l_s[...] = jnp.zeros_like(l_s)
    acc[...] = jnp.zeros_like(acc)

    def process(j, ok):
        k_rows = kv_ref[j, :HEAD_DIM, :].T
        v_cols = kv_ref[j, HEAD_DIM:, :]
        for h in range(GROUPS):
            hs = slice(h * HEAD_DIM, (h + 1) * HEAD_DIM)
            s = mm(k_rows, q_ref[hs, :])
            if ok is not None:
                s = jnp.where(ok, s, masked_score)
            old_max = m_s[h : h + 1, :]
            new_max = jnp.maximum(old_max, jnp.max(s, axis=0, keepdims=True))
            p = jnp.exp(s - new_max)
            fade = jnp.exp(old_max - new_max)
            m_s[h : h + 1, :] = new_max
            l_s[h : h + 1, :] = l_s[h : h + 1, :] * fade + jnp.sum(p, axis=0, keepdims=True)
            acc[hs, :] = acc[hs, :] * fade + mm(v_cols, p.astype(bf16))

    each_block(layout, starts, ids, prefix, process)
    for h in range(GROUPS):
        hs = slice(h * HEAD_DIM, (h + 1) * HEAD_DIM)
        o_ref[hs, :] = acc[hs, :] / l_s[h : h + 1, :]
    lse_ref[...] = m_s[...] + jnp.log(l_s[...])


def attention_forward(layout, starts, ids, prefix, q_cols, kv):
    count = kv.shape[0]
    grid_spec = pltpu.PrefetchScalarGridSpec(
        num_scalar_prefetch=3,
        grid=(2,),
        in_specs=[
            pl.BlockSpec((QW, TMB), lambda b, *_: (0, b)),
            pl.BlockSpec((count, 2 * HEAD_DIM, TMB), lambda b, *_: (0, 0, 0)),
        ],
        out_specs=[
            pl.BlockSpec((QW, TMB), lambda b, *_: (0, b)),
            pl.BlockSpec((8, TMB), lambda b, *_: (0, b)),
        ],
        scratch_shapes=[
            pltpu.VMEM((8, TMB), f32),
            pltpu.VMEM((8, TMB), f32),
            pltpu.VMEM((QW, TMB), f32),
        ],
    )
    pairs = count * TMB * TMB * GROUPS
    return pl.pallas_call(
        functools.partial(forward_kernel, layout),
        grid_spec=grid_spec,
        out_shape=[
            jax.ShapeDtypeStruct((QW, 2 * TMB), f32),
            jax.ShapeDtypeStruct((8, 2 * TMB), f32),
        ],
        cost_estimate=pl.CostEstimate(
            flops=pairs * 16 * HEAD_DIM,
            transcendentals=pairs,
            bytes_accessed=count * TMB * 4 * HEAD_DIM,
        ),
        compiler_params=pltpu.CompilerParams(dimension_semantics=("arbitrary",)),
        name="attention_forward",
    )(starts, ids, prefix, q_cols, kv)


def backward_kernel(
    layout, starts, ids, prefix, q_ref, kv_ref, do_ref, lse_ref, delta_ref, dq_ref, dkv_ref, acc
):
    b = pl.program_id(0)

    @pl.when(b == 0)
    def _():
        acc[...] = jnp.zeros_like(acc)

    dq_ref[...] = jnp.zeros_like(dq_ref)

    def process(j, ok):
        k_cols = kv_ref[j, :HEAD_DIM, :]
        k_rows = k_cols.T
        v_rows = kv_ref[j, HEAD_DIM:, :].T
        dk = dv = None
        for h in range(GROUPS):
            hs = slice(h * HEAD_DIM, (h + 1) * HEAD_DIM)
            s = mm(k_rows, q_ref[hs, :])
            if ok is not None:
                s = jnp.where(ok, s, masked_score)
            p = jnp.exp(s - lse_ref[h : h + 1, :])
            dp = mm(v_rows, do_ref[hs, :])
            ds = (p * (dp - delta_ref[h : h + 1, :])).astype(bf16)
            dq_ref[hs, :] += mm(k_cols, ds)
            dk_part = mm(q_ref[hs, :], ds, NT)
            dv_part = mm(do_ref[hs, :], p.astype(bf16), NT)
            dk = dk_part if dk is None else dk + dk_part
            dv = dv_part if dv is None else dv + dv_part
        acc[j, :HEAD_DIM, :] += dk
        acc[j, HEAD_DIM:, :] += dv

    each_block(layout, starts, ids, prefix, process)

    @pl.when(b == 1)
    def _():
        dkv_ref[...] = acc[...].astype(bf16)


def attention_backward(layout, starts, ids, prefix, q_cols, kv, do_cols, lse, delta):
    count = kv.shape[0]
    grid_spec = pltpu.PrefetchScalarGridSpec(
        num_scalar_prefetch=3,
        grid=(2,),
        in_specs=[
            pl.BlockSpec((QW, TMB), lambda b, *_: (0, b)),
            pl.BlockSpec((count, 2 * HEAD_DIM, TMB), lambda b, *_: (0, 0, 0)),
            pl.BlockSpec((QW, TMB), lambda b, *_: (0, b)),
            pl.BlockSpec((8, TMB), lambda b, *_: (0, b)),
            pl.BlockSpec((8, TMB), lambda b, *_: (0, b)),
        ],
        out_specs=[
            pl.BlockSpec((QW, TMB), lambda b, *_: (0, b)),
            pl.BlockSpec((count, 2 * HEAD_DIM, TMB), lambda b, *_: (0, 0, 0)),
        ],
        scratch_shapes=[pltpu.VMEM((count, 2 * HEAD_DIM, TMB), f32)],
    )
    pairs = count * TMB * TMB * GROUPS
    return pl.pallas_call(
        functools.partial(backward_kernel, layout),
        grid_spec=grid_spec,
        out_shape=[
            jax.ShapeDtypeStruct((QW, 2 * TMB), f32),
            jax.ShapeDtypeStruct((count, 2 * HEAD_DIM, TMB), bf16),
        ],
        cost_estimate=pl.CostEstimate(
            flops=pairs * 24 * HEAD_DIM,
            transcendentals=pairs,
            bytes_accessed=count * TMB * 12 * HEAD_DIM,
        ),
        compiler_params=pltpu.CompilerParams(dimension_semantics=("arbitrary",)),
        name="attention_backward",
    )(starts, ids, prefix, q_cols, kv, do_cols, lse, delta)


def rotate(values, cosine, sine):
    half = HEAD_DIM // 2
    low, high = values[:, :half], values[:, half:]
    return jnp.concatenate([low * cosine - high * sine, high * cosine + low * sine], axis=1)


def unrotate(grads, cosine, sine):
    half = HEAD_DIM // 2
    low, high = grads[:, :half], grads[:, half:]
    return jnp.concatenate([low * cosine + high * sine, high * cosine - low * sine], axis=1)


def ordered(first, own, other, axis):
    return jnp.where(
        first, jnp.concatenate([own, other], axis), jnp.concatenate([other, own], axis)
    )


def on_device(
    tokens,
    cotangent,
    place,
    prefix,
    attn_norm,
    q_weight,
    q_bias,
    k_weight,
    k_bias,
    v_weight,
    v_bias,
    o_weight,
    mlp_norm,
    gate_weight,
    up_projection_weight,
    down_weight,
):
    chips = lax.axis_size("chip")
    chip = lax.axis_index("chip")
    core = lax.axis_index("core")
    rep = lax.axis_index("rep")
    lead_core = core == 0
    lead_rep = rep == 0
    direct = chips <= DIRECT_MAX
    width = q_weight.shape[1]
    rows = q_weight.shape[0]
    seq_length = min(SEQ_MAX, TMB * chips * 2)
    block_count = 2 * chips

    hop = [[(i, (i + k) % chips) for i in range(chips)] for k in range(chips)]
    back_hop = [[(i, (i - k) % chips) for i in range(chips)] for k in range(chips)]

    def gather_chips(a):
        if not direct:
            return lax.all_gather(a, "chip", axis=0, tiled=False)
        parts = [a] + [lax.ppermute(a, "chip", hop[k]) for k in range(1, chips)]
        return jnp.stack(parts, axis=0)

    def sum_from_chips(chunk_of):
        total = chunk_of(0).astype(f32)
        for k in range(1, chips):
            total = total + lax.ppermute(chunk_of(k), "chip", back_hop[k]).astype(f32)
        return total

    def scatter_chips(stacked):
        if not direct:
            return lax.psum_scatter(stacked, "chip", scatter_dimension=0, tiled=False).astype(f32)

        def chunk_of(k):
            return lax.dynamic_index_in_dim(stacked, (chip - k) % chips, 0, keepdims=False)

        return sum_from_chips(chunk_of)


    cols = QW + 2 * HEAD_DIM
    with jax.named_scope("weights_qkv"):
        vectors = (attn_norm, mlp_norm, q_bias, k_bias, v_bias)
        row_pad = -(rows + len(vectors)) % 16
        vectors = [jnp.pad(v, (0, cols - v.shape[0]))[None] for v in vectors]

        def head_columns(c):
            part = jnp.concatenate(
                [
                    q_weight[:, c * QW : (c + 1) * QW],
                    k_weight[:, c * HEAD_DIM : (c + 1) * HEAD_DIM],
                    v_weight[:, c * HEAD_DIM : (c + 1) * HEAD_DIM],
                ],
                axis=1,
            )
            return jnp.concatenate([part, *vectors, jnp.zeros((row_pad, cols), bf16)], axis=0)

        columns = (head_columns(0), head_columns(1))
        own_columns = jnp.where(lead_core, columns[0], columns[1])
        sent_columns = jnp.where(lead_core, columns[1], columns[0])
        chip_rows = ordered(lead_core, own_columns[None], swap(sent_columns, "core")[None], 0)
        qkv_all = lax.all_gather(chip_rows, "chip", axis=0, tiled=False)
        qkv_full = qkv_all[:, :, :rows].reshape(width, cols)
        vec_all = qkv_all[:, :, rows : rows + len(vectors)].astype(f32)
        vec_all = vec_all.reshape(2 * chips, len(vectors), cols)
        kv_rows = k_bias.shape[0]
        gain_one = vec_all[:, 0, :rows].reshape(1, width)
        gain_two = vec_all[:, 1, :rows].reshape(1, width)
        q_add = vec_all[:, 2, :rows].reshape(2, QW)
        k_add = vec_all[:, 3, :kv_rows].reshape(2, HEAD_DIM)
        v_add = vec_all[:, 4, :kv_rows].reshape(2, HEAD_DIM)
        biases = jnp.concatenate([q_add, k_add, v_add], axis=1)
        bias_col = jnp.where(lead_core, biases[0], biases[1])[:, None]

    with jax.named_scope("weights_mlp"):
        after = chip_rows[1, 0, 0] * 0
        gate_weight, up_projection_weight = gate_weight + after, up_projection_weight + after
        ff_rows = down_weight.shape[0]
        half_rows = ff_rows // 2
        half_pad = -(-half_rows // 16) * 16
        quarter = chips * half_pad

        down_half = jnp.where(lead_rep, down_weight[:half_rows], down_weight[half_rows:])
        o_pair = ordered(lead_core, o_weight, swap(o_weight, "core"), 0)
        o_pad = -(-2 * rows // 16) * 16
        down_o = jnp.concatenate(
            [
                jnp.pad(down_half, ((0, half_pad - half_rows), (0, 0))),
                jnp.pad(o_pair, ((0, o_pad - 2 * rows), (0, 0))),
            ],
            axis=0,
        )
        def quarter_columns(w, c):
            split = w.reshape(rows, chips, 2, 2, half_rows)[:, :, c]
            part = jnp.where(lead_rep, split[:, :, 0], split[:, :, 1])
            return jnp.pad(part, ((0, 0), (0, 0), (0, half_pad - half_rows))).reshape(rows, quarter)

        def quarter_pair(c):
            return jnp.concatenate(
                [quarter_columns(gate_weight, c), quarter_columns(up_projection_weight, c)], axis=1
            )

        pairs = (quarter_pair(0), quarter_pair(1))
        own_pair = jnp.where(lead_core, pairs[0], pairs[1])
        sent_pair = jnp.where(lead_core, pairs[1], pairs[0])
        pair_rows = ordered(lead_core, own_pair, swap(sent_pair, "core"), 0)

    with jax.named_scope("visibility"):
        starts = place.reshape(-1, TMB)[:, 0]
        ids = jnp.stack([rep, chip, core]).astype(jnp.int32)
        layouts = [Layout(m, chips, seq_length, direct and m == 0) for m in range(MB)]

    own_rows = MB * TMB

    def group_rows(a):
        both = jnp.concatenate([a, swap(a, "rep")], axis=0)
        return jnp.concatenate([both, swap(both, "core")], axis=0)

    def core_pair_sum(a):
        half = a.shape[0] // 2
        return a[:half] + swap(a[half:].astype(bf16), "core").astype(f32)

    def rep_pair_sum(a):
        half = a.shape[0] // 2
        return a[:half] + swap(a[half:].astype(bf16), "rep").astype(f32)

    def micro(a, m):
        return jnp.concatenate(
            [a[:, m * TMB : (m + 1) * TMB], a[:, own_rows + m * TMB : own_rows + (m + 1) * TMB]],
            axis=1,
        )

    def both_micros(parts):
        return jnp.concatenate([p[:, :TMB] for p in parts] + [p[:, TMB:] for p in parts], axis=1)

    with jax.named_scope("gather_cotangent"):
        cot_rep = swap(cotangent, "rep")
        cot_parts = (cotangent, cot_rep, swap(cotangent, "core"), swap(cot_rep, "core"))
        qkv_full, cot_parts = lax.optimization_barrier((qkv_full, cot_parts))
        cot_group = jnp.concatenate(cot_parts, axis=0)
    with jax.named_scope("project"):
        x = tokens.astype(f32)
        pair = jnp.concatenate([tokens, swap(tokens, "core")], axis=0).astype(f32)
        r_pair = lax.rsqrt(jnp.mean(pair * pair, axis=-1, keepdims=True) + norm_eps)
        normed = (pair * r_pair * gain_one).astype(bf16)
        qkv = mm(qkv_full, normed, ((0,), (1,))) + bias_col
        exponent = jnp.arange(HEAD_DIM // 2).astype(f32) * (2.0 / HEAD_DIM)
        frequency = (rope_base ** (-exponent))[:, None]
        pos = lax.dynamic_slice_in_dim(starts, (rep * chips + chip) * 2 * MB, 2 * MB) % seq_length
        pos = ordered(lead_core, pos[:MB], pos[MB:], 0)
        pos = (pos[:, None] + jnp.arange(TMB)[None]).reshape(1, 2 * own_rows)
        angles = frequency * pos.astype(f32)
        cosine, sine = jnp.cos(angles)[None], jnp.sin(angles)[None]
        k_rot = rotate(qkv[None, QW : QW + HEAD_DIM], cosine, sine)[0].astype(bf16)
        kv_own = jnp.concatenate([k_rot, qkv[QW + HEAD_DIM :].astype(bf16)], axis=0)
        q_rot = rotate(qkv[:QW].reshape(GROUPS, HEAD_DIM, 2 * own_rows), cosine, sine)
        q_all = (q_rot.astype(bf16) * HEAD_DIM**-0.5).astype(bf16).reshape(QW, 2 * own_rows)
        q_cols = [micro(q_all, m) for m in range(MB)]
    kv = []
    with jax.named_scope("gather_keys"):
        for m in range(MB):
            mine = micro(kv_own, m)
            mine = jnp.stack([mine[:, :TMB], mine[:, TMB:]], axis=0)
            every = gather_chips(mine) if m == 0 else lax.all_gather(mine, "chip", axis=0)
            kv.append(every.reshape(block_count, 2 * HEAD_DIM, TMB))
    with jax.named_scope("gather_mlp"):
        kv[0], down_o, pair_rows = lax.optimization_barrier((kv[0], down_o, pair_rows))
        down_o_all = lax.all_gather(down_o, "chip", axis=0, tiled=False)
        down = down_o_all[:, :half_pad].reshape(quarter, width)
        o_full = down_o_all[:, half_pad : half_pad + 2 * rows].reshape(width, width)

        gate_up = lax.all_gather(pair_rows, "chip", axis=0, tiled=True)

    heads, lse = [], []
    for m in range(MB):
        o_m, lse_m = attention_forward(layouts[m], starts, ids, prefix, q_cols[m], kv[m])
        heads.append(o_m)
        lse.append(lse_m)
    with jax.named_scope("attention_out"):
        att = both_micros([h.astype(bf16) for h in heads])
        att_cols = ordered(lead_core, att[:, :own_rows], swap(att[:, own_rows:], "core"), 0)
        middle = x + mm(att_cols, o_full, TN)
        r2 = lax.rsqrt(jnp.mean(middle * middle, axis=-1, keepdims=True) + norm_eps)
        normed_two = (middle * r2 * gain_two).astype(bf16)
        n2_group = group_rows(normed_two)
    with jax.named_scope("feed_forward"):
        gate_up_pre = mm(n2_group, gate_up)
        gate, up = gate_up_pre[:, :quarter], gate_up_pre[:, quarter:]
        sig = jax.nn.sigmoid(gate)
        silu = gate * sig
        hidden = (silu * up).astype(bf16)
    with jax.named_scope("feed_forward_grad"):
        dh = mm(cot_group, down, NT)
        dgate = (dh * up * (sig * (1.0 + gate * (1.0 - sig)))).astype(bf16)
        dup = (dh * silu).astype(bf16)
        dgu = jnp.concatenate([dgate, dup], axis=1)
        dn2 = rep_pair_sum(core_pair_sum(mm(dgu, gate_up, NT)))
    with jax.named_scope("feed_forward_out"):
        result_half = core_pair_sum(mm(hidden, down))

    with jax.named_scope("attention_out_grad"):
        gain_two_grad = jnp.sum(dn2 * (middle * r2), axis=0)
        e = dn2 * gain_two
        dmiddle = (
            cotangent.astype(f32)
            + r2 * e
            - middle * r2**3 * jnp.mean(e * middle, axis=-1, keepdims=True)
        )
        dbranch = dmiddle.astype(bf16)
        datt = mm(o_full, dbranch, NT).astype(bf16)
        own_datt = jnp.where(lead_core, datt[:QW], datt[QW:])
        sent_datt = jnp.where(lead_core, datt[QW:], datt[:QW])
        datt_all = jnp.concatenate([own_datt, swap(sent_datt, "core")], axis=1)
    with jax.named_scope("o_weight_grad"):
        o_parts = mm(att_cols, dbranch).reshape(chips, 2, rows, width)
        o_own = jnp.where(lead_core, o_parts[:, 0], o_parts[:, 1])
        o_sent = jnp.where(lead_core, o_parts[:, 1], o_parts[:, 0])
        o_own = (o_own + swap(o_sent.astype(bf16), "core").astype(f32)).astype(bf16)
    with jax.named_scope("feed_forward_weight_grads"):
        down_grad = mm(hidden, cot_group, TN).astype(bf16).reshape(chips, half_pad, width)
        gate_up_grad = mm(n2_group, dgu, TN).astype(bf16).reshape(chips, 2 * rows, 2 * quarter)
        pieces = []
        for start in range(0, 2 * quarter, width):
            piece = gate_up_grad[:, :, start : start + width]
            pieces.append(jnp.pad(piece, ((0, 0), (0, 0), (0, width - piece.shape[2]))))
        blob_rows = half_pad + 2 * rows * len(pieces) + rows
        blob_pad = jnp.zeros((chips, -blob_rows % 16, width), bf16)
        blob = jnp.concatenate([down_grad] + pieces + [o_own, blob_pad], axis=1)
        blob = blob.reshape(-1, width)
        datt_all, blob = lax.optimization_barrier((datt_all, blob))
        blob_share = lax.psum_scatter(blob, "chip", scatter_dimension=0, tiled=True)
        down_share = blob_share[:half_pad]
        gate_up_share = jnp.concatenate(
            [
                blob_share[half_pad + 2 * rows * i : half_pad + 2 * rows * (i + 1)]
                for i in range(len(pieces))
            ],
            axis=1,
        )[:, : 2 * quarter]
        o_share = blob_share[blob_rows - rows : blob_rows]
    dq, dkv = [], []
    for m in range(MB):
        with jax.named_scope("attention_out_grad"):
            do_cols = micro(datt_all, m)
            delta = jnp.sum(
                (do_cols.astype(f32) * heads[m]).reshape(GROUPS, HEAD_DIM, 2 * TMB), axis=1
            )
            delta = jnp.pad(delta, ((0, 8 - GROUPS), (0, 0)))
        dq_m, dkv_m = attention_backward(
            layouts[m], starts, ids, prefix, q_cols[m], kv[m], do_cols, lse[m], delta
        )
        dq.append(dq_m)
        dkv.append(dkv_m.reshape(chips, 2, 2 * HEAD_DIM, TMB))
    with jax.named_scope("feed_forward_out"):
        dq[0], result_half = lax.optimization_barrier((dq[0], result_half))
        result = (middle + rep_pair_sum(result_half)).astype(bf16)
    with jax.named_scope("return_keys"):
        if direct:


            def returned(k):
                later = lax.dynamic_index_in_dim(dkv[1], (chip - k) % chips, 0, keepdims=False)
                return jnp.stack([dkv[0][k], later], axis=0)

            dkv_sum = sum_from_chips(returned)
        else:
            dkv_sum = lax.psum_scatter(
                jnp.stack(dkv, axis=1), "chip", scatter_dimension=0, tiled=False
            ).astype(f32)
        dkv = [jnp.concatenate([dkv_sum[m, 0], dkv_sum[m, 1]], axis=1) for m in range(MB)]
    with jax.named_scope("unrotate"):
        dq_all = both_micros(dq).reshape(GROUPS, HEAD_DIM, 2 * own_rows) * HEAD_DIM**-0.5
        dq_low = unrotate(dq_all, cosine, sine).reshape(QW, 2 * own_rows).astype(bf16)
        dkv_all = both_micros(dkv)
        dk = unrotate(dkv_all[None, :HEAD_DIM], cosine, sine)[0]
        dkv_low = jnp.concatenate([dk, dkv_all[HEAD_DIM:]], axis=0).astype(bf16)

    with jax.named_scope("project_grad"):
        q_grad = mm(normed, dq_low, ((0,), (1,))).astype(bf16)
        dn1 = core_pair_sum(
            mm(dq_low, qkv_full[:, :QW], ((0,), (1,)))
            + mm(dkv_low, qkv_full[:, QW:], ((0,), (1,)))
        )
        kv_grad = mm(normed, dkv_low, ((0,), (1,))).astype(bf16)
        qkv_grad = jnp.concatenate([q_grad, kv_grad], axis=1)
        bias_grad = [jnp.sum(g.astype(f32), axis=1) for g in (dq_low, dkv_low)]
        r1 = r_pair[:own_rows]
        gain_one_grad = jnp.sum(dn1 * (x * r1), axis=0)
        e1 = dn1 * gain_one
        dx = dmiddle + r1 * e1 - x * r1**3 * jnp.mean(e1 * x, axis=-1, keepdims=True)
        input_grad = dx.astype(bf16)
    with jax.named_scope("shares"):
        packed = jnp.concatenate(bias_grad + [gain_one_grad, gain_two_grad])
        pack_count = packed.shape[0]
        pack_rows = -(-pack_count // (cols * 16)) * 16
        packed = jnp.pad(packed, (0, pack_rows * cols - pack_count)).reshape(pack_rows, cols)
        share = scatter_chips(
            jnp.concatenate(
                [
                    jnp.broadcast_to(packed.astype(bf16)[None], (chips, pack_rows, cols)),
                    qkv_grad.reshape(chips, 2 * rows, cols),
                ],
                axis=1,
            )
        ).astype(bf16)

    def rep_sum(a):
        return a.astype(f32) + swap(a, "rep").astype(f32)

    with jax.named_scope("owners"):
        o_total = rep_sum(o_share)

        def both_cores(head, body):
            own = jnp.where(lead_core, body[:rows], body[rows:])
            sent = jnp.where(lead_core, body[rows:], body[:rows])
            own = jnp.concatenate([head, own], axis=0)
            other = swap(jnp.concatenate([head, sent], axis=0), "core")
            return rep_sum(ordered(lead_core, own[None], other[None], 0))

        both = both_cores(share[:pack_rows], share[pack_rows:])
        w_both = both[:, pack_rows:]
        k_at, v_at = QW, QW + HEAD_DIM
        q_total = jnp.concatenate([w_both[0, :, :k_at], w_both[1, :, :k_at]], axis=1)
        k_total = jnp.concatenate([w_both[0, :, k_at:v_at], w_both[1, :, k_at:v_at]], axis=1)
        v_total = jnp.concatenate([w_both[0, :, v_at:], w_both[1, :, v_at:]], axis=1)
        vec = both[:, :pack_rows].reshape(2, pack_rows * cols)[:, :pack_count]
        gains = vec[0, cols:] + vec[1, cols:]
        everything = jnp.concatenate(
            [
                vec[:, :QW].reshape(2 * QW),
                vec[:, k_at:v_at].reshape(2 * HEAD_DIM),
                vec[:, v_at:cols].reshape(2 * HEAD_DIM),
                gains,
            ]
        )
        shard = 2 * chip + core
        vec_outs, offset = [], 0
        for size in (2 * QW, 2 * HEAD_DIM, 2 * HEAD_DIM, width, width):
            each = size // (2 * chips)
            vec_outs.append(lax.dynamic_slice_in_dim(everything, offset + shard * each, each, 0))
            offset += size
        q_b, k_b, v_b, gain_one_out, gain_two_out = vec_outs

        mine = jnp.where(lead_core, gate_up_share[:rows], gate_up_share[rows:])
        sent = jnp.where(lead_core, gate_up_share[rows:], gate_up_share[:rows])
        two = ordered(lead_core, mine[None], swap(sent, "core")[None], 0)
        four = ordered(lead_rep, two[None], swap(two, "rep")[None], 0)

        def whole_columns(part):
            part = part.reshape(2, 2, rows, chips, half_pad)[..., :half_rows]
            return part.transpose(2, 3, 1, 0, 4).reshape(rows, 4 * chips * half_rows).astype(f32)

        gate_out = whole_columns(four[..., :quarter])
        up_out = whole_columns(four[..., quarter:])
        down_mine = down_share[:half_rows]
        down_out = ordered(lead_rep, down_mine, swap(down_mine, "rep"), 0).astype(f32)

    return (
        result,
        input_grad,
        gain_one_out,
        q_total,
        q_b,
        k_total,
        k_b,
        v_total,
        v_b,
        o_total,
        gain_two_out,
        gate_out,
        up_out,
        down_out,
    )


def solution(mesh):
    split = Mesh(mesh.devices.reshape(mesh.shape["rep"], -1, 2), ("rep", "chip", "core"))
    shard = ("chip", "core")
    token_spec = P(("rep", "chip", "core"), None)
    row_spec, vec_spec = P(shard, None), P(shard)
    in_specs = (
        token_spec,
        token_spec,
        P(),
        P(),
        vec_spec,
        row_spec,
        vec_spec,
        row_spec,
        vec_spec,
        row_spec,
        vec_spec,
        row_spec,
        vec_spec,
        row_spec,
        row_spec,
        row_spec,
    )
    out_specs = (token_spec, token_spec) + in_specs[4:]
    return jax.shard_map(
        on_device, mesh=split, in_specs=in_specs, out_specs=out_specs, check_vma=False
    )
```

time: 801 us -> 706 us (0.88)
  starting transfers between devices: 229 us -> 52 us
  Pallas kernels: 128 us -> 202 us
  waiting for transfers between devices: 145 us -> 189 us
  other arithmetic: 66.6 us -> 54.3 us
  local copies, waits for them, and re-layouts: 93.8 us -> 83.4 us
  matrix products: 108 us -> 99.6 us
    ppermute x49 -> x21, starting transfers between devices: 195 us -> 38.8 us  [the longest x14 27.3 us: sum_from_chips(): total = total + lax.ppermute(chunk_of(k), 'chip', back_hop[k]).astype(f32)]
    pallas_call x4, Pallas kernels: 128 us -> 202 us  [the longest x2 108 us: attention_backward(): pl.pallas_call(functools.partial(backward_kernel, layout), grid_spec=grid...]
    all_gather x2, waiting for transfers between devices: 41.5 us -> 0.04 us  [the longest x1 0.02 us: on_device(): lax.all_gather(mine, 'chip', axis=0)]
    ppermute x49 -> x21, waiting for transfers between devices: 30.8 us -> 66.6 us  [the longest x14 56.2 us: sum_from_chips(): total = total + lax.ppermute(chunk_of(k), 'chip', back_hop[k]).astype(f32)]
    all_gather x1, waiting for transfers between devices: 6.26 us -> 35.1 us  [on_device(): gate_up = lax.all_gather(pair_rows, 'chip', axis=0, tiled=True)]
    ppermute x39 -> x23, starting transfers between devices: 33.1 us -> 12.9 us  [swap(): return lax.ppermute(a, axis, [(0, 1), (1, 0)])]
    all_gather x1, waiting for transfers between devices: 12.8 us -> 28.6 us  [on_device(): qkv_all = lax.all_gather(chip_rows, 'chip', axis=0, tiled=False)]
    concatenate x5 -> x16, other arithmetic: 5.73 us -> 16 us  [the longest x2 7.58 us: on_device(): jnp.concatenate([jnp.broadcast_to(packed.astype(bf16)[None], (chips, pack...]
  transfers between devices with their start and end apart: 94 -> 49, of which waited for: 30 -> 20; matrix products, arithmetic and copies ran while one was open for 31% -> 21% of each run, Pallas kernels for 16% -> 29%
where the time goes in v2:
time: 706 us; the launch traced here: 698 us
  Pallas kernels  202 us (29%)
  waiting for transfers between devices  189 us (27%)
  matrix products  99.6 us (14%)
  local copies, waits for them, and re-layouts  83.4 us (12%)
  other arithmetic  54.3 us (8%)
  starting transfers between devices  52 us (7%)
  between operations  17.2 us (2%)
    pallas_call x2, Pallas kernels, attention_backward(): pl.pallas_call(functools.partial(backward_kernel, layout), grid_spec=grid...  108 us
    dot_general x14, matrix products, mm(): return lax.dot_general(a, b, (dims, ((), ())), preferred_element_type=f32)  99.6 us
    pallas_call x2, Pallas kernels, attention_forward(): pl.pallas_call(functools.partial(forward_kernel, layout), grid_spec=grid_...  94.3 us
    ppermute x23, waiting for transfers between devices, swap(): return lax.ppermute(a, axis, [(0, 1), (1, 0)])  58.4 us
    ppermute x14, waiting for transfers between devices, sum_from_chips(): total = total + lax.ppermute(chunk_of(k), 'chip', back_hop[k]).astype(f32)  56.2 us
    all_gather x1, waiting for transfers between devices, on_device(): gate_up = lax.all_gather(pair_rows, 'chip', axis=0, tiled=True)  35.1 us
    all_gather x1, waiting for transfers between devices, on_device(): qkv_all = lax.all_gather(chip_rows, 'chip', axis=0, tiled=False)  28.6 us
    ppermute x14, starting transfers between devices, sum_from_chips(): total = total + lax.ppermute(chunk_of(k), 'chip', back_hop[k]).astype(f32)  27.3 us
  transfers between devices with their start and end apart: 49, of which 20 were waited for; matrix products, arithmetic and copies ran while one was open for 21% of the time, Pallas kernels for 29%

profile of v2, /device:TPU:0, one launch (start us, length us, event | category | flops | bytes accessed | tf_op | source)
XLA Modules:
  0.0 697.9 jit_solution(14002112197251879248)
XLA Ops:
  7.2 3.1 collective-permute-start.1
  23.0 2.5 reshape.884
  27.3 2.5 reshape.886
  33.2 1.6 fusion.4
  34.8 28.6 %all-gather.7.cloned.1.call-done = bf16[8,2,64,576]{3,2,1,0:T(8,128)(2,1)} async-done(((bf16[1,2,64,576]{3,2,1,0:T(8,128)(2,1)}), bf16[8,2,64,576]{3,2,1,0:T(8,128)(2,1)}) %all-gather.7.cloned.1.call-update) | async-done | bytes 1179664 | tf_op jit(solution)/shard_map/weights_qkv/all_gather | solution.py:321
  66.3 3.0 convolution_add_fusion.1
  72.7 2.0 maximum_select_fusion.2
  76.0 2.4 collective-permute-start.7
  78.4 2.3 collective-permute-start.8
  81.4 1.8 collective-permute-start.10
  83.2 2.5 collective-permute-start.11
  85.7 7.6 %collective-permute-done.7 = bf16[2,128,256]{2,1,0:T(8,128)(2,1)S(1)} collective-permute-done((bf16[2,128,256]{2,1,0:T(8,128)(2,1)S(1)}, bf16[2,128,256]{2,1,0:T(8,128)(2,1)S(1)}, u32[]{:S(2)}, u32[]{:S(2)}) %collective-permute-start.7) | collective-permute-done | bytes 131104 | tf_op jit(solution)/shard_map/gather_keys/ppermute | solution.py:281
  93.3 2.5 collective-permute-done.8
  101.8 57.8 %attention_forward.2 = (f32[448,512]{1,0:T(8,128)}, f32[8,512]{1,0:T(8,128)}) custom-call(s32[64]{0:T(128)} %get-tuple-element.184.starts, s32[3]{0:T(128)} %pad_add_fusion.ids, s32[4]{0:T(128)} %prefix.7, bf16[448,512]{1,0:T(8,128)(2,1)} %pad_maximum_fusion.13.q_ref, bf16[16,128,256]{2,1,0:T(8,128)(2,1)} %bitcast.268), custom_call_target="tpu_custom_call" | custom-call | flops 7516192768 | bytes 1048576 | tf_op jit(solution)/shard_map/attention_forward/pallas_call | solution.py:135
  160.9 36.5 %attention_forward.3 = (f32[448,512]{1,0:T(8,128)}, f32[8,512]{1,0:T(8,128)}) custom-call(s32[64]{0:T(128)} %get-tuple-element.184.starts, s32[3]{0:T(128)} %pad_add_fusion.ids, s32[4]{0:T(128)} %prefix.7, bf16[448,512]{1,0:T(8,128)(2,1)} %pad_maximum_fusion.14.q_ref, bf16[16,128,256]{2,1,0:T(8,128)(2,1)} %all-gather.11.cloned.1.call-done.kv_ref), custom_call_target="tpu_custom_call" | custom-call | flops 7516192768 | bytes 1048576 | tf_op jit(solution)/shard_map/attention_forward/pallas_call | solution.py:135
  201.5 2.6 multiply_reduce_fusion.2
  204.5 22.5 %collective-permute-done.15 = bf16[512,896]{1,0:T(8,128)(2,1)S(1)} collective-permute-done((bf16[512,896]{1,0:T(8,128)(2,1)S(1)}, bf16[512,896]{1,0:T(8,128)(2,1)S(1)}, u32[]{:S(2)}, u32[]{:S(2)}) %collective-permute-start.15) | collective-permute-done | bytes 917536 | tf_op jit(solution)/shard_map/attention_out/ppermute | solution.py:37
  229.6 2.4 constant_dynamic-update-slice_fusion.6
  232.0 2.2 constant_dynamic-update-slice_fusion.5
  234.2 2.2 constant_dynamic-update-slice_fusion.4
  236.4 1.6 slice.632
  238.0 35.1 %all-gather.9.cloned.1.call-done = bf16[896,2560]{1,0:T(8,128)(2,1)} async-done(((bf16[112,2560]{1,0:T(8,128)(2,1)}), bf16[896,2560]{1,0:T(8,128)(2,1)}) %all-gather.9.cloned.1.call-update) | async-done | bytes 4587536 | tf_op jit(solution)/shard_map/gather_mlp/all_gather | solution.py:431
  273.1 18.5 %fusion.14 = f32[2048,2560]{0,1:T(8,128)} fusion(bf16[896,2560]{1,0:T(8,128)(2,1)} %all-gather.9.cloned.1.call-done, bf16[1024,896]{1,0:T(8,128)(2,1)} %collective-permute-done.16, bf16[512,896]{1,0:T(8,128)(2,1)} %copy-done.28, bf16[512,896]{1,0:T(8,128)(2,1)} %copy-done.17), kind=kOutput, calls=%fused_computation.65 | convolution fusion | flops 9406251008 | bytes 29229056 | tf_op jit(solution)/shard_map/feed_forward/dot_general | solution.py:33
  291.7 19.5 %multiply_convert_fusion.2 = (bf16[2048,1280]{0,1:T(8,128)(2,1)}, bf16[2048,1280]{0,1:T(8,128)(2,1)}, bf16[2048,1280]{0,1:T(8,128)(2,1)}) fusion(f32[2048,2560]{0,1:T(8,128)} %fusion.14, bf16[2048,896]{1,0:T(8,128)(2,1)} %constant_dynamic-update-slice_fusion.4, bf16[1280,896]{1,0:T(8,128)(2,1)S(1)} %bitcast.235), kind=kOutput, calls=%fused_computation.3 | convolution fusion | flops 4736942080 | bytes 42663936 | tf_op jit(solution)/shard_map/feed_forward_grad/dot_general | solution.py:33
  311.2 15.3 %fusion.2 = f32[2048,896]{1,0:T(8,128)S(1)} fusion(bf16[896,2560]{1,0:T(8,128)(2,1)} %all-gather.9.cloned.1.call-done, bf16[2048,1280]{0,1:T(8,128)(2,1)} %get-tuple-element.95, bf16[2048,1280]{0,1:T(8,128)(2,1)} %get-tuple-element.94), kind=kOutput, calls=%fused_computation.7 | convolution fusion | flops 9416212480 | bytes 22413312 | tf_op jit(solution)/shard_map/feed_forward_grad/dot_general | solution.py:33
  326.5 3.0 copy-done.12
  330.6 15.0 %fusion.3 = bf16[896,2560]{1,0:T(8,128)(2,1)} fusion(bf16[2048,1280]{0,1:T(8,128)(2,1)} %get-tuple-element.95, bf16[2048,1280]{0,1:T(8,128)(2,1)} %get-tuple-element.94, bf16[1024,896]{1,0:T(8,128)(2,1)} %collective-permute-done.16, bf16[512,896]{1,0:T(8,128)(2,1)} %copy-done.28, bf16[512,896]{1,0:T(8,128)(2,1)S(1)} %copy-done.18), kind=kOutput, calls=%fused_computation.8 | convolution fusion | flops 9429516288 | bytes 18743296 | tf_op jit(solution)/shard_map/feed_forward_weight_grads/dot_general | solution.py:33
  345.6 2.9 slice_add_fusion.1
  350.1 8.8 %convolution_convert_fusion = bf16[1280,896]{1,0:T(8,128)(2,1)S(1)} fusion(bf16[2048,1280]{0,1:T(8,128)(2,1)} %get-tuple-element.96, bf16[2048,896]{1,0:T(8,128)(2,1)} %constant_dynamic-update-slice_fusion.4), kind=kOutput, calls=%fused_computation.27 | convolution fusion | flops 4698767360 | bytes 11206656 | tf_op jit(solution)/shard_map/feed_forward_weight_grads/dot_general | solution.py:33
  360.5 10.0 %collective-permute-done.18 = bf16[512,896]{1,0:T(8,128)(2,1)S(1)} collective-permute-done((bf16[512,896]{1,0:T(8,128)(2,1)S(1)}, bf16[512,896]{1,0:T(8,128)(2,1)S(1)}, u32[]{:S(2)}, u32[]{:S(2)}) %collective-permute-start.18) | collective-permute-done | bytes 917536 | tf_op jit(solution)/shard_map/feed_forward_grad/ppermute | solution.py:37
  382.0 8.3 %fusion.96 = f32[2048,896]{1,0:T(8,128)S(1)} fusion(bf16[2048,1280]{0,1:T(8,128)(2,1)} %get-tuple-element.96, bf16[1280,896]{1,0:T(8,128)(2,1)} %bitcast.234), kind=kOutput, calls=%fused_computation.308 | convolution fusion | flops 4697620480 | bytes 14876672 | tf_op jit(solution)/shard_map/feed_forward_out/dot_general | solution.py:33
  390.4 2.9 copy-done.11
  394.8 4.1 collective-permute-done.21
  398.9 4.7 slice_add_fusion
  407.7 1.7 pad_maximum_fusion.17.do_ref
  410.2 42.2 %attention_backward.3 = (f32[448,512]{1,0:T(8,128)}, bf16[16,128,256]{2,1,0:T(8,128)(2,1)}) custom-call(s32[64]{0:T(128)} %get-tuple-element.184.starts, s32[3]{0:T(128)} %pad_add_fusion.ids, s32[4]{0:T(128)} %prefix.7, bf16[448,512]{1,0:T(8,128)(2,1)} %pad_maximum_fusion.14.q_ref, bf16[16,128,256]{2,1,0:T(8,128)(2,1)} %all-gather.11.cloned.1.call-done.kv_ref, ...), custom_call_target="tpu_custom_call" | custom-call | flops 11274289152 | bytes 3145728 | tf_op jit(solution)/shard_map/attention_backward/pallas_call | solution.py:210
  453.9 65.6 %attention_backward.2 = (f32[448,512]{1,0:T(8,128)}, bf16[16,128,256]{2,1,0:T(8,128)(2,1)}) custom-call(s32[64]{0:T(128)} %get-tuple-element.184.starts, s32[3]{0:T(128)} %pad_add_fusion.ids, s32[4]{0:T(128)} %prefix.7, bf16[448,512]{1,0:T(8,128)(2,1)} %pad_maximum_fusion.13.q_ref, bf16[16,128,256]{2,1,0:T(8,128)(2,1)} %bitcast.269, ...), custom_call_target="tpu_custom_call" | custom-call | flops 11274289152 | bytes 3145728 | tf_op jit(solution)/shard_map/attention_backward/pallas_call | solution.py:210
  522.1 13.6 %collective-permute-start.25 = (bf16[2,2,128,256]{3,2,1,0:T(8,128)(2,1)S(1)}, bf16[2,2,128,256]{3,2,1,0:T(8,128)(2,1)S(1)}, u32[]{:S(2)}, u32[]{:S(2)}) collective-permute-start(bf16[2,2,128,256]{3,2,1,0:T(8,128)(2,1)S(1)} %pad_maximum_fusion.23), channel_id=1, source_target_pairs={{0,10},{2,12},{4,14},{6,0},{8,2},{10,4},{12,6},{14,8},{1,11},{3,13... | collective-permute-start | bytes 786440 | tf_op jit(solution)/shard_map/return_keys/ppermute | solution.py:287
  537.9 3.1 collective-permute-start.28
  541.0 3.9 collective-permute-done.24
  546.1 28.1 %collective-permute-done.26 = bf16[2,2,128,256]{3,2,1,0:T(8,128)(2,1)S(1)} collective-permute-done((bf16[2,2,128,256]{3,2,1,0:T(8,128)(2,1)S(1)}, bf16[2,2,128,256]{3,2,1,0:T(8,128)(2,1)S(1)}, u32[]{:S(2)}, u32[]{:S(2)}) %collective-permute-start.26) | collective-permute-done | bytes 262176 | tf_op jit(solution)/shard_map/return_keys/ppermute | solution.py:287
  574.2 8.5 %collective-permute-done.27 = bf16[2,2,128,256]{3,2,1,0:T(8,128)(2,1)S(1)} collective-permute-done((bf16[2,2,128,256]{3,2,1,0:T(8,128)(2,1)S(1)}, bf16[2,2,128,256]{3,2,1,0:T(8,128)(2,1)S(1)}, u32[]{:S(2)}, u32[]{:S(2)}) %collective-permute-start.27) | collective-permute-done | bytes 262176 | tf_op jit(solution)/shard_map/return_keys/ppermute | solution.py:287
  586.4 1.9 copy-done
  589.4 2.6 slice.848
  592.1 2.4 convolution_convert_fusion.2
  594.5 1.8 convolution_convert_fusion.3
  597.4 2.6 reshape.900
  600.1 2.8 fusion.12
  603.5 5.7 fusion.26
  610.4 3.4 collective-permute-start.34
  613.9 1.9 fusion.31
  616.0 2.1 collective-permute-start.36
  619.7 2.6 add_convert_fusion
  622.2 11.4 %collective-permute-done.34 = bf16[128,576]{0,1:T(8,128)(2,1)S(1)} collective-permute-done((bf16[128,576]{0,1:T(8,128)(2,1)S(1)}, bf16[128,576]{0,1:T(8,128)(2,1)S(1)}, u32[]{:S(2)}, u32[]{:S(2)}) %collective-permute-start.34) | collective-permute-done | bytes 147488 | tf_op jit(solution)/shard_map/shares/ppermute | solution.py:287
  633.6 3.1 collective-permute-done.35
  638.7 1.8 collective-permute-start.39
  640.5 2.7 fusion.9
  643.3 4.6 collective-permute-done.39
  655.4 1.8 collective-permute-start.43
  658.5 1.8 collective-permute-start.42
  660.3 6.7 collective-permute-done.40
  669.7 9.0 %collective-permute-done.42 = bf16[2,56,2560]{2,1,0:T(8,128)(2,1)S(1)} collective-permute-done((bf16[2,56,2560]{2,1,0:T(8,128)(2,1)S(1)}, bf16[2,56,2560]{2,1,0:T(8,128)(2,1)S(1)}, u32[]{:S(2)}, u32[]{:S(2)}) %collective-permute-start.42) | collective-permute-done | bytes 573472 | tf_op jit(solution)/shard_map/owners/ppermute | solution.py:37
  681.8 3.2 reshape.910
  687.8 3.2 reshape.911
  (396 shorter events, 96.5 us)
Async XLA Ops:
  7.2 13.1 %copy-start.31 = (bf16[304,896]{1,0:T(8,128)(2,1)S(1)}, bf16[304,896]{1,0:T(8,128)(2,1)}, u32[]{:S(2)}) copy-start(bf16[304,896]{1,0:T(8,128)(2,1)} %param.31) | copy-start | bytes 1634308
  7.2 15.8 %copy-start.32 = (bf16[56,4864]{1,0:T(8,128)(2,1)S(1)}, bf16[56,4864]{1,0:T(8,128)(2,1)}, u32[]{:S(2)}) copy-start(bf16[56,4864]{1,0:T(8,128)(2,1)} %param.29) | copy-start | bytes 1634308
  7.2 56.2 %all-gather.7.cloned.1.call-start = ((), (), s32[]{:S(2)}) async-start(), calls=%async_computation.1 | async-start | bytes 1474560 | tf_op jit(solution)/shard_map/weights_qkv/all_gather | solution.py:321
  7.2 25.6 %collective-permute-start.1 = (bf16[512,896]{1,0:T(8,128)(2,1)}, bf16[512,896]{1,0:T(8,128)(2,1)}, u32[]{:S(2)}, u32[]{:S(2)}) collective-permute-start(bf16[512,896]{1,0:T(8,128)(2,1)} %param.17), channel_id=1, source_target_pairs={{0,16},{16,0},{1,17},{17,1},{2,18},{18,2},{3,19},{19,3},{4,20},{20... | collective-permute-start | bytes 2752520 | tf_op jit(solution)/shard_map/gather_cotangent/ppermute | solution.py:37
  10.3 55.9 %collective-permute-start.2 = (bf16[512,896]{1,0:T(8,128)(2,1)}, bf16[512,896]{1,0:T(8,128)(2,1)}, u32[]{:S(2)}, u32[]{:S(2)}) collective-permute-start(bf16[512,896]{1,0:T(8,128)(2,1)} %param.17), channel_id=1, source_target_pairs={{0,1},{1,0},{2,3},{3,2},{4,5},{5,4},{6,7},{7,6},{8,9},{9,8},{10,11... | collective-permute-start | bytes 2752520 | tf_op jit(solution)/shard_map/gather_cotangent/ppermute | solution.py:37
  16.6 3.7 collective-permute-start
  17.2 16.0 %collective-permute-start.4 = (bf16[512,896]{1,0:T(8,128)(2,1)}, bf16[512,896]{1,0:T(8,128)(2,1)}, u32[]{:S(2)}, u32[]{:S(2)}) collective-permute-start(bf16[512,896]{1,0:T(8,128)(2,1)} %param.16), channel_id=1, source_target_pairs={{0,1},{1,0},{2,3},{3,2},{4,5},{5,4},{6,7},{7,6},{8,9},{9,8},{10,11... | collective-permute-start | bytes 2752520 | tf_op jit(solution)/shard_map/project/ppermute | solution.py:37
  17.3 14.6 %collective-permute-start.12 = (bf16[56,896]{1,0:T(8,128)(2,1)}, bf16[56,896]{1,0:T(8,128)(2,1)S(1)}, u32[]{:S(2)}, u32[]{:S(2)}) collective-permute-start(bf16[56,896]{1,0:T(8,128)(2,1)} %param.27), channel_id=1, source_target_pairs={{0,1},{1,0},{2,3},{3,2},{4,5},{5,4},{6,7},{7,6},{8,9},{9,8},{10,11... | collective-permute-start | bytes 301064 | tf_op jit(solution)/shard_map/weights_mlp/ppermute | solution.py:37
  19.8 77.7 %copy-start.35 = (f32[1,2,4,128]{3,1,2,0:T(2,128)}, f32[1,2,4,128]{3,1,2,0:T(2,128)S(1)}, u32[]{:S(2)}) copy-start(f32[1,2,4,128]{3,1,2,0:T(2,128)S(1)} %copy.111) | copy-start | bytes 12292
  20.4 77.1 %copy-start.42 = (f32[32]{0:T(128)}, f32[32]{0:T(128)S(1)}, u32[]{:S(2)}) copy-start(f32[32]{0:T(128)S(1)} %negate_power_fusion) | copy-start | bytes 388
  21.1 139.8 %all-gather.11.cloned.1.call-start = ((), (), s32[]{:S(2)}) async-start(), calls=%async_computation.4 | async-start | bytes 1179648 | tf_op jit(solution)/shard_map/gather_keys/all_gather | solution.py:423
  31.7 41.0 %collective-permute-start.13 = (bf16[56,2560]{1,0:T(8,128)(2,1)S(1)}, bf16[56,2560]{1,0:T(8,128)(2,1)}, u32[]{:S(2)}, u32[]{:S(2)}) collective-permute-start(bf16[56,2560]{1,0:T(8,128)(2,1)S(1)} %get-tuple-element.157), channel_id=1, source_target_pairs={{0,1},{1,0},{2,3},{3,2},{4,5},{5,4},{6,7},{7,6},{8,9},{9,8},{10,11... | collective-permute-start | bytes 860168 | tf_op jit(solution)/shard_map/weights_mlp/ppermute | solution.py:37
  32.8 33.4 %collective-permute-start.3 = (bf16[512,896]{1,0:T(8,128)(2,1)}, bf16[512,896]{1,0:T(8,128)(2,1)}, u32[]{:S(2)}, u32[]{:S(2)}) collective-permute-start(bf16[512,896]{1,0:T(8,128)(2,1)} %collective-permute-done.1), channel_id=1, source_target_pairs={{0,1},{1,0},{2,3},{3,2},{4,5},{5,4},{6,7},{7,6},{8,9},{9,8},{10,11... | collective-permute-start | bytes 2752520 | tf_op jit(solution)/shard_map/gather_cotangent/ppermute | solution.py:37
  34.8 34.5 %copy-start.40 = (f32[1024]{0:T(1024)}, f32[1024]{0:T(1024)S(1)}, u32[]{:S(2)}) copy-start(f32[1024]{0:T(1024)S(1)} %add_rsqrt_fusion) | copy-start | bytes 12292
  71.4 9.9 %collective-permute-start.5 = (bf16[2,128,256]{2,1,0:T(8,128)(2,1)S(1)}, bf16[2,128,256]{2,1,0:T(8,128)(2,1)S(1)}, u32[]{:S(2)}, u32[]{:S(2)}) collective-permute-start(bf16[2,128,256]{2,1,0:T(8,128)(2,1)S(1)} %pad_maximum_fusion.31), channel_id=1, source_target_pairs={{0,2},{2,4},{4,6},{6,8},{8,10},{10,12},{12,14},{14,0},{1,3},{3,5},... | collective-permute-start | bytes 393224 | tf_op jit(solution)/shard_map/gather_keys/ppermute | solution.py:281
  72.7 126.2 %all-gather.13.cloned.1.call-start = ((), (), s32[]{:S(2)}) async-start(), calls=%async_computation.5 | async-start | bytes 4386816 | tf_op jit(solution)/shard_map/gather_mlp/all_gather | solution.py:427
  74.8 8.4 %collective-permute-start.6 = (bf16[2,128,256]{2,1,0:T(8,128)(2,1)S(1)}, bf16[2,128,256]{2,1,0:T(8,128)(2,1)S(1)}, u32[]{:S(2)}, u32[]{:S(2)}) collective-permute-start(bf16[2,128,256]{2,1,0:T(8,128)(2,1)S(1)} %pad_maximum_fusion.31), channel_id=1, source_target_pairs={{0,4},{2,6},{4,8},{6,10},{8,12},{10,14},{12,0},{14,2},{1,5},{3,7},... | collective-permute-start | bytes 393224 | tf_op jit(solution)/shard_map/gather_keys/ppermute | solution.py:281
  76.0 17.3 %collective-permute-start.7 = (bf16[2,128,256]{2,1,0:T(8,128)(2,1)S(1)}, bf16[2,128,256]{2,1,0:T(8,128)(2,1)S(1)}, u32[]{:S(2)}, u32[]{:S(2)}) collective-permute-start(bf16[2,128,256]{2,1,0:T(8,128)(2,1)S(1)} %pad_maximum_fusion.31), channel_id=1, source_target_pairs={{0,6},{2,8},{4,10},{6,12},{8,14},{10,0},{12,2},{14,4},{1,7},{3,9},... | collective-permute-start | bytes 393224 | tf_op jit(solution)/shard_map/gather_keys/ppermute | solution.py:281
  78.4 17.4 %collective-permute-start.8 = (bf16[2,128,256]{2,1,0:T(8,128)(2,1)S(1)}, bf16[2,128,256]{2,1,0:T(8,128)(2,1)S(1)}, u32[]{:S(2)}, u32[]{:S(2)}) collective-permute-start(bf16[2,128,256]{2,1,0:T(8,128)(2,1)S(1)} %pad_maximum_fusion.31), channel_id=1, source_target_pairs={{0,8},{2,10},{4,12},{6,14},{8,0},{10,2},{12,4},{14,6},{1,9},{3,11}... | collective-permute-start | bytes 393224 | tf_op jit(solution)/shard_map/gather_keys/ppermute | solution.py:281
  80.7 15.1 %collective-permute-start.9 = (bf16[2,128,256]{2,1,0:T(8,128)(2,1)S(1)}, bf16[2,128,256]{2,1,0:T(8,128)(2,1)S(1)}, u32[]{:S(2)}, u32[]{:S(2)}) collective-permute-start(bf16[2,128,256]{2,1,0:T(8,128)(2,1)S(1)} %pad_maximum_fusion.31), channel_id=1, source_target_pairs={{0,10},{2,12},{4,14},{6,0},{8,2},{10,4},{12,6},{14,8},{1,11},{3,13... | collective-permute-start | bytes 393224 | tf_op jit(solution)/shard_map/gather_keys/ppermute | solution.py:281
  81.4 14.5 %collective-permute-start.10 = (bf16[2,128,256]{2,1,0:T(8,128)(2,1)S(1)}, bf16[2,128,256]{2,1,0:T(8,128)(2,1)S(1)}, u32[]{:S(2)}, u32[]{:S(2)}) collective-permute-start(bf16[2,128,256]{2,1,0:T(8,128)(2,1)S(1)} %pad_maximum_fusion.31), channel_id=1, source_target_pairs={{0,12},{2,14},{4,0},{6,2},{8,4},{10,6},{12,8},{14,10},{1,13},{3,15... | collective-permute-start | bytes 393224 | tf_op jit(solution)/shard_map/gather_keys/ppermute | solution.py:281
  83.2 13.0 %collective-permute-start.11 = (bf16[2,128,256]{2,1,0:T(8,128)(2,1)S(1)}, bf16[2,128,256]{2,1,0:T(8,128)(2,1)S(1)}, u32[]{:S(2)}, u32[]{:S(2)}) collective-permute-start(bf16[2,128,256]{2,1,0:T(8,128)(2,1)S(1)} %pad_maximum_fusion.31), channel_id=1, source_target_pairs={{0,14},{2,0},{4,2},{6,4},{8,6},{10,8},{12,10},{14,12},{1,15},{3,1}... | collective-permute-start | bytes 393224 | tf_op jit(solution)/shard_map/gather_keys/ppermute | solution.py:281
  96.2 176.9 %all-gather.9.cloned.1.call-start = ((), (), s32[]{:S(2)}) async-start(), calls=%async_computation.2 | async-start | bytes 5160960 | tf_op jit(solution)/shard_map/gather_mlp/all_gather | solution.py:431
  96.8 554.1 %reduce-scatter.2.cloned.1.call-start = ((), (), s32[]{:S(2)}) async-start(), calls=%async_computation.3 | async-start | bytes 9031680 | tf_op jit(solution)/shard_map/feed_forward_weight_grads/reduce_scatter | solution.py:490
  198.7 1.9 collective-permute-start.14
  204.4 24.1 %copy-start.17 = (bf16[512,896]{1,0:T(8,128)(2,1)}, bf16[512,896]{1,0:T(8,128)(2,1)S(1)}, u32[]{:S(2)}) copy-start(bf16[512,896]{1,0:T(8,128)(2,1)S(1)} %multiply_convert_fusion.3) | copy-start | bytes 2752516
  204.4 24.1 %copy-start.16 = (bf16[512,896]{1,0:T(8,128)(2,1)S(1)}, bf16[512,896]{1,0:T(8,128)(2,1)}, u32[]{:S(2)}) copy-start(bf16[512,896]{1,0:T(8,128)(2,1)} %param.17) | copy-start | bytes 2752516
  204.4 22.6 %collective-permute-start.15 = (bf16[512,896]{1,0:T(8,128)(2,1)S(1)}, bf16[512,896]{1,0:T(8,128)(2,1)S(1)}, u32[]{:S(2)}, u32[]{:S(2)}) collective-permute-start(bf16[512,896]{1,0:T(8,128)(2,1)S(1)} %multiply_convert_fusion.3), channel_id=1, source_target_pairs={{0,16},{16,0},{1,17},{17,1},{2,18},{18,2},{3,19},{19,3},{4,20},{20... | collective-permute-start | bytes 2752520 | tf_op jit(solution)/shard_map/attention_out/ppermute | solution.py:37
  228.5 44.6 %collective-permute-start.16 = (bf16[1024,896]{1,0:T(8,128)(2,1)}, bf16[1024,896]{1,0:T(8,128)(2,1)}, u32[]{:S(2)}, u32[]{:S(2)}) collective-permute-start(bf16[1024,896]{1,0:T(8,128)(2,1)} %pad_maximum_fusion.7), channel_id=1, source_target_pairs={{0,1},{1,0},{2,3},{3,2},{4,5},{5,4},{6,7},{7,6},{8,9},{9,8},{10,11... | collective-permute-start | bytes 5505032 | tf_op jit(solution)/shard_map/attention_out/ppermute | solution.py:37
  273.1 18.5 %copy-start.20 = (bf16[8,160,896]{2,1,0:T(8,128)(2,1)S(1)}, bf16[8,160,896]{2,1,0:T(8,128)(2,1)}, u32[]{:S(2)}) copy-start(bf16[8,160,896]{2,1,0:T(8,128)(2,1)} %slice.632) | copy-start | bytes 6881284
  329.6 16.0 %collective-permute-start.17 = (bf16[1024,896]{1,0:T(8,128)(2,1)S(1)}, bf16[1024,896]{1,0:T(8,128)(2,1)}, u32[]{:S(2)}, u32[]{:S(2)}) collective-permute-start(bf16[1024,896]{1,0:T(8,128)(2,1)S(1)} %slice.846), channel_id=1, source_target_pairs={{0,1},{1,0},{2,3},{3,2},{4,5},{5,4},{6,7},{7,6},{8,9},{9,8},{10,11... | collective-permute-start | bytes 5505032 | tf_op jit(solution)/shard_map/feed_forward_grad/ppermute | solution.py:37
  348.6 21.9 %collective-permute-start.18 = (bf16[512,896]{1,0:T(8,128)(2,1)S(1)}, bf16[512,896]{1,0:T(8,128)(2,1)S(1)}, u32[]{:S(2)}, u32[]{:S(2)}) collective-permute-start(bf16[512,896]{1,0:T(8,128)(2,1)S(1)} %slice.849), channel_id=1, source_target_pairs={{0,16},{16,0},{1,17},{17,1},{2,18},{18,2},{3,19},{19,3},{4,20},{20... | collective-permute-start | bytes 2752520 | tf_op jit(solution)/shard_map/feed_forward_grad/ppermute | solution.py:37
  375.3 4.9 collective-permute-start.20
  375.4 4.6 collective-permute-start.19
  394.7 4.1 collective-permute-start.21
  520.8 16.6 %copy-start.29 = (f32[448,512]{1,0:T(8,128)S(1)}, f32[448,512]{1,0:T(8,128)}, u32[]{:S(2)}) copy-start(f32[448,512]{1,0:T(8,128)} %get-tuple-element.50) | copy-start | bytes 2752516
  520.8 17.0 %collective-permute-start.23 = (bf16[2,2,128,256]{3,2,1,0:T(8,128)(2,1)S(1)}, bf16[2,2,128,256]{3,2,1,0:T(8,128)(2,1)S(1)}, u32[]{:S(2)}, u32[]{:S(2)}) collective-permute-start(bf16[2,2,128,256]{3,2,1,0:T(8,128)(2,1)S(1)} %pad_maximum_fusion.21), channel_id=1, source_target_pairs={{0,14},{2,0},{4,2},{6,4},{8,6},{10,8},{12,10},{14,12},{1,15},{3,1}... | collective-permute-start | bytes 786440 | tf_op jit(solution)/shard_map/return_keys/ppermute | solution.py:287
  520.9 23.9 %collective-permute-start.24 = (bf16[2,2,128,256]{3,2,1,0:T(8,128)(2,1)S(1)}, bf16[2,2,128,256]{3,2,1,0:T(8,128)(2,1)S(1)}, u32[]{:S(2)}, u32[]{:S(2)}) collective-permute-start(bf16[2,2,128,256]{3,2,1,0:T(8,128)(2,1)S(1)} %pad_maximum_fusion.22), channel_id=1, source_target_pairs={{0,12},{2,14},{4,0},{6,2},{8,4},{10,6},{12,8},{14,10},{1,13},{3,15... | collective-permute-start | bytes 786440 | tf_op jit(solution)/shard_map/return_keys/ppermute | solution.py:287
  522.1 15.4 %copy-start.30 = (f32[448,512]{1,0:T(8,128)S(1)}, f32[448,512]{1,0:T(8,128)}, u32[]{:S(2)}) copy-start(f32[448,512]{1,0:T(8,128)} %get-tuple-element.48) | copy-start | bytes 2752516
  522.1 24.0 %collective-permute-start.25 = (bf16[2,2,128,256]{3,2,1,0:T(8,128)(2,1)S(1)}, bf16[2,2,128,256]{3,2,1,0:T(8,128)(2,1)S(1)}, u32[]{:S(2)}, u32[]{:S(2)}) collective-permute-start(bf16[2,2,128,256]{3,2,1,0:T(8,128)(2,1)S(1)} %pad_maximum_fusion.23), channel_id=1, source_target_pairs={{0,10},{2,12},{4,14},{6,0},{8,2},{10,4},{12,6},{14,8},{1,11},{3,13... | collective-permute-start | bytes 786440 | tf_op jit(solution)/shard_map/return_keys/ppermute | solution.py:287
  535.7 38.5 %collective-permute-start.26 = (bf16[2,2,128,256]{3,2,1,0:T(8,128)(2,1)S(1)}, bf16[2,2,128,256]{3,2,1,0:T(8,128)(2,1)S(1)}, u32[]{:S(2)}, u32[]{:S(2)}) collective-permute-start(bf16[2,2,128,256]{3,2,1,0:T(8,128)(2,1)S(1)} %pad_maximum_fusion.24), channel_id=1, source_target_pairs={{0,8},{2,10},{4,12},{6,14},{8,0},{10,2},{12,4},{14,6},{1,9},{3,11}... | collective-permute-start | bytes 786440 | tf_op jit(solution)/shard_map/return_keys/ppermute | solution.py:287
  535.9 46.9 %collective-permute-start.27 = (bf16[2,2,128,256]{3,2,1,0:T(8,128)(2,1)S(1)}, bf16[2,2,128,256]{3,2,1,0:T(8,128)(2,1)S(1)}, u32[]{:S(2)}, u32[]{:S(2)}) collective-permute-start(bf16[2,2,128,256]{3,2,1,0:T(8,128)(2,1)S(1)} %pad_maximum_fusion.25), channel_id=1, source_target_pairs={{0,6},{2,8},{4,10},{6,12},{8,14},{10,0},{12,2},{14,4},{1,7},{3,9},... | collective-permute-start | bytes 786440 | tf_op jit(solution)/shard_map/return_keys/ppermute | solution.py:287
  537.6 7.5 %copy-start.25 = (f32[32,1024]{1,0:T(8,128)S(1)}, f32[32,1024]{1,0:T(8,128)}, u32[]{:S(2)}) copy-start(f32[32,1024]{1,0:T(8,128)} %copy-done.24) | copy-start | bytes 393220
  537.9 44.9 %collective-permute-start.28 = (bf16[2,2,128,256]{3,2,1,0:T(8,128)(2,1)S(1)}, bf16[2,2,128,256]{3,2,1,0:T(8,128)(2,1)S(1)}, u32[]{:S(2)}, u32[]{:S(2)}) collective-permute-start(bf16[2,2,128,256]{3,2,1,0:T(8,128)(2,1)S(1)} %pad_maximum_fusion.26), channel_id=1, source_target_pairs={{0,4},{2,6},{4,8},{6,10},{8,12},{10,14},{12,0},{14,2},{1,5},{3,7},... | collective-permute-start | bytes 786440 | tf_op jit(solution)/shard_map/return_keys/ppermute | solution.py:287
  544.9 37.9 %collective-permute-start.29 = (bf16[2,2,128,256]{3,2,1,0:T(8,128)(2,1)S(1)}, bf16[2,2,128,256]{3,2,1,0:T(8,128)(2,1)S(1)}, u32[]{:S(2)}, u32[]{:S(2)}) collective-permute-start(bf16[2,2,128,256]{3,2,1,0:T(8,128)(2,1)S(1)} %pad_maximum_fusion.27), channel_id=1, source_target_pairs={{0,2},{2,4},{4,6},{6,8},{8,10},{10,12},{12,14},{14,0},{1,3},{3,5},... | collective-permute-start | bytes 786440 | tf_op jit(solution)/shard_map/return_keys/ppermute | solution.py:287
  545.6 39.5 %copy-start.14 = (bf16[7,64,1024]{2,1,0:T(8,128)(2,1)}, bf16[7,64,1024]{2,1,0:T(8,128)(2,1)S(1)}, u32[]{:S(2)}) copy-start(bf16[7,64,1024]{2,1,0:T(8,128)(2,1)S(1)} %get-tuple-element.93) | copy-start | bytes 2752516
  589.3 10.8 %collective-permute-start.30 = (bf16[512,896]{1,0:T(8,128)(2,1)}, bf16[512,896]{1,0:T(8,128)(2,1)}, u32[]{:S(2)}, u32[]{:S(2)}) collective-permute-start(bf16[512,896]{1,0:T(8,128)(2,1)} %slice.847), channel_id=1, source_target_pairs={{0,1},{1,0},{2,3},{3,2},{4,5},{5,4},{6,7},{7,6},{8,9},{9,8},{10,11... | collective-permute-start | bytes 2752520 | tf_op jit(solution)/shard_map/project_grad/ppermute | solution.py:37
  592.0 23.9 %collective-permute-start.22 = (bf16[512,896]{1,0:T(8,128)(2,1)}, bf16[512,896]{1,0:T(8,128)(2,1)}, u32[]{:S(2)}, u32[]{:S(2)}) collective-permute-start(bf16[512,896]{1,0:T(8,128)(2,1)} %slice.848), channel_id=1, source_target_pairs={{0,16},{16,0},{1,17},{17,1},{2,18},{18,2},{3,19},{19,3},{4,20},{20... | collective-permute-start | bytes 2752520 | tf_op jit(solution)/shard_map/feed_forward_out/ppermute | solution.py:37
  609.2 6.8 collective-permute-start.31
  609.3 9.4 %collective-permute-start.32 = (bf16[128,576]{0,1:T(8,128)(2,1)S(1)}, bf16[128,576]{0,1:T(8,128)(2,1)S(1)}, u32[]{:S(2)}, u32[]{:S(2)}) collective-permute-start(bf16[128,576]{0,1:T(8,128)(2,1)S(1)} %bitcast.256), channel_id=1, source_target_pairs={{0,12},{2,14},{4,0},{6,2},{8,4},{10,6},{12,8},{14,10},{1,13},{3,15... | collective-permute-start | bytes 442376 | tf_op jit(solution)/shard_map/shares/ppermute | solution.py:287
  610.3 11.9 %collective-permute-start.33 = (bf16[128,576]{0,1:T(8,128)(2,1)S(1)}, bf16[128,576]{0,1:T(8,128)(2,1)S(1)}, u32[]{:S(2)}, u32[]{:S(2)}) collective-permute-start(bf16[128,576]{0,1:T(8,128)(2,1)S(1)} %bitcast.253), channel_id=1, source_target_pairs={{0,10},{2,12},{4,14},{6,0},{8,2},{10,4},{12,6},{14,8},{1,11},{3,13... | collective-permute-start | bytes 442376 | tf_op jit(solution)/shard_map/shares/ppermute | solution.py:287
  610.4 23.2 %collective-permute-start.34 = (bf16[128,576]{0,1:T(8,128)(2,1)S(1)}, bf16[128,576]{0,1:T(8,128)(2,1)S(1)}, u32[]{:S(2)}, u32[]{:S(2)}) collective-permute-start(bf16[128,576]{0,1:T(8,128)(2,1)S(1)} %bitcast.254), channel_id=1, source_target_pairs={{0,8},{2,10},{4,12},{6,14},{8,0},{10,2},{12,4},{14,6},{1,9},{3,11}... | collective-permute-start | bytes 442376 | tf_op jit(solution)/shard_map/shares/ppermute | solution.py:287
  615.9 20.8 %collective-permute-start.35 = (bf16[128,576]{0,1:T(8,128)(2,1)S(1)}, bf16[128,576]{0,1:T(8,128)(2,1)S(1)}, u32[]{:S(2)}, u32[]{:S(2)}) collective-permute-start(bf16[128,576]{0,1:T(8,128)(2,1)S(1)} %bitcast.255), channel_id=1, source_target_pairs={{0,6},{2,8},{4,10},{6,12},{8,14},{10,0},{12,2},{14,4},{1,7},{3,9},... | collective-permute-start | bytes 442376 | tf_op jit(solution)/shard_map/shares/ppermute | solution.py:287
  616.0 20.7 %collective-permute-start.36 = (bf16[128,576]{0,1:T(8,128)(2,1)S(1)}, bf16[128,576]{0,1:T(8,128)(2,1)S(1)}, u32[]{:S(2)}, u32[]{:S(2)}) collective-permute-start(bf16[128,576]{0,1:T(8,128)(2,1)S(1)} %bitcast.259), channel_id=1, source_target_pairs={{0,4},{2,6},{4,8},{6,10},{8,12},{10,14},{12,0},{14,2},{1,5},{3,7},... | collective-permute-start | bytes 442376 | tf_op jit(solution)/shard_map/shares/ppermute | solution.py:287
  618.7 18.0 %collective-permute-start.37 = (bf16[128,576]{0,1:T(8,128)(2,1)S(1)}, bf16[128,576]{0,1:T(8,128)(2,1)S(1)}, u32[]{:S(2)}, u32[]{:S(2)}) collective-permute-start(bf16[128,576]{0,1:T(8,128)(2,1)S(1)} %bitcast.258), channel_id=1, source_target_pairs={{0,2},{2,4},{4,6},{6,8},{8,10},{10,12},{12,14},{14,0},{1,3},{3,5},... | collective-permute-start | bytes 442376 | tf_op jit(solution)/shard_map/shares/ppermute | solution.py:287
  619.6 20.9 %copy-start.1 = (f32[1024,896]{1,0:T(8,128)S(1)}, f32[1024,896]{1,0:T(8,128)}, u32[]{:S(2)}) copy-start(f32[1024,896]{1,0:T(8,128)} %copy-done) | copy-start | bytes 11010052
  622.2 18.3 %copy-start.5 = (bf16[512,896]{1,0:T(8,128)(2,1)S(1)}, bf16[512,896]{1,0:T(8,128)(2,1)}, u32[]{:S(2)}) copy-start(bf16[512,896]{1,0:T(8,128)(2,1)} %param.16) | copy-start | bytes 2752516
  622.2 18.3 %copy-start.8 = (f32[512,896]{1,0:T(8,128)S(1)}, f32[512,896]{1,0:T(8,128)}, u32[]{:S(2)}) copy-start(f32[512,896]{1,0:T(8,128)} %copy-done.7) | copy-start | bytes 5505028
  637.2 1.4 collective-permute-start.38
  638.7 9.1 %collective-permute-start.39 = (bf16[2,72,576]{1,2,0:T(8,128)(2,1)S(1)}, bf16[2,72,576]{1,2,0:T(8,128)(2,1)S(1)}, u32[]{:S(2)}, u32[]{:S(2)}) collective-permute-start(bf16[2,72,576]{1,2,0:T(8,128)(2,1)S(1)} %maximum_select_fusion.6), channel_id=1, source_target_pairs={{0,16},{16,0},{1,17},{17,1},{2,18},{18,2},{3,19},{19,3},{4,20},{20... | collective-permute-start | bytes 497672 | tf_op jit(solution)/shard_map/owners/ppermute | solution.py:37
  652.2 6.2 collective-permute-start.41
  655.4 13.2 %collective-permute-start.43 = (bf16[152,896]{1,0:T(8,128)(2,1)S(1)}, bf16[152,896]{1,0:T(8,128)(2,1)S(1)}, u32[]{:S(2)}, u32[]{:S(2)}) collective-permute-start(bf16[152,896]{1,0:T(8,128)(2,1)S(1)} %slice.685), channel_id=1, source_target_pairs={{0,16},{16,0},{1,17},{17,1},{2,18},{18,2},{3,19},{19,3},{4,20},{20... | collective-permute-start | bytes 817160 | tf_op jit(solution)/shard_map/owners/ppermute | solution.py:37
  658.1 8.9 %collective-permute-start.40 = (bf16[56,896]{1,0:T(8,128)(2,1)S(1)}, bf16[56,896]{1,0:T(8,128)(2,1)S(1)}, u32[]{:S(2)}, u32[]{:S(2)}) collective-permute-start(bf16[56,896]{1,0:T(8,128)(2,1)S(1)} %slice.677), channel_id=1, source_target_pairs={{0,16},{16,0},{1,17},{17,1},{2,18},{18,2},{3,19},{19,3},{4,20},{20... | collective-permute-start | bytes 301064 | tf_op jit(solution)/shard_map/owners/ppermute | solution.py:37
  658.5 20.3 %collective-permute-start.42 = (bf16[2,56,2560]{2,1,0:T(8,128)(2,1)S(1)}, bf16[2,56,2560]{2,1,0:T(8,128)(2,1)S(1)}, u32[]{:S(2)}, u32[]{:S(2)}) collective-permute-start(bf16[2,56,2560]{2,1,0:T(8,128)(2,1)S(1)} %maximum_select_fusion.4), channel_id=1, source_target_pairs={{0,16},{16,0},{1,17},{17,1},{2,18},{18,2},{3,19},{19,3},{4,20},{20... | collective-permute-start | bytes 1720328 | tf_op jit(solution)/shard_map/owners/ppermute | solution.py:37
  (34 other events, 77.4 us)
Sparse Core Ops, SparseCore 0:
  21.2 42.1 all-gather.6
  72.8 51.0 all-gather.10
  126.7 68.0 all-gather.12
  196.8 76.3 all-gather.8
  382.1 145.7 reduce-scatter.1
